TPU v7x, 32 devices: a whole 2x2x4 slice. The times are simulated.
32 devices in a mesh: dp: 8 (over y, x, core), tensor: 4 (over z).
Axes of the slice: x: 2, y: 2, z: 4, core: 2. Of those that a mesh axis runs over, the one named last changes fastest.
Arguments:
- tokens: bfloat16 [32768, 768], P(('dp', 'tensor')), may hold values from -6 to 6
- cotangent: bfloat16 [32768, 768], P(('dp', 'tensor')), may hold values from -6 to 6
- source: int32 [32768], P(('dp', 'tensor')), may hold values from 0 to 32767, as said below
- target: int32 [32768], P(('dp', 'tensor')), may hold values from 0 to 32767, as said below
- lengths: int32 [8, 3], P('dp'), may hold values from 1 to 2048, as said below
- ln_gain: float32 [768], P(('dp', 'tensor')), may hold values from 0.5 to 1.5
- ln_bias: float32 [768], P(('dp', 'tensor')), may hold values from -1.75 to 1.75
- w_fwd: bfloat16 [768, 1536], P('dp', 'tensor'), may hold values from -0.21875 to 0.21875
- b_fwd: float32 [1536], P(('dp', 'tensor')), may hold values from -3 to 3
- w_bwd: bfloat16 [768, 1536], P('dp', 'tensor'), may hold values from -0.21875 to 0.21875
- b_bwd: float32 [1536], P(('dp', 'tensor')), may hold values from -3 to 3
- w_gate: bfloat16 [768, 2, 1536], P('dp', None, 'tensor'), may hold values from -0.21875 to 0.21875
- b_gate: float32 [2, 1536], P(None, ('dp', 'tensor')), may hold values from -3 to 3
- w_out: bfloat16 [2, 1536, 768], P(None, 'tensor', 'dp'), may hold values from -0.109375 to 0.109375
- b_out: float32 [768], P(('dp', 'tensor')), may hold values from -1.75 to 1.75
- log_dt: float32 [2, 1536], P(None, ('dp', 'tensor')), may hold values from -6.9 to -2.3
- log_rate: float32 [2, 1536, 64], P(None, ('dp', 'tensor')), may hold values from -0.7 to 4.2
- ssm_b: float32 [2, 1536, 64], P(None, ('dp', 'tensor')), may hold values from -6 to 6
- ssm_c: float32 [2, 1536, 64], P(None, ('dp', 'tensor')), may hold values from -6 to 6
- ssm_d: float32 [2, 1536], P(None, ('dp', 'tensor')), may hold values from -6 to 6
Outputs:
- layer_out: bfloat16 [32768, 768], P(('dp', 'tensor'))
- input_grad: bfloat16 [32768, 768], P(('dp', 'tensor'))
- ln_gain_grad: float32 [768], P(('dp', 'tensor'))
- ln_bias_grad: float32 [768], P(('dp', 'tensor'))
- w_fwd_grad: float32 [768, 1536], P('dp', 'tensor')
- b_fwd_grad: float32 [1536], P(('dp', 'tensor'))
- w_bwd_grad: float32 [768, 1536], P('dp', 'tensor')
- b_bwd_grad: float32 [1536], P(('dp', 'tensor'))
- w_gate_grad: float32 [768, 2, 1536], P('dp', None, 'tensor')
- b_gate_grad: float32 [2, 1536], P(None, ('dp', 'tensor'))
- w_out_grad: float32 [2, 1536, 768], P(None, 'tensor', 'dp')
- b_out_grad: float32 [768], P(('dp', 'tensor'))
- log_dt_grad: float32 [2, 1536], P(None, ('dp', 'tensor'))
- log_rate_grad: float32 [2, 1536, 64], P(None, ('dp', 'tensor'))
- ssm_b_grad: float32 [2, 1536, 64], P(None, ('dp', 'tensor'))
- ssm_c_grad: float32 [2, 1536, 64], P(None, ('dp', 'tensor'))
- ssm_d_grad: float32 [2, 1536], P(None, ('dp', 'tensor'))
Inputs may be any that keep to these rules, and one draw needn't show every extreme that they name: Row q of the dealt order takes row source[q] of the given order. Both orders are cut into blocks of 1024 rows, one a device in the order of the dp+tensor placement; a row moves only between devices with the same tensor index, and exactly 1024 / (devices of dp) rows move from each such device to each such device. The inverse of source: source[target[r]] = r. `lengths`: the slots of a group's sequences, each rounded up to a multiple of 128 rows, fit in its 4096 rows; every group has a sequence of exactly 2048 rows.
All inputs are finite; a program needn't handle non-finite values.
Results may differ from a plain program's by a relative error of at most 0.012.
Values may be sent and summed in bfloat16 or wider, within the bound.
A program may use at most 448 MiB of HBM per device.

v0:
```python
from functools import partial

import jax
import jax.numpy as jnp
import numpy as np
from jax import lax
from jax.experimental import pallas as pl
from jax.experimental.pallas import tpu as pltpu
from jax.sharding import PartitionSpec as P

BLK = 128
BIG = 256
MOST = 2048
LAGS = MOST // BIG
STATE = 64
epsilon = 1e-05
log2e = 1.4426950408889634
f32 = jnp.float32
bf16 = jnp.bfloat16
MIB = 2**20


def nn(a, b):
    return lax.dot_general(a, b, (((1,), (0,)), ((), ())), preferred_element_type=f32)


def nt(a, b):
    return lax.dot_general(a, b, (((1,), (1,)), ((), ())), preferred_element_type=f32)


def params(limit):
    return pltpu.CompilerParams(vmem_limit_bytes=60 * MIB)


def cost(flops, moved, trans=0):
    scale = 0.05
    return pl.CostEstimate(
        flops=int(scale * flops), bytes_accessed=int(scale * moved), transcendentals=int(scale * trans)
    )


def halves(x):
    high = x.astype(bf16)
    return high, (x - high.astype(f32)).astype(bf16)


def wave_table():
    pos = np.arange(BIG)[:, None]
    freq = np.arange(BIG)[None, :]
    angle = 2 * np.pi * ((2 * freq + 1) * pos % (4 * BIG)) / (4 * BIG)
    return np.concatenate([np.cos(angle), np.sin(angle)], 1).astype(np.float32)


def chunk_of(channels, most):
    best = 16
    for size in range(16, most + 1, 16):
        if channels % size == 0:
            best = size
    return best


def permute_row_body(count, rank_ref, *refs):
    rows = rank_ref.shape[1]
    spot = lax.broadcasted_iota(jnp.int32, (rows, rows), 0)
    pick = jnp.where(spot == rank_ref[...], 1.0, 0.0).astype(bf16)
    for at in range(count):
        refs[count + at][...] = nn(pick, refs[at][...]).astype(bf16)


def permute_to(rank, arrays):
    rows, width = arrays[0].shape
    count = len(arrays)
    return pl.pallas_call(
        partial(permute_row_body, count),
        out_shape=[jax.ShapeDtypeStruct((rows, width), bf16)] * count,
        compiler_params=params(48),
        cost_estimate=cost(2 * count * rows * rows * width, 4 * count * rows * width),
    )(rank.reshape(1, rows), *arrays)


def permute_col_body(rank_ref, x_ref, o_ref):
    rows = x_ref.shape[0]
    spot = lax.broadcasted_iota(jnp.int32, (rows, rows), 1)
    pick = jnp.where(spot == rank_ref[...], 1.0, 0.0).astype(bf16)
    o_ref[...] = nn(pick, x_ref[...]).astype(bf16)


def permute_from(rank, x):
    rows, width = x.shape
    return pl.pallas_call(
        permute_col_body,
        out_shape=jax.ShapeDtypeStruct((rows, width), bf16),
        compiler_params=params(48),
        cost_estimate=cost(2 * rows * rows * width, 4 * rows * width),
    )(rank.reshape(rows, 1), x)


def pick_rows(place_ref, x_ref):
    spot = lax.broadcasted_iota(jnp.int32, (BLK, x_ref.shape[0]), 1)
    pick = jnp.where(spot == place_ref[...], 1.0, 0.0).astype(bf16)
    return nn(pick, x_ref[...]).T


def deal_x_body(place_ref, x_ref, gain_ref, shift_ref, xt_ref, xd_ref):
    x = pick_rows(place_ref, x_ref)
    xd_ref[0] = x.astype(bf16)
    centred = x - jnp.mean(x, axis=0, keepdims=True)
    inv_std = lax.rsqrt(jnp.mean(centred * centred, axis=0, keepdims=True) + epsilon)
    xt_ref[0] = (centred * inv_std * gain_ref[...] + shift_ref[...]).astype(bf16)


def deal_g_body(place_ref, g_ref, live_ref, gt_ref, gd_ref, bo_ref):
    g = pick_rows(place_ref, g_ref)
    gd_ref[0] = g.astype(bf16)
    g = g * live_ref[0]
    gt_ref[0] = g.astype(bf16)

    @pl.when(pl.program_id(0) == 0)
    def _():
        bo_ref[...] = jnp.zeros_like(bo_ref)

    bo_ref[...] += g


def deal_specs(rows, width):
    place = pl.BlockSpec((BLK, 1), lambda i: (i, 0))
    whole = pl.BlockSpec((rows, width), lambda i: (0, 0))
    wide = pl.BlockSpec((width, BLK), lambda i: (0, 0))
    out = pl.BlockSpec((1, width, BLK), lambda i: (i, 0, 0))
    return place, whole, wide, out


def deal_x(place, x, gain, shift):
    rows, width = x.shape
    blocks = rows // BLK
    spot, whole, wide, out = deal_specs(rows, width)
    return pl.pallas_call(
        deal_x_body,
        grid=(blocks,),
        in_specs=[spot, whole, wide, wide],
        out_specs=[out, out],
        out_shape=[jax.ShapeDtypeStruct((blocks, width, BLK), bf16)] * 2,
        compiler_params=params(40),
        cost_estimate=cost(2 * rows * rows * width, 6 * rows * width),
    )(place.reshape(rows, 1), x, gain, shift)


def deal_g(place, g, live):
    rows, width = g.shape
    blocks = rows // BLK
    spot, whole, wide, out = deal_specs(rows, width)
    return pl.pallas_call(
        deal_g_body,
        grid=(blocks,),
        in_specs=[spot, whole, pl.BlockSpec((1, 1, BLK), lambda i: (i, 0, 0))],
        out_specs=[out, out, wide],
        out_shape=[jax.ShapeDtypeStruct((blocks, width, BLK), bf16)] * 2
        + [jax.ShapeDtypeStruct((width, BLK), f32)],
        compiler_params=params(40),
        cost_estimate=cost(2 * rows * rows * width, 6 * rows * width),
    )(place.reshape(rows, 1), g, live)


def send_back(place_ref, out_s, o_ref):
    rows = out_s.shape[0]
    spot = lax.broadcasted_iota(jnp.int32, (rows, rows), 0)
    pick = jnp.where(spot == place_ref[...], 1.0, 0.0).astype(bf16)
    o_ref[...] = nn(pick, out_s[...]).astype(bf16)


def total(refs, at):
    value = refs[0][at].astype(f32)
    for ref in refs[1:]:
        value = value + ref[at].astype(f32)
    return value


def layer_body(place_ref, xd_ref, live_ref, bias_ref, *refs):
    o_ref, out_s = refs[-2:]
    for at in range(xd_ref.shape[0]):
        y = xd_ref[at].astype(f32) + live_ref[at] * (total(refs[:-2], at) + bias_ref[...])
        out_s[at * BLK : (at + 1) * BLK, :] = y.T.astype(bf16)
    send_back(place_ref, out_s, o_ref)


def layer_rows(place, parts, xd, live, bias):
    blocks, width, _ = xd.shape
    rows = blocks * BLK
    return pl.pallas_call(
        layer_body,
        out_shape=jax.ShapeDtypeStruct((rows, width), bf16),
        scratch_shapes=[pltpu.VMEM((rows, width), bf16)],
        compiler_params=params(48),
        cost_estimate=cost(2 * rows * rows * width, 6 * rows * width),
    )(place.reshape(1, rows), xd, live, bias, *parts)


def input_body(place_ref, xd_ref, gd_ref, gain_ref, *refs):
    o_ref, sums_ref, out_s = refs[-3:]
    g_gain = jnp.zeros(gain_ref.shape, f32)
    g_shift = jnp.zeros(gain_ref.shape, f32)
    for at in range(xd_ref.shape[0]):
        x = xd_ref[at].astype(f32)
        centred = x - jnp.mean(x, axis=0, keepdims=True)
        inv_std = lax.rsqrt(jnp.mean(centred * centred, axis=0, keepdims=True) + epsilon)
        x_hat = centred * inv_std
        g = total(refs[:-3], at)
        g_gain = g_gain + g * x_hat
        g_shift = g_shift + g
        hat = g * gain_ref[...]
        back = inv_std * (
            hat
            - jnp.mean(hat, axis=0, keepdims=True)
            - x_hat * jnp.mean(hat * x_hat, axis=0, keepdims=True)
        )
        out_s[at * BLK : (at + 1) * BLK, :] = (gd_ref[at].astype(f32) + back).T.astype(bf16)
    sums_ref[0] = g_gain
    sums_ref[1] = g_shift
    send_back(place_ref, out_s, o_ref)


def input_rows(place, parts, xd, gd, gain):
    blocks, width, _ = xd.shape
    rows = blocks * BLK
    return pl.pallas_call(
        input_body,
        out_shape=[
            jax.ShapeDtypeStruct((rows, width), bf16),
            jax.ShapeDtypeStruct((2, width, BLK), f32),
        ],
        scratch_shapes=[pltpu.VMEM((rows, width), bf16)],
        compiler_params=params(48),
        cost_estimate=cost(2 * rows * rows * width, 8 * rows * width),
    )(place.reshape(1, rows), xd, gd, gain, *parts)


def project_body(ch, many, start_ref, x_ref, live_ref, wt_ref, bias_ref, *refs):
    a_ref, da_ref, gg_ref, dg_ref = refs[-4:]
    x = jnp.concatenate([x_ref[0], x_ref[1]], axis=1)
    live = live_ref[0]
    root = 0.7978845608028654
    step = 64 if ch % 128 else 128

    def act(pre):
        square = pre * pre
        rise = 0.5 + 0.5 * jnp.tanh(pre * (root + (0.044715 * root) * square))
        value = pre * rise
        slope = rise + rise * (pre - value) * (2.0 * root + (6.0 * 0.044715 * root) * square)
        return value, slope

    def put(ref, k, at, value):
        value = value.astype(bf16)
        ref[k, 0, at, :] = value[:, :BLK]
        ref[k, 1, at, :] = value[:, BLK:]

    for k in range(2):
        for first, value_ref, slope_ref in ((k * ch, a_ref, da_ref), ((2 + k) * ch, gg_ref, dg_ref)):
            for at in range(0, ch, step):
                rows = pl.ds(first + at, step)
                bias = bias_ref[rows, :]
                pre = nn(wt_ref[rows, :], x) + jnp.concatenate([bias, bias], axis=1)
                value, slope = act(pre)
                if value_ref is a_ref:
                    value, slope = live * value, live * slope
                put(value_ref, k, pl.ds(at, step), value)
                put(slope_ref, k, pl.ds(at, step), slope)


def chained(body, grid, in_specs, out_specs, shapes, scratch, limit, estimate, start, operands, kept):
    kept = [] if kept is None else list(kept)
    specs = list(in_specs) + [pl.BlockSpec(memory_space=pl.ANY)] * len(kept)
    first = 1 + len(operands)
    return pl.pallas_call(
        body,
        grid_spec=pltpu.PrefetchScalarGridSpec(
            num_scalar_prefetch=1, grid=grid, in_specs=specs, out_specs=out_specs, scratch_shapes=scratch
        ),
        out_shape=shapes,
        input_output_aliases={first + at: at for at in range(len(kept))},
        compiler_params=params(limit),
        cost_estimate=estimate,
    )(start, *operands, *kept)


def project(xt, start, nb, live, wt, bias, kept):
    many, width, _ = xt.shape
    ch = wt.shape[0] // 4
    out = pl.BlockSpec((2, 2, ch, BLK), lambda i, at: (0, at[0] + i, 0, 0))
    tok = many * BLK
    return chained(
        partial(project_body, ch, many),
        (many // 2,),
        [
            pl.BlockSpec((2, width, BLK), lambda i, at: (i, 0, 0)),
            pl.BlockSpec((1, 1, BIG), lambda i, at: (at[0] + i, 0, 0)),
            pl.BlockSpec((4 * ch, width), lambda i, at: (0, 0)),
            pl.BlockSpec((4 * ch, BLK), lambda i, at: (0, 0)),
        ],
        [out] * 4,
        [jax.ShapeDtypeStruct((2, nb, ch, BLK), bf16)] * 4,
        [],
        48,
        cost(8 * tok * width * ch, 2 * tok * width + 16 * tok * ch, 4 * tok * ch),
        start // 2,
        [xt, live, wt, bias],
        kept,
    )


def gate_grad_body(ch, parts, at_ref, *refs):
    wt_ref, o_ref = refs[parts:]
    steps = pl.num_programs(0) // parts

    def work(g_ref):
        gm = nn(wt_ref[...], jnp.concatenate([g_ref[0], g_ref[1]], axis=1)).astype(bf16)
        for k in range(2):
            for h in range(2):
                o_ref[k, h] = gm[k * ch : (k + 1) * ch, h * BLK : (h + 1) * BLK]

    for part in range(parts):

        @pl.when(pl.program_id(0) // steps == part)
        def _(part=part):
            work(refs[part])


def gate_grad(gs, nb, wt):
    parts = len(gs)
    many, width, _ = gs[0][0].shape
    steps = many // 2
    ch = wt.shape[0] // 2
    tok = nb * BLK

    def rows(part):
        return pl.BlockSpec((2, width, BLK), lambda i, at: (jnp.clip(i - part * steps, 0, steps - 1), 0, 0))

    order = jnp.concatenate([start // 2 for _, start in gs]).astype(jnp.int32)
    return pl.pallas_call(
        partial(gate_grad_body, ch, parts),
        grid_spec=pltpu.PrefetchScalarGridSpec(
            num_scalar_prefetch=1,
            grid=(parts * steps,),
            in_specs=[rows(part) for part in range(parts)] + [pl.BlockSpec((2 * ch, width), lambda i, at: (0, 0))],
            out_specs=pl.BlockSpec((2, 2, ch, BLK), lambda i, at: (0, at[i // steps] + i % steps, 0, 0)),
        ),
        out_shape=jax.ShapeDtypeStruct((2, nb, ch, BLK), bf16),
        compiler_params=params(40),
        cost_estimate=cost(4 * tok * width * ch, 2 * tok * width + 4 * tok * ch),
    )(order, *[part for part, _ in gs], wt)


def spectra_body(cc, ld_ref, w_ref, d_ref, wave_ref, kh_ref, k_s):
    t = lax.broadcasted_iota(jnp.int32, (BLK, BLK), 0).astype(f32)
    block = lax.broadcasted_iota(jnp.int32, (2 * LAGS, BLK), 0).astype(f32) * float(BLK)
    low = lax.broadcasted_iota(jnp.int32, (2 * LAGS, BLK), 1) < STATE
    count = 2 * LAGS

    def one(p, carry):
        ld = ld_ref[0, pl.ds(p, 1), :]
        decay = jnp.exp2(t * ld)
        scale = w_ref[0, pl.ds(p, 1), :] * jnp.exp2(block * ld)
        lhs = jnp.concatenate([jnp.where(low, scale, 0.0), jnp.where(low, 0.0, scale)], axis=0)
        lhs_high, lhs_low = halves(lhs)
        k = nt(jnp.concatenate([lhs_high, lhs_low], axis=0), decay.astype(bf16))
        k = k[0 : 2 * count] + k[2 * count : 4 * count]
        k_s[pl.ds(2 * p, count, stride=cc), :] = k[0:count]
        k_s[pl.ds(2 * p + 1, count, stride=cc), :] = k[count : 2 * count]
        return carry

    lax.fori_loop(0, cc // 2, one, 0, unroll=16)
    sign = jnp.where(lax.broadcasted_iota(jnp.int32, (cc, BIG), 1) % 2 == 0, 1.0, -1.0)
    before = None
    for big in range(LAGS):
        rows = jnp.concatenate(
            [k_s[pl.ds(2 * big * cc, cc), :], k_s[pl.ds((2 * big + 1) * cc, cc), :]], axis=1
        )
        high, rest = halves(rows)
        x = nn(high, wave_ref[...]) + nn(rest, wave_ref[...])
        xc, xs = x[:, :BIG], x[:, BIG:]
        if big == 0:
            kh_ref[0, 0, :, :BIG] = xc + d_ref[0][:, 0:1]
            kh_ref[0, 0, :, BIG:] = xs
        else:
            kh_ref[0, big, :, :BIG] = xc + sign * before[1]
            kh_ref[0, big, :, BIG:] = xs - sign * before[0]
        before = (xc, xs)


def spectra(ld, w, d, wave):
    ch = 2 * ld.shape[1]
    cc = chunk_of(ch, 128)
    return pl.pallas_call(
        partial(spectra_body, cc),
        grid=(2, ch // cc),
        in_specs=[pl.BlockSpec((1, cc // 2, BLK), lambda k, i: (k, i, 0))] * 2
        + [
            pl.BlockSpec((1, cc, BLK), lambda k, i: (k, i, 0)),
            pl.BlockSpec((BIG, 2 * BIG), lambda k, i: (0, 0)),
        ],
        out_specs=pl.BlockSpec((1, LAGS, cc, 2 * BIG), lambda k, i: (k, 0, i, 0)),
        out_shape=jax.ShapeDtypeStruct((2, LAGS, ch, 2 * BIG), f32),
        scratch_shapes=[pltpu.VMEM((2 * LAGS * cc, BLK), f32)],
        compiler_params=params(40),
        cost_estimate=cost(2 * ch * 40e6, 2 * ch * LAGS * 2 * BIG * 4),
    )(ld, w, d, wave)


def moments_body(cc, ld_ref, gh_ref, back_ref, s0_ref, s1_ref, g0_ref, g_s):
    sign = jnp.where(lax.broadcasted_iota(jnp.int32, (cc, BIG), 1) % 2 == 0, 1.0, -1.0)
    count = 2 * LAGS
    for big in range(LAGS):
        c = gh_ref[0, big, :, :BIG]
        s = gh_ref[0, big, :, BIG:]
        if big < LAGS - 1:
            c, s = c - sign * gh_ref[0, big + 1, :, BIG:], s + sign * gh_ref[0, big + 1, :, :BIG]
        high, rest = halves(jnp.concatenate([c, s], axis=1))
        g = nn(high, back_ref[...]) + nn(rest, back_ref[...])
        g_s[pl.ds(2 * big * cc, cc), :] = g[:, :BLK]
        g_s[pl.ds((2 * big + 1) * cc, cc), :] = g[:, BLK:]
        if big == 0:
            g0_ref[0] = g[:, :BLK]
    t = lax.broadcasted_iota(jnp.int32, (BLK, BLK), 0).astype(f32)
    lane = lax.broadcasted_iota(jnp.int32, (count, BLK), 1)
    lag = lane.astype(f32)
    block = lax.broadcasted_iota(jnp.int32, (count, BLK), 0).astype(f32) * float(BLK)
    low = lane < STATE

    def one(p, carry):
        ld = ld_ref[0, pl.ds(p, 1), :]
        decay = jnp.exp2(t * ld).astype(bf16)
        far = jnp.exp2(block * ld)
        ga = g_s[pl.ds(2 * p, count, stride=cc), :]
        gb = g_s[pl.ds(2 * p + 1, count, stride=cc), :]
        high, rest = halves(jnp.concatenate([ga, gb, ga * lag, gb * lag], axis=0))
        m = nn(jnp.concatenate([high, rest], axis=0), decay)
        m = m[0 : 4 * count] + m[4 * count : 8 * count]
        m0 = jnp.where(low, m[0:count], m[count : 2 * count])
        m1 = jnp.where(low, m[2 * count : 3 * count], m[3 * count : 4 * count]) + block * m0
        s0_ref[0, pl.ds(p, 1), :] = jnp.sum(far * m0, axis=0, keepdims=True)
        s1_ref[0, pl.ds(p, 1), :] = jnp.sum(far * m1, axis=0, keepdims=True)
        return carry

    lax.fori_loop(0, cc // 2, one, 0, unroll=16)


def moments(k, ld, gh, back):
    ch = gh.shape[2]
    cc = chunk_of(ch, 128)
    row = pl.BlockSpec((1, cc // 2, BLK), lambda i: (0, i, 0))
    return pl.pallas_call(
        partial(moments_body, cc),
        grid=(ch // cc,),
        in_specs=[
            pl.BlockSpec((1, cc // 2, BLK), lambda i: (k, i, 0)),
            pl.BlockSpec((1, LAGS, cc, 2 * BIG), lambda i: (0, 0, i, 0)),
            pl.BlockSpec((2 * BIG, BIG), lambda i: (0, 0)),
        ],
        out_specs=[row, row, pl.BlockSpec((1, cc, BLK), lambda i: (0, i, 0))],
        out_shape=[jax.ShapeDtypeStruct((1, ch // 2, BLK), f32)] * 2
        + [jax.ShapeDtypeStruct((1, ch, BLK), f32)],
        scratch_shapes=[pltpu.VMEM((2 * LAGS * cc, BLK), f32)],
        compiler_params=params(40),
        cost_estimate=cost(ch * 40e6, ch * LAGS * 2 * BIG * 4),
    )(ld, gh, back)


def load_pieces(nb, pieces, cc, tab_ref, block, in_s, wave_ref, dst):
    for h in range(pieces):
        first = tab_ref[0, h]
        whole = tab_ref[1, h].astype(f32)
        in_s[pl.ds(h * cc, cc), 0:BLK] = block(first).astype(bf16)
        in_s[pl.ds(h * cc, cc), BLK:BIG] = (block(jnp.minimum(first + 1, nb - 1)) * whole).astype(bf16)
    for h in range(pieces):
        at = pl.ds(h * cc, cc)
        dst[at, :] = nn(in_s[at, :], wave_ref[...])


def over_pieces(nseq, cc, rg, seq_ref, piece):
    def group(r, carry):
        off = pl.multiple_of(r * rg, rg)
        for s in range(nseq):
            base = seq_ref[0, s]
            count = seq_ref[1, s]

            def outer(i, carry):
                piece(i, count, base, off)
                return carry

            lax.fori_loop(0, count, outer, 0)
        return carry

    lax.fori_loop(0, cc // rg, group, 0)


def scan_body(
    nb, nseq, cc, rg, tab_ref, seq_ref, a_ref, kh_ref, wave_ref, back_ref, gg_ref, y_ref, mix_ref, in_s, ah_s, yh_s, y_s
):
    pieces = (nb + nseq) // 2
    load_pieces(nb, pieces, cc, tab_ref, lambda b: a_ref[0, b].astype(f32), in_s, wave_ref, ah_s)
    zero = jnp.zeros((rg, BIG), f32)

    def products(flip):
        def piece(i, count, base, off):
            def inner(j, acc):
                yc, ys = acc
                other = (base + i + j) if flip else (base + i - j)
                m = pl.ds(pl.multiple_of(other * cc + off, rg), rg)
                rows = pl.ds(off, rg)
                ac = ah_s[m, :BIG]
                as_ = ah_s[m, BIG:]
                kc = kh_ref[0, j, rows, :BIG]
                ks = kh_ref[0, j, rows, BIG:]
                if flip:
                    return (yc + kc * ac + ks * as_, ys + kc * as_ - ks * ac)
                return (yc + kc * ac - ks * as_, ys + kc * as_ + ks * ac)

            yc, ys = lax.fori_loop(0, (count - i) if flip else (i + 1), inner, (zero, zero))
            at = pl.ds(pl.multiple_of((base + i) * cc + off, rg), rg)
            yh_s[at, :BIG] = yc.astype(bf16)
            yh_s[at, BIG:] = ys.astype(bf16)

        over_pieces(nseq, cc, rg, seq_ref, piece)

    @pl.when(pl.program_id(0) == 0)
    def _():
        products(False)

    @pl.when(pl.program_id(0) == 1)
    def _():
        products(True)

    for h in range(pieces):
        at = pl.ds(h * cc, cc)
        y_s[at, :] = nn(yh_s[at, :], back_ref[...])

    def one(b, y):
        y_ref[0, b] = y.astype(bf16)
        mix_ref[0, b] = (y * gg_ref[0, b].astype(f32)).astype(bf16)

    def last(h, carry):
        b = tab_ref[0, h]
        at = pl.ds(pl.multiple_of(h * cc, cc), cc)
        one(b, y_s[at, 0:BLK])

        @pl.when(tab_ref[1, h] == 1)
        def _():
            one(b + 1, y_s[at, BLK:])

        return carry

    lax.fori_loop(0, seq_ref[1, nseq], last, 0)
    nothing = jnp.zeros((cc, BLK), bf16)

    def fill(b, carry):
        y_ref[0, b] = nothing
        mix_ref[0, b] = nothing
        return carry

    lax.fori_loop(seq_ref[0, nseq], nb, fill, 0)


def back_body(
    nb, nseq, cc, rg, flip, tab_ref, seq_ref, a_ref, gm_ref, kh_ref, wave_ref, back_ref, gg_ref, y_ref, dg_ref, da_ref,
    gpg_ref, gp_ref, gh_ref, bs_ref, in_s, ah_s, gh_s, xh_s, x_s,
):
    pieces = (nb + nseq) // 2
    load_pieces(nb, pieces, cc, tab_ref, lambda b: a_ref[0, b].astype(f32), in_s, wave_ref, ah_s)
    load_pieces(
        nb, pieces, cc, tab_ref, lambda b: gm_ref[0, b].astype(f32) * gg_ref[0, b].astype(f32), in_s, wave_ref, gh_s
    )
    gh_ref[...] = jnp.zeros_like(gh_ref)
    zero = jnp.zeros((rg, BIG), f32)

    def piece(i, count, base, off):
        at = pl.ds(pl.multiple_of((base + i) * cc + off, rg), rg)
        ac = ah_s[at, :BIG]
        as_ = ah_s[at, BIG:]

        def inner(j, acc):
            xc, xs = acc
            other = (base + i - j) if flip else (base + i + j)
            m = pl.ds(pl.multiple_of(other * cc + off, rg), rg)
            rows = pl.ds(off, rg)
            gc = gh_s[m, :BIG]
            gs = gh_s[m, BIG:]
            kc = kh_ref[0, j, rows, :BIG]
            ks = kh_ref[0, j, rows, BIG:]
            gh_ref[0, j, rows, :BIG] += ac * gc + as_ * gs
            if flip:
                gh_ref[0, j, rows, BIG:] += gc * as_ - gs * ac
                return (xc + kc * gc - ks * gs, xs + kc * gs + ks * gc)
            gh_ref[0, j, rows, BIG:] += ac * gs - as_ * gc
            return (xc + kc * gc + ks * gs, xs + kc * gs - ks * gc)

        xc, xs = lax.fori_loop(0, (i + 1) if flip else (count - i), inner, (zero, zero))
        xh_s[at, :BIG] = xc.astype(bf16)
        xh_s[at, BIG:] = xs.astype(bf16)

    over_pieces(nseq, cc, rg, seq_ref, piece)

    for h in range(pieces):
        at = pl.ds(h * cc, cc)
        x_s[at, :] = nn(xh_s[at, :], back_ref[...])

    none = jnp.zeros((cc, BLK), f32)

    def one(b, gx, carry):
        s0, s1 = carry
        gpg = (y_ref[0, b].astype(f32) * gm_ref[0, b].astype(f32) * dg_ref[0, b].astype(f32)).astype(bf16)
        gpg_ref[0, b] = gpg
        gp = (gx * da_ref[0, b].astype(f32)).astype(bf16)
        gp_ref[0, b] = gp
        return (s0 + gpg.astype(f32), s1 + gp.astype(f32))

    def last(h, carry):
        b = tab_ref[0, h]
        at = pl.ds(pl.multiple_of(h * cc, cc), cc)
        carry = one(b, x_s[at, 0:BLK], carry)

        def more(kept):
            return one(b + 1, x_s[at, BLK:], kept)

        return lax.cond(tab_ref[1, h] == 1, more, lambda kept: kept, carry)

    s0, s1 = lax.fori_loop(0, seq_ref[1, nseq], last, (none, none))
    bs_ref[0, :, 0:BLK] = s0
    bs_ref[0, :, BLK:] = s1
    nothing = jnp.zeros((cc, BLK), bf16)

    def fill(b, carry):
        gpg_ref[0, b] = nothing
        gp_ref[0, b] = nothing
        return carry

    lax.fori_loop(seq_ref[0, nseq], nb, fill, 0)


def ssm_specs(shape, seq):
    _, nb, ch, _ = shape
    nseq = seq.shape[1] - 1
    pieces = (nb + nseq) // 2
    cc = chunk_of(ch, 128 if nb <= 32 else 64)
    big = pl.BlockSpec((1, nb, cc, BLK), lambda k, i: (k, 0, i, 0))
    spec = pl.BlockSpec((1, LAGS, cc, 2 * BIG), lambda k, i: (k, 0, i, 0))
    smem = pl.BlockSpec(memory_space=pltpu.SMEM)
    head = [smem, smem]
    tables = [pl.BlockSpec((BIG, 2 * BIG), lambda k, i: (0, 0)), pl.BlockSpec((2 * BIG, BIG), lambda k, i: (0, 0))]
    return nb, nseq, ch, cc, pieces * cc, big, spec, head, tables


def ssm_scan(tab, seq, a, kh, wave, back, gg):
    nb, nseq, ch, cc, size, big, spec, head, tables = ssm_specs(a.shape, seq)
    return pl.pallas_call(
        partial(scan_body, nb, nseq, cc, 32),
        grid=(2, ch // cc),
        in_specs=head + [big, spec] + tables + [big],
        out_specs=[big, big],
        out_shape=[jax.ShapeDtypeStruct(a.shape, bf16)] * 2,
        scratch_shapes=[
            pltpu.VMEM((size, BIG), bf16),
            pltpu.VMEM((size, 2 * BIG), f32),
            pltpu.VMEM((size, 2 * BIG), bf16),
            pltpu.VMEM((size, BIG), f32),
        ],
        compiler_params=params(56),
        cost_estimate=cost(2 * ch * 50e6, 2 * ch * nb * BLK * 8),
    )(tab, seq, a, kh, wave, back, gg)


def ssm_back(k, tab, seq, a, gm, kh, wave, back, gg, y, dg, da):
    nb, nseq, ch, cc, size, _, _, head, tables = ssm_specs(a.shape, seq)
    big = pl.BlockSpec((1, nb, cc, BLK), lambda i: (k, 0, i, 0))
    spec = pl.BlockSpec((1, LAGS, cc, 2 * BIG), lambda i: (k, 0, i, 0))
    out = pl.BlockSpec((1, nb, cc, BLK), lambda i: (0, 0, i, 0))
    out_spec = pl.BlockSpec((1, LAGS, cc, 2 * BIG), lambda i: (0, 0, i, 0))
    tables = [
        pl.BlockSpec((BIG, 2 * BIG), lambda i: (0, 0)),
        pl.BlockSpec((2 * BIG, BIG), lambda i: (0, 0)),
    ]
    return pl.pallas_call(
        partial(back_body, nb, nseq, cc, 64, k == 1),
        grid=(ch // cc,),
        in_specs=head + [big, big, spec] + tables + [big] * 4,
        out_specs=[out, out, out_spec, pl.BlockSpec((1, cc, 2 * BLK), lambda i: (0, i, 0))],
        out_shape=[jax.ShapeDtypeStruct((1,) + a.shape[1:], bf16)] * 2
        + [
            jax.ShapeDtypeStruct((1, LAGS, ch, 2 * BIG), f32),
            jax.ShapeDtypeStruct((1, ch, 2 * BLK), f32),
        ],
        scratch_shapes=[
            pltpu.VMEM((size, BIG), bf16),
            pltpu.VMEM((size, 2 * BIG), f32),
            pltpu.VMEM((size, 2 * BIG), f32),
            pltpu.VMEM((size, 2 * BIG), bf16),
            pltpu.VMEM((size, BIG), f32),
        ],
        compiler_params=params(60),
        cost_estimate=cost(ch * 80e6, ch * nb * BLK * 16),
    )(tab, seq, a, gm, kh, wave, back, gg, y, dg, da)


def stack_pair(refs):
    return jnp.concatenate(
        [jnp.concatenate([ref[k, 0], ref[k, 1]], axis=1) for ref in refs for k in range(ref.shape[0])], axis=0
    )


def mul_body(count, more, start_ref, w_ref, *refs):
    out = nn(w_ref[...], stack_pair(refs[:count]))
    o_ref = refs[-1]
    for h in range(2):
        part = out[:, h * BLK : (h + 1) * BLK]
        if more:
            part = part + refs[count][h].astype(f32)
        o_ref[h] = part.astype(o_ref.dtype)


def mul_rows(w, arrays, start, many, dtype=bf16, extra=None):
    width, deep = w.shape
    ch = arrays[0].shape[2]
    count = len(arrays)
    out = pl.BlockSpec((2, width, BLK), lambda i, at: (i, 0, 0))
    return pl.pallas_call(
        partial(mul_body, count, extra is not None),
        grid_spec=pltpu.PrefetchScalarGridSpec(
            num_scalar_prefetch=1,
            grid=(many // 2,),
            in_specs=[pl.BlockSpec((width, deep), lambda i, at: (0, 0))]
            + [pl.BlockSpec((x.shape[0], 2, ch, BLK), lambda i, at: (0, at[0] + i, 0, 0)) for x in arrays]
            + ([] if extra is None else [out]),
            out_specs=out,
        ),
        out_shape=jax.ShapeDtypeStruct((many, width, BLK), dtype),
        compiler_params=params(40),
        cost_estimate=cost(2 * many * BLK * width * deep, 2 * many * BLK * (2 * width + deep)),
    )(start // 2, w, *arrays, *([] if extra is None else [extra]))


def outer_body(ch, many, cuts, parts, at_ref, *refs):
    step = pl.program_id(0)
    xs, gs = refs[:parts], refs[parts : 2 * parts]
    gp_refs, gpg_refs, mix_ref = refs[2 * parts : 2 * parts + 2], refs[2 * parts + 2 : 2 * parts + 4], refs[2 * parts + 4]
    outs = refs[2 * parts + 5 : 2 * parts + 5 + cuts]
    acc_s, x_s, g_s = refs[-3:]

    def fill(at):
        for b in range(many):
            x_s[:, b * BLK : (b + 1) * BLK] = xs[at][b]
            g_s[:, b * BLK : (b + 1) * BLK] = gs[at][b]

    if parts == 1:
        fill(0)
    else:
        for at in range(parts):

            @pl.when(step == at)
            def _(at=at):
                fill(at)

    def part(ref, k):
        return jnp.concatenate([ref[k, b] for b in range(many)], axis=1)

    @pl.when(step == 0)
    def _():
        acc_s[...] = jnp.zeros_like(acc_s)

    split = 4 * ch
    left = jnp.concatenate([part(ref, 0) for ref in (*gp_refs, *gpg_refs)], axis=0)
    acc_s[:, :split] += nt(x_s[...], left)
    acc_s[:, split:] += nt(g_s[...], jnp.concatenate([part(mix_ref, 0), part(mix_ref, 1)], axis=0))

    @pl.when(step == pl.num_programs(0) - 1)
    def _():
        deep = acc_s.shape[0] // cuts
        for cut in range(cuts):
            start = pl.multiple_of(at_ref[pl.num_programs(0) + cut] * deep, 8)
            outs[cut][...] = acc_s[pl.ds(start, deep), :].astype(bf16)


def outer_sums(order, cuts, xs, gs, gp, gpg, mix):
    width = xs[0].shape[1]
    _, nb, ch, _ = mix.shape
    many = 8
    parts = len(xs)
    if parts == 1:
        rows = pl.BlockSpec((many, width, BLK), lambda i, at: (i, 0, 0))
    else:
        rows = pl.BlockSpec((many, width, BLK), lambda i, at: (0, 0, 0), pipeline_mode=pl.Buffered(1))
    chan = pl.BlockSpec((2, many, ch, BLK), lambda i, at: (0, at[i], 0, 0))
    one = pl.BlockSpec((1, many, ch, BLK), lambda i, at: (0, at[i], 0, 0))
    tok = nb * BLK
    return pl.pallas_call(
        partial(outer_body, ch, many, cuts, parts),
        grid_spec=pltpu.PrefetchScalarGridSpec(
            num_scalar_prefetch=1,
            grid=(nb // many,),
            in_specs=[rows] * (2 * parts) + [one] * 4 + [chan],
            out_specs=[pl.BlockSpec((width // cuts, 6 * ch), lambda i, at: (0, 0))] * cuts,
            scratch_shapes=[
                pltpu.VMEM((width, 6 * ch), f32),
                pltpu.VMEM((width, many * BLK), bf16),
                pltpu.VMEM((width, many * BLK), bf16),
            ],
        ),
        out_shape=[jax.ShapeDtypeStruct((width // cuts, 6 * ch), bf16)] * cuts,
        compiler_params=params(60),
        cost_estimate=cost(12 * tok * width * ch, tok * (4 * width + 12 * ch)),
    )(order, *xs, *gs, *gp, *gpg, mix)


def join_body(split, w_ref, head_ref, tail_ref, head_t_ref, tail_t_ref):
    head_ref[...] = w_ref[:, :split]
    tail_ref[...] = w_ref[:, split:]
    head_t_ref[...] = w_ref[:, :split].T
    tail_t_ref[...] = w_ref[:, split:].T


def split_weights(w, split):
    rows, wide = w.shape
    vmem = pl.BlockSpec(memory_space=pltpu.VMEM)
    return pl.pallas_call(
        partial(join_body, split),
        in_specs=[vmem],
        out_specs=[vmem] * 4,
        out_shape=[
            jax.ShapeDtypeStruct(shape, bf16)
            for shape in ((rows, split), (rows, wide - split), (split, rows), (wide - split, rows))
        ],
        compiler_params=params(48),
        cost_estimate=cost(0, 6 * rows * wide),
    )(w)


def meet_body(
    axes, rank_ref, x_ref, chan_ref, norm_ref, pack_ref, got_ref, call_ref, nall_ref, wall_ref, send_s, *sems
):
    xs_sem, xr_sem, cs_sem, cr_sem, ns_sem, nr_sem, ws_sem, wr_sem, own_sem = sems
    q, c, h, w = (lax.axis_index(name) for name in axes)
    rows = x_ref.shape[0]
    piece = rows // 8
    flat = ((2 * q + c) * 2 + h) * 2 + w

    def peer(bits):
        return (q ^ (bits // 8), c ^ (bits // 4 % 2), h ^ (bits // 2 % 2), w ^ (bits % 2))

    barrier = pltpu.get_barrier_semaphore()
    for bits in range(1, 32):
        pl.semaphore_signal(barrier, inc=1, device_id=peer(bits), device_id_type=pl.DeviceIdType.MESH)
    pl.semaphore_wait(barrier, 31)

    def remote(src, dst, send, recv, to):
        return pltpu.make_async_remote_copy(
            src_ref=src, dst_ref=dst, send_sem=send, recv_sem=recv, device_id=to, device_id_type=pl.DeviceIdType.MESH
        )

    deep = pack_ref.shape[0]

    def shard(at):
        return wall_ref.at[pl.ds(pl.multiple_of(at * deep, 16), deep)]

    def first_copy():
        return remote(pack_ref, shard(2 * q + c), ws_sem.at[0], wr_sem.at[c], (q, 1 - h, c, w))

    def second_copy():
        return remote(pack_ref, shard(2 * q + c), ws_sem.at[1], wr_sem.at[c], (q, 1 - h, 1 - c, w))

    def own_shard():
        return pltpu.make_async_copy(pack_ref, shard(2 * q + c), own_sem.at[2])

    def shard_came(at):
        return remote(pack_ref, shard(2 * q + at), ws_sem.at[0], wr_sem.at[at], peer(1))

    def pass_on(at, bits):
        spot_w = 3 * at + bits + 1
        return remote(shard(2 * q + at), shard(2 * q + at), ws_sem.at[spot_w], wr_sem.at[spot_w], (q ^ bits, c, h, w))

    first_copy().start()

    @pl.when(c != h)
    def _():
        own_shard().start()

    @pl.when(c == h)
    def _():
        second_copy().start()

    nall_ref[flat] = norm_ref[...]

    def norm_copy(bits):
        return remote(norm_ref, nall_ref.at[flat], ns_sem.at[bits], nr_sem.at[bits], peer(bits))

    for bits in range(1, 32):
        norm_copy(bits).start()

    pieces = [(kq, kh) for kh in (0, 1) for kq in (1, 2, 3, 0)]
    spot = lax.broadcasted_iota(jnp.int32, (piece, rows), 0)

    def row_copy(kq, kh):
        at = 2 * kq + kh
        return remote(
            send_s.at[at], got_ref.at[2 * q + c], xs_sem.at[at], xr_sem.at[2 * kq + c], (q ^ kq, 1 - h, h ^ kh, w)
        )

    def own_copy():
        return pltpu.make_async_copy(send_s.at[0], got_ref.at[2 * q + c], own_sem.at[0])

    for kq, kh in pieces:
        chunk = 2 * (q ^ kq) + (h ^ kh)
        pick = jnp.where(spot + chunk * piece == rank_ref[...], 1.0, 0.0).astype(bf16)
        send_s[2 * kq + kh] = nn(pick, x_ref[...]).astype(bf16)
        if (kq, kh) == (1, 1):
            for at in range(2):

                @pl.when((c != h) & (at == c))
                def _():
                    own_shard().wait()

                @pl.when(jnp.logical_not((c != h) & (at == c)))
                def _(at=at):
                    shard_came(at).wait_recv()

                for bits in range(1, 4):
                    pass_on(at, bits).start()
        if (kq, kh) == (0, 0):

            @pl.when(c != h)
            def _():
                own_copy().start()

            @pl.when(c == h)
            def _():
                row_copy(0, 0).start()

        else:
            row_copy(kq, kh).start()

    place = 2 * (1 - c) + w
    spot_c = 4 * c + 2 * h + w

    def chan_copy(at):
        to = (q ^ at, 1 - q // 2, h, q % 2) if at < 4 else (2 * c + w, 1 - q // 2, 1 - h, q % 2)
        return remote(chan_ref, call_ref.at[spot_c], cs_sem.at[at], cr_sem.at[spot_c], to)

    def own_chan():
        return pltpu.make_async_copy(chan_ref, call_ref.at[spot_c], own_sem.at[1])

    def chan_came(at):
        return remote(chan_ref, call_ref.at[at], cs_sem.at[0], cr_sem.at[at], peer(1))

    far_spot = 4 * (q // 2) + 2 * (1 - h) + q % 2

    def chan_pass(bits):
        return remote(
            call_ref.at[far_spot], call_ref.at[far_spot], cs_sem.at[4 + bits], cr_sem.at[far_spot], (q ^ bits, c, h, w)
        )

    for at in (4, 1, 2, 3, 0):
        if at:
            chan_copy(at).start()
        else:

            @pl.when(place == q)
            def _():
                own_chan().start()

            @pl.when(place != q)
            def _():
                chan_copy(0).start()

    for bits in range(1, 32):
        norm_copy(bits).wait()
    for at in range(8):

        @pl.when((c != h) & (at == c))
        def _():
            own_copy().wait()

        @pl.when(jnp.logical_not((c != h) & (at == c)))
        def _(at=at):
            remote(send_s.at[at], got_ref.at[at], xs_sem.at[at], xr_sem.at[at], peer(1)).wait_recv()

    chan_came(far_spot).wait_recv()
    for bits in range(1, 4):
        chan_pass(bits).start()
    for at in range(8):

        @pl.when((place == q) & (at == spot_c))
        def _():
            own_chan().wait()

        @pl.when(jnp.logical_not((place == q) & (at == spot_c)) & (at != far_spot))
        def _(at=at):
            chan_came(at).wait_recv()

    for bits in range(1, 4):
        chan_pass(bits).wait_send()
    for at in range(2):
        for bits in range(1, 4):
            pass_on(at, bits).wait()
    first_copy().wait_send()

    @pl.when(c == h)
    def _():
        second_copy().wait_send()

    for kq, kh in pieces:
        if (kq, kh) == (0, 0):

            @pl.when(c == h)
            def _():
                row_copy(0, 0).wait_send()

        else:
            row_copy(kq, kh).wait_send()
    for at in range(1, 5):
        chan_copy(at).wait_send()

    @pl.when(place != q)
    def _():
        chan_copy(0).wait_send()


def meet(axes, rank, x, chan, norm, pack):
    rows, width = x.shape
    vmem = pl.BlockSpec(memory_space=pltpu.VMEM)
    sem = pltpu.SemaphoreType.DMA
    return pl.pallas_call(
        partial(meet_body, axes),
        in_specs=[vmem] * 5,
        out_specs=[vmem] * 4,
        out_shape=[
            jax.ShapeDtypeStruct((8, rows // 8, width), bf16),
            jax.ShapeDtypeStruct((8,) + chan.shape, f32),
            jax.ShapeDtypeStruct((32,) + norm.shape, f32),
            jax.ShapeDtypeStruct((8 * pack.shape[0], pack.shape[1]), bf16),
        ],
        scratch_shapes=[pltpu.VMEM((8, rows // 8, width), bf16)]
        + [sem((8,)), sem((8,)), sem((8,)), sem((8,)), sem((32,)), sem((32,)), sem((8,)), sem((8,)), sem((3,))],
        compiler_params=pltpu.CompilerParams(collective_id=1, has_side_effects=True, vmem_limit_bytes=60 * MIB),
        cost_estimate=cost(2 * rows * rows * width, 100 * rows * width),
    )(rank.reshape(1, rows), x, chan, norm, pack)


def sequence_tables(lens, nb):
    nseq = lens.shape[0]
    blocks = (lens + BLK - 1) // BLK
    start = jnp.cumsum(blocks) - blocks
    bigs = (blocks + 1) // 2
    first_big = jnp.cumsum(bigs) - bigs
    h = jnp.arange((nb + nseq) // 2, dtype=jnp.int32)
    owner = (h[:, None] >= first_big[None, :]).astype(jnp.int32).sum(axis=1) - 1
    mine = owner[:, None] == jnp.arange(nseq, dtype=jnp.int32)[None, :]

    def at_owner(values):
        return jnp.sum(jnp.where(mine, values[None, :], 0), axis=1)

    rel = h - at_owner(first_big)
    first = jnp.minimum(at_owner(start) + 2 * rel, nb - 1)
    whole = (2 * rel + 1 < at_owner(blocks)).astype(jnp.int32)
    tab = jnp.stack([first, whole]).astype(jnp.int32)
    seq = jnp.stack(
        [jnp.append(first_big, jnp.sum(blocks)), jnp.append(bigs, jnp.sum(bigs))]
    ).astype(jnp.int32)
    return tab, seq


def live_rows(lens, rows):
    slot = (lens + BLK - 1) // BLK * BLK
    begin = jnp.cumsum(slot) - slot
    pos = jnp.arange(rows, dtype=jnp.int32)
    inside = (pos[:, None] >= begin[None, :]) & (pos[:, None] < (begin + lens)[None, :])
    return jnp.sum(inside.astype(f32), axis=1)


def after(values):
    return lax.optimization_barrier(values)


def rank_of(keys):
    return jnp.sum((keys[None, :] < keys[:, None]).astype(jnp.int32), axis=1)


class Line:
    def __init__(self, n_dp, n_t):
        self.n_dp, self.n_t = n_dp, n_t
        self.axes = {"dp": n_dp, "tensor": n_t}
        self.both = ("dp", "tensor")
        self.cuts = 1

    def place_of_group(self):
        return lax.axis_index("tensor")

    def regroup(self, x):
        return x

    def gather_first(self, x):
        return [lax.all_gather(x, "tensor", axis=0, tiled=True)]

    def gathered(self, x, early):
        return []

    def gather_last(self, x, got):
        return [(got[0], jnp.zeros((1,), jnp.int32))]

    def scatter_first(self, w, arrays, many):
        return [mul_rows(w, arrays, jnp.zeros((1,), jnp.int32), many * self.n_t)]

    def scatter_send(self, parts):
        return [lax.psum_scatter(parts[0], "tensor", scatter_dimension=0, tiled=True)]

    def scatter_own(self, w, arrays, many):
        return []

    def ungroup(self, x):
        return x

    def spread(self, x):
        return lax.all_to_all(x, "dp", split_axis=0, concat_axis=0, tiled=True)

    def order(self, pieces):
        return jnp.append(jnp.arange(pieces * self.n_t, dtype=jnp.int32), 0)

    def enter(self, rank, x, chan, norm, pack):
        (sent,) = permute_to(rank, [x])
        return (self.spread(sent),) + self.gather_channels(chan, norm) + (lax.all_gather(pack, "dp", axis=0, tiled=True),)

    def gather_channels(self, chan, norm):
        perm = [(f, (f % self.n_dp) * self.n_t + f // self.n_dp) for f in range(self.n_dp * self.n_t)]
        chan = lax.ppermute(chan, self.both, perm)
        norm = lax.all_gather(norm, self.both, axis=1, tiled=True)
        return lax.all_gather(chan[None], "dp", axis=0, tiled=True), norm

    def cut_order(self):
        return jnp.zeros((1,), jnp.int32)

    def grads_send(self, gw):
        return [lax.psum_scatter(gw[0], "dp", scatter_dimension=0, tiled=True)]

    def grads_last(self, parts):
        return parts[0].astype(f32)

    def scatter_channels(self, sums):
        return lax.psum_scatter(sums, "dp", scatter_dimension=0, tiled=True)

    def owner_channels(self, sums):
        perm = [((f % self.n_dp) * self.n_t + f // self.n_dp, f) for f in range(self.n_dp * self.n_t)]
        return lax.ppermute(sums, self.both, perm)

    def scatter_norm(self, sums):
        return lax.psum_scatter(sums, self.both, scatter_dimension=1, tiled=True)


class Pairs:
    def __init__(self, n_dp, n_t):
        self.quads = n_dp // 2
        self.axes = {"q": self.quads, "c": 2, "h": 2, "w": 2}
        self.both = ("q", "c", "h", "w")
        self.cuts = self.quads
        self.other = [(0, 1), (1, 0)]
        self.there = [(2 * c + h, 2 * (1 - h) + c) for c in range(2) for h in range(2)]
        self.back = [(b, a) for a, b in self.there]
        self.turned = [(2 * c + h, 2 * (1 - h) + 1 - c) for c in range(2) for h in range(2)]

    def flip(self, x, axis, bit=1):
        return lax.ppermute(x, axis, [(i, i ^ bit) for i in range(self.axes[axis])])

    def place_of_group(self):
        return 2 * (1 - lax.axis_index("c")) + lax.axis_index("w")

    def regroup(self, x):
        return lax.ppermute(x, ("c", "h"), self.there)

    def ungroup(self, x):
        return lax.ppermute(x, ("c", "h"), self.back)

    def spread(self, x):
        return lax.all_to_all(x, ("q", "c"), split_axis=0, concat_axis=0, tiled=True)

    def places(self):
        c, w = lax.axis_index("c"), lax.axis_index("w")
        return [2 * (1 - c) + w, 2 * c + w, 2 * (1 - c) + 1 - w, 2 * c + 1 - w]

    def starts(self, many):
        return [(place * many).astype(jnp.int32).reshape(1) for place in self.places()]

    def gather_first(self, x):
        return [self.flip(x, "c"), self.flip(x, "w")]

    def gathered(self, x, early):
        return list(zip([x] + early, self.starts(x.shape[0])))

    def gather_last(self, x, got):
        beside, near = got
        return list(zip([x, beside, near, self.flip(near, "c")], self.starts(x.shape[0])))

    def scatter_first(self, w, arrays, many):
        _, beside, near, far = self.starts(many)
        first = mul_rows(w, arrays, far, many)
        give = self.flip(first, "c")
        beside, first = after((beside, first))
        second = mul_rows(w, arrays, beside, many)
        second, give = after((second, give))
        return [second, mul_rows(w, arrays, near, many, extra=give)]

    def scatter_send(self, parts):
        return [self.flip(parts[0], "c"), self.flip(parts[1], "w")]

    def scatter_own(self, w, arrays, many):
        return [mul_rows(w, arrays, self.starts(many)[0], many, dtype=f32)]

    def order(self, pieces):
        place = jnp.stack(self.places())[:, None] * pieces + jnp.arange(pieces)[None, :]
        return jnp.concatenate([place.reshape(-1).astype(jnp.int32), self.cut_order()])

    def steps(self):
        bit = self.quads // 2
        while bit:
            yield "q", bit
            bit //= 2
        yield "h", 1

    def spot(self):
        return 2 * lax.axis_index("q") + lax.axis_index("h")

    def enter(self, rank, x, chan, norm, pack):
        small = norm.shape[1]
        norm = jnp.pad(norm, ((0, 5), (0, BLK - small)))
        got, chan, norm, weights = meet(self.both, rank, x, chan, norm, pack)
        norm = norm[:, :3, :small].transpose(1, 0, 2).reshape(3, -1)
        return got.reshape(x.shape), chan, norm, weights

    def grads_send(self, gw):
        return [gw[0]] + [self.flip(gw[bit], "q", bit) for bit in range(1, self.quads)]

    def grads_last(self, parts):
        total = parts[0].astype(f32)
        for part in parts[1:]:
            total = total + part.astype(f32)
        total = total.astype(bf16)
        half = total.shape[0] // 2
        h = lax.axis_index("h")
        first = jnp.where(h == 0, total[:half], total[half:])
        second = jnp.where(h == 0, total[half:], total[:half])
        return self.ungroup(first).astype(f32) + lax.ppermute(second, ("c", "h"), self.turned).astype(f32)

    def cut_order(self):
        return (lax.axis_index("q") ^ jnp.arange(self.quads)).astype(jnp.int32)

    def scatter_channels(self, sums):
        count = 2 * self.quads
        rows, wide = sums.shape[0] // count, sums.shape[1]
        sums = jnp.pad(sums, ((0, 0), (0, -wide % 8))).reshape(count, -1, BLK)
        sums = jnp.take(sums, jnp.arange(count) ^ self.spot(), axis=0)
        total = None
        for apart in range(count):
            perm = []
            for source in range(4 * count):
                q, c, h, w = source // 8, source // 4 % 2, source // 2 % 2, source % 2
                perm.append((source, count * (2 * (1 - c) + w) + ((2 * q + h) ^ apart)))
            part = lax.ppermute(sums[apart], self.both, perm)
            total = part if total is None else total + part
        return total.reshape(rows, -1)[:, :wide]

    def owner_channels(self, sums):
        return sums

    def scatter_norm(self, sums):
        count = 8 * self.quads
        part = sums.reshape(3, count, -1).transpose(1, 0, 2)
        wide = part.shape[2]
        part = jnp.pad(part, ((0, 0), (0, 5), (0, BLK - wide)))
        part = lax.all_to_all(part, self.both, split_axis=0, concat_axis=0, tiled=True)
        return jnp.sum(part, axis=0)[:3, :wide]


def local(
    net, wave, tokens, cotangent, source, target, lengths, ln_gain, ln_bias, w_fwd, b_fwd, w_bwd, b_bwd,
    w_gate, b_gate, w_out, b_out, log_dt, log_rate, ssm_b, ssm_c, ssm_d,
):
    rows, width = tokens.shape
    many = rows // BLK
    n_t = net.n_t
    group = rows * n_t
    nb = group // BLK
    ch = w_fwd.shape[1]
    back = (wave.T / BIG).astype(bf16)
    wave = wave.astype(bf16)

    def lanes(column):
        return jnp.broadcast_to(column[..., None], column.shape + (BLK,))

    def decays(log_dt, log_rate, ssm_b):
        rate = jnp.exp(log_rate)
        ld = -jnp.exp(log_dt)[..., None] * rate
        return rate, ld, (1.0 - jnp.exp(ld)) / rate * ssm_b

    rank = rank_of(target)
    sender = source // group
    place = rank_of(sender * rows + jnp.arange(rows, dtype=jnp.int32))
    pack = jnp.concatenate(
        [w_fwd, w_bwd, w_gate.reshape(-1, 2 * ch), w_out.transpose(2, 0, 1).reshape(-1, 2 * ch)], axis=1
    )
    table = net.regroup(jnp.concatenate([place, lengths[0]]))
    rate, ld, drive = decays(log_dt, log_rate, ssm_b)
    own = b_fwd.shape[0]
    small = jnp.concatenate([ssm_d, b_fwd[None], b_bwd[None], b_gate])
    chan = jnp.concatenate(
        [
            (ld * log2e).reshape(own, 2 * STATE),
            (ssm_c * drive).reshape(own, 2 * STATE),
            jnp.pad(small, ((0, -(2 * own + 6) % 8 + 0), (0, 2 * STATE - own))),
        ]
    )
    norm = jnp.stack([ln_gain, ln_bias, b_out])
    got_x, chan_all, norm_all, w_all = net.enter(rank, tokens, chan, norm, pack)
    got_x, chan_all, norm_all, w_all, table, cotangent = after((got_x, chan_all, norm_all, w_all, table, cotangent))

    place, lens = table[:rows], table[rows:]
    gain = lanes(norm_all[0])
    shift = lanes(norm_all[1])
    small = chan_all[:, 2 * own : 2 * own + 6, :own].transpose(1, 0, 2).reshape(6, ch)

    def pairs(at):
        both = chan_all[:, at : at + own].reshape(-1, 2, own // 2, 2 * STATE)
        return both.transpose(1, 0, 2, 3).reshape(2, ch // 2, 2 * STATE)

    ld_pairs = pairs(0)
    w_pairs = pairs(own)
    skip = lanes(small[0:2])
    live = live_rows(lens, group)
    live_own = lax.dynamic_slice_in_dim(live, net.place_of_group() * rows, rows, 0).reshape(many, 1, BLK)
    live = live.reshape(nb // 2, 1, BIG)
    tab, seq = sequence_tables(lens, nb)

    xt, xd = deal_x(place, got_x, gain, shift)
    xt, cotangent, ld_pairs, w_pairs, skip, w_all = after((xt, cotangent, ld_pairs, w_pairs, skip, w_all))
    x_got = net.gather_first(xt)
    (sent_g,) = permute_to(rank, [cotangent])
    got_g = net.spread(sent_g)
    kh = spectra(ld_pairs, w_pairs, skip, wave)
    w_in, w_back, w_in_t, w_back_t = split_weights(w_all, 4 * ch)
    bias_in = lanes(small[2:6].reshape(-1))
    bias_out = lanes(norm_all[2])
    early, got_g, kh, w_in_t, bias_in = after((x_got[:-1], got_g, kh, w_in_t, bias_in))
    got_g = net.regroup(got_g)
    kept = None
    for part, start in net.gathered(xt, early):
        kept = project(part, start, nb, live, w_in_t, bias_in, kept)
    kept, late = after((kept, x_got[-1]))
    xs = net.gather_last(xt, early + [late])
    for part, start in xs[len(early) + 1 if early else 0 :]:
        kept = project(part, start, nb, live, w_in_t, bias_in, kept)
    kept, got_g = after((kept, got_g))
    a, da, gg, dg = kept
    gt, gd, g_bias_out = deal_g(place, got_g, live_own)
    gt, a = after((gt, a))
    g_got = net.gather_first(gt)
    y, mix = ssm_scan(tab, seq, a, kh, wave, back, gg)
    g_got, y, mix = after((g_got, y, mix))
    gs = net.gather_last(gt, g_got)
    branch = net.scatter_first(w_back, [mix], many)
    gm = gate_grad(gs, nb, w_back_t)
    branch, gm = after((branch, gm))

    branch = net.scatter_send(branch)
    branch = net.scatter_own(w_back, [mix], many) + branch
    first = ssm_back(0, tab, seq, a, gm, kh, wave, back, gg, y, dg, da)
    branch, first, a = after((branch, first, a))
    sent_out = layer_rows(place, branch, xd, live_own, bias_out)
    sent_out, a = after((sent_out, a))
    sent_out = net.ungroup(sent_out)
    second = ssm_back(1, tab, seq, a, gm, kh, wave, back, gg, y, dg, da)
    sent_out, first, second = after((sent_out, first, second))
    gpg, gp, gh, bsum = zip(first, second)
    sent_out = net.spread(sent_out)
    back_list = [gp[0], gp[1], gpg[0], gpg[1]]
    g_normed = net.scatter_first(w_in, back_list, many)
    g_normed, back_list, mix = after((g_normed, back_list, mix))
    gp, gpg = back_list[:2], back_list[2:]
    g_normed = net.scatter_send(g_normed)
    g_normed = net.scatter_own(w_in, back_list, many) + g_normed
    gw = outer_sums(net.order(many // 8), net.cuts, [part for part, _ in xs], [part for part, _ in gs], gp, gpg, mix)
    g_normed, gw, gh, sent_out = after((g_normed, gw, gh, sent_out))
    sent_in, norm_sums = input_rows(place, g_normed, xd, gd, gain)
    sent_in, gh, gw, norm_sums, sent_out, bsum = after((sent_in, gh, gw, norm_sums, sent_out, bsum))
    sent_in = net.ungroup(sent_in)
    gw = net.grads_send(gw)
    s0, s1, g0 = [jnp.concatenate(part) for part in zip(*[moments(k, ld_pairs, gh[k], back) for k in range(2)])]
    layer_out = permute_from(rank, sent_out)

    s0 = s0.reshape(2, ch, STATE)
    s1 = s1.reshape(2, ch, STATE)
    bsum = jnp.concatenate(bsum)
    gb_gate = jnp.sum(bsum[:, :, :BLK], axis=2)
    gb_in = jnp.sum(bsum[:, :, BLK:], axis=2)
    sums = jnp.concatenate(
        [s0[0], s0[1], s1[0], s1[1], jnp.concatenate([g0[:, :, 0], gb_gate, gb_in], axis=0).T], axis=1
    )
    norm_sums = net.scatter_norm(jnp.sum(jnp.concatenate([norm_sums, g_bias_out[None]], axis=0), axis=2))
    sent_in, gw, sums, norm_sums, layer_out = after((sent_in, gw, sums, norm_sums, layer_out))
    in_grad = permute_from(rank, net.spread(sent_in))
    sums = net.owner_channels(net.scatter_channels(sums))
    gw = net.grads_last(gw)
    s0 = jnp.stack([sums[:, :STATE], sums[:, STATE : 2 * STATE]])
    s1 = jnp.stack([sums[:, 2 * STATE : 3 * STATE], sums[:, 3 * STATE : 4 * STATE]])
    tail = sums[:, 4 * STATE :].T
    step = jnp.exp(log_dt)[..., None]
    g_c = s0 * drive
    g_drive = s0 * ssm_c
    g_b = g_drive * (1.0 - jnp.exp(ld)) / rate
    g_ld = s1 * ssm_c * drive - g_drive * ssm_b / rate * jnp.exp(ld)
    g_rate = -g_drive * drive / rate - g_ld * step
    g_dt = jnp.sum(g_ld * ld, axis=2)
    return (
        layer_out,
        in_grad,
        norm_sums[0],
        norm_sums[1],
        gw[:, :ch],
        tail[4],
        gw[:, ch : 2 * ch],
        tail[5],
        gw[:, 2 * ch : 4 * ch].reshape(-1, 2, ch),
        tail[2:4],
        gw[:, 4 * ch :].T.reshape(2, ch, -1),
        norm_sums[2],
        g_dt,
        g_rate * rate,
        g_b,
        g_c,
        tail[0:2],
    )


def solution(mesh):
    n_dp, n_t = mesh.shape["dp"], mesh.shape["tensor"]
    if n_t == 4 and n_dp == 8:
        net = Pairs(n_dp, n_t)
        dp, tensor = ("q", "c"), ("h", "w")
    else:
        net = Line(n_dp, n_t)
        dp, tensor = ("dp",), ("tensor",)
    net.n_t = n_t
    mesh = jax.sharding.Mesh(mesh.devices.reshape(tuple(net.axes.values())), tuple(net.axes))
    both = P(dp + tensor)
    rows = P(dp + tensor, None)
    pair = P(None, dp + tensor)
    state = P(None, dp + tensor, None)
    proj = P(dp, tensor)
    gate = P(dp, None, tensor)
    out = P(None, tensor, dp)
    wave = wave_table()

    def run(*args):
        return local(net, jnp.asarray(wave), *args)

    return jax.shard_map(
        run,
        mesh=mesh,
        in_specs=(
            rows, rows, both, both, P(dp, None), both, both, proj, both, proj, both, gate, pair, out, both,
            pair, state, state, state, pair,
        ),
        out_specs=(
            rows, rows, both, both, proj, both, proj, both, gate, pair, out, both, pair, state, state, state, pair,
        ),
        check_vma=False,
    )
```

profile of v0, /device:TPU:1, one launch (start us, length us, event | category | flops | bytes accessed | tf_op | source)
XLA Modules:
  0.0 553.2 jit_solution(6341600461707385432)
XLA Ops:
  2.6 3.1 collective-permute-start
  5.7 1.9 convert_reduce_fusion.1
  15.6 73.1 %shard_map.332 = (bf16[8,128,768]{2,1,0:T(8,128)(2,1)}, f32[8,104,128]{2,1,0:T(8,128)}, f32[32,8,128]{2,1,0:T(8,128)}, bf16[768,2304]{1,0:T(8,128)(2,1)}) custom-call(s32[1,1024]{1,0:T(1,128)} %bitcast.141, bf16[1024,768]{1,0:T(8,128)(2,1)} %x_ref.1, f32[104,128]{1,0:T(8,128)} %pad_maximum_fusion.2.chan_ref, f32[8,128]{1,0:T(8,128)} %select_maximum_fusion.norm_ref, ...), custom_call_target="tpu_custom_call" | custom-call | flops 80530640 | bytes 3932160 | tf_op jit(solution)/shard_map/pallas_call | solution.py:1027
  96.0 8.9 %shard_map.333 = (bf16[8,768,128]{2,1,0:T(8,128)(2,1)}, bf16[8,768,128]{2,1,0:T(8,128)(2,1)}) custom-call(s32[1024,1]{1,0:T(8,128)} %copy.111.place_ref, bf16[1024,768]{1,0:T(8,128)(2,1)} %bitcast.124, f32[768,128]{1,0:T(8,128)} %broadcast_in_dim.97.gain_ref, f32[768,128]{1,0:T(8,128)} %broadcast_in_dim.99.shift_ref), custom_call_target="tpu_custom_call" | custom-call | flops 80530640 | bytes 235929 | tf_op jit(solution)/shard_map/pallas_call | solution.py:137
  105.9 4.6 collective-permute-start.1
  110.5 4.4 shard_map.334
  114.9 5.1 all-to-all-start
  120.1 5.8 %shard_map.336 = (bf16[768,1536]{1,0:T(8,128)(2,1)}, bf16[768,768]{1,0:T(8,128)(2,1)}, bf16[1536,768]{1,0:T(8,128)(2,1)}, bf16[768,768]{1,0:T(8,128)(2,1)}) custom-call(bf16[768,2304]{1,0:T(8,128)(2,1)} %get-tuple-element.182.w_ref), custom_call_target="tpu_custom_call" | custom-call | bytes 530841 | tf_op jit(solution)/shard_map/pallas_call | solution.py:821
  128.3 18.3 %shard_map.335.kh_ref = f32[2,8,384,512]{3,2,1,0:T(8,128)} custom-call(f32[2,192,128]{2,1,0:T(8,128)} %bitcast.120, f32[2,192,128]{2,1,0:T(8,128)} %bitcast.129, f32[2,384,128]{2,1,0:T(8,128)} %broadcast_in_dim.101.d_ref, bf16[256,512]{1,0:T(8,128)(2,1)} %constant.217.wave_ref), custom_call_target="tpu_custom_call" | custom-call | flops 1536000000 | bytes 629145 | tf_op jit(solution)/shard_map/pallas_call | solution.py:392
  148.1 8.4 %shard_map.337 = (bf16[2,32,384,128]{3,2,1,0:T(8,128)(2,1)}, bf16[2,32,384,128]{3,2,1,0:T(8,128)(2,1)}, bf16[2,32,384,128]{3,2,1,0:T(8,128)(2,1)}, bf16[2,32,384,128]{3,2,1,0:T(8,128)(2,1)}) custom-call(s32[1]{0:T(128)S(6)} %select_n.93.start_ref, bf16[8,768,128]{2,1,0:T(8,128)(2,1)} %get-tuple-element.177.x_ref.refs_0_, f32[16,1,256]{2,1,0:T(1,128)} %bitcast.132, ...), custom_call_target="tpu_custom_call" | custom-call | flops 120795952 | bytes 393216 | tf_op jit(solution)/shard_map/pallas_call | solution.py:273
  156.5 8.5 %shard_map.338 = (bf16[2,32,384,128]{3,2,1,0:T(8,128)(2,1)}, bf16[2,32,384,128]{3,2,1,0:T(8,128)(2,1)}, bf16[2,32,384,128]{3,2,1,0:T(8,128)(2,1)}, bf16[2,32,384,128]{3,2,1,0:T(8,128)(2,1)}) custom-call(s32[1]{0:T(128)S(6)} %select_n.91.start_ref, ...), custom_call_target="tpu_custom_call", output_to_operand_aliasing={{0}: (5, {}), {1}: (6, {}), {2}: (7, {}), {3}: (8, {})} | custom-call | flops 120795952 | bytes 393216 | tf_op jit(solution)/shard_map/pallas_call | solution.py:273
  167.2 8.5 %shard_map.339 = (bf16[2,32,384,128]{3,2,1,0:T(8,128)(2,1)}, bf16[2,32,384,128]{3,2,1,0:T(8,128)(2,1)}, bf16[2,32,384,128]{3,2,1,0:T(8,128)(2,1)}, bf16[2,32,384,128]{3,2,1,0:T(8,128)(2,1)}) custom-call(s32[1]{0:T(128)S(6)} %select_n.94.start_ref, ...), custom_call_target="tpu_custom_call", output_to_operand_aliasing={{0}: (5, {}), {1}: (6, {}), {2}: (7, {}), {3}: (8, {})} | custom-call | flops 120795952 | bytes 393216 | tf_op jit(solution)/shard_map/pallas_call | solution.py:273
  176.8 8.4 %shard_map.340 = (bf16[2,32,384,128]{3,2,1,0:T(8,128)(2,1)}, bf16[2,32,384,128]{3,2,1,0:T(8,128)(2,1)}, bf16[2,32,384,128]{3,2,1,0:T(8,128)(2,1)}, bf16[2,32,384,128]{3,2,1,0:T(8,128)(2,1)}) custom-call(s32[1]{0:T(128)S(6)} %select_n.90.start_ref, ...), custom_call_target="tpu_custom_call", output_to_operand_aliasing={{0}: (5, {}), {1}: (6, {}), {2}: (7, {}), {3}: (8, {})} | custom-call | flops 120795952 | bytes 393216 | tf_op jit(solution)/shard_map/pallas_call | solution.py:273
  185.2 8.1 %shard_map.341 = (bf16[8,768,128]{2,1,0:T(8,128)(2,1)}, bf16[8,768,128]{2,1,0:T(8,128)(2,1)}, f32[768,128]{1,0:T(8,128)}) custom-call(s32[1024,1]{1,0:T(8,128)} %copy.111.place_ref, bf16[1024,768]{1,0:T(8,128)(2,1)} %collective-permute-done.4.g_ref, f32[8,1,128]{2,1,0:T(1,128)} %bitcast.147), custom_call_target="tpu_custom_call" | custom-call | flops 80530640 | bytes 235929 | tf_op jit(solution)/shard_map/pallas_call | solution.py:152
  193.4 19.3 %collective-permute-start.5 = (bf16[8,768,128]{2,1,0:T(8,128)(2,1)}, bf16[8,768,128]{2,1,0:T(8,128)(2,1)S(1)}, u32[]{:S(2)}, u32[]{:S(2)}) collective-permute-start(bf16[8,768,128]{2,1,0:T(8,128)(2,1)} %get-tuple-element.215.refs_0_.refs_4_), channel_id=1, source_target_pairs={{0,4},{4,0},{1,5},{5,1},{2,6},{6,2},{3,7},{7,3},{8,12},{12,8},{9,1... | collective-permute-start | bytes 4718600 | tf_op jit(solution)/shard_map/ppermute | solution.py:1165
  215.4 36.5 %shard_map.342 = (bf16[2,32,384,128]{3,2,1,0:T(8,128)(2,1)}, bf16[2,32,384,128]{3,2,1,0:T(8,128)(2,1)}) custom-call(s32[2,17]{1,0:T(2,128)} %pad_add_fusion.1.tab_ref, s32[2,4]{1,0:T(2,128)} %pad_add_fusion.2.seq_ref, bf16[2,32,384,128]{3,2,1,0:T(8,128)(2,1)} %get-tuple-element.247.a_ref, f32[2,8,384,512]{3,2,1,0:T(8,128)} %shard_map.335.kh_ref, ...), custom_call_target="tpu_custom_call" | custom-call | flops 1920000000 | bytes 1258291 | tf_op jit(solution)/shard_map/pallas_call | solution.py:653
  252.0 6.0 %shard_map.344 = bf16[8,768,128]{2,1,0:T(8,128)(2,1)} custom-call(s32[1]{0:T(128)S(6)} %select_n.90.start_ref, bf16[768,768]{1,0:T(8,128)(2,1)} %get-tuple-element.212.w_ref, bf16[2,32,384,128]{3,2,1,0:T(8,128)(2,1)} %get-tuple-element.265.refs_0_.refs_12_), custom_call_target="tpu_custom_call" | custom-call | flops 60397976 | bytes 235929 | tf_op jit(solution)/shard_map/pallas_call | solution.py:723
  259.1 4.9 shard_map.345
  264.0 5.2 shard_map.346
  270.4 16.0 %shard_map.347.gm_ref = bf16[2,32,384,128]{3,2,1,0:T(8,128)(2,1)} custom-call(s32[4]{0:T(128)} %pad_add_fusion.3.at_ref, bf16[8,768,128]{2,1,0:T(8,128)(2,1)} %get-tuple-element.215.refs_0_.refs_4_, bf16[8,768,128]{2,1,0:T(8,128)(2,1)} %copy-done.3, bf16[8,768,128]{2,1,0:T(8,128)(2,1)} %copy-done.4, bf16[8,768,128]{2,1,0:T(8,128)(2,1)} %copy-done.5, ...), custom_call_target="tpu_custom_call" | custom-call | flops 241591904 | bytes 629145 | tf_op jit(solution)/shard_map/pallas_call | solution.py:338
  286.6 1.7 collective-permute-start.10
  288.3 5.2 shard_map.343.refs_0_
  293.5 28.8 %shard_map.348 = (bf16[1,32,384,128]{3,2,1,0:T(8,128)(2,1)}, bf16[1,32,384,128]{3,2,1,0:T(8,128)(2,1)}, f32[1,8,384,512]{3,2,1,0:T(8,128)}, f32[1,384,256]{2,1,0:T(8,128)}) custom-call(s32[2,17]{1,0:T(2,128)} %pad_add_fusion.1.tab_ref, s32[2,4]{1,0:T(2,128)} %pad_add_fusion.2.seq_ref, bf16[2,32,384,128]{3,2,1,0:T(8,128)(2,1)} %get-tuple-element.247.a_ref, ...), custom_call_target="tpu_custom_call" | custom-call | flops 1536000000 | bytes 1258291 | tf_op jit(solution)/shard_map/pallas_call | solution.py:680
  323.9 6.8 %shard_map.349 = bf16[1024,768]{1,0:T(8,128)(2,1)} custom-call(s32[1,1024]{1,0:T(1,128)} %bitcast.145, bf16[8,768,128]{2,1,0:T(8,128)(2,1)} %get-tuple-element.172.xd_ref, f32[8,1,128]{2,1,0:T(1,128)} %bitcast.148, f32[768,128]{1,0:T(8,128)} %broadcast_in_dim.105.bias_ref, f32[8,768,128]{2,1,0:T(8,128)} %shard_map.343.refs_0_, ...), custom_call_target="tpu_custom_call" | custom-call | flops 80530640 | bytes 235929 | tf_op jit(solution)/shard_map/pallas_call | solution.py:189
  331.7 28.7 %shard_map.350 = (bf16[1,32,384,128]{3,2,1,0:T(8,128)(2,1)}, bf16[1,32,384,128]{3,2,1,0:T(8,128)(2,1)}, f32[1,8,384,512]{3,2,1,0:T(8,128)}, f32[1,384,256]{2,1,0:T(8,128)}) custom-call(s32[2,17]{1,0:T(2,128)} %pad_add_fusion.1.tab_ref, s32[2,4]{1,0:T(2,128)} %pad_add_fusion.2.seq_ref, bf16[2,32,384,128]{3,2,1,0:T(8,128)(2,1)} %get-tuple-element.247.a_ref, ...), custom_call_target="tpu_custom_call" | custom-call | flops 1536000000 | bytes 1258291 | tf_op jit(solution)/shard_map/pallas_call | solution.py:680
  360.4 7.6 %collective-permute-done.11 = bf16[1024,768]{1,0:T(8,128)(2,1)S(1)} collective-permute-done((bf16[1024,768]{1,0:T(8,128)(2,1)}, bf16[1024,768]{1,0:T(8,128)(2,1)S(1)}, u32[]{:S(2)}, u32[]{:S(2)}) %collective-permute-start.11) | collective-permute-done | bytes 1572896 | tf_op jit(solution)/shard_map/ppermute | solution.py:1174
  368.0 7.1 %shard_map.351 = bf16[8,768,128]{2,1,0:T(8,128)(2,1)} custom-call(s32[1]{0:T(128)S(6)} %select_n.90.start_ref, bf16[768,1536]{1,0:T(8,128)(2,1)} %get-tuple-element.211.w_ref, bf16[1,32,384,128]{3,2,1,0:T(8,128)(2,1)} %get-tuple-element.259.refs_0_.refs_8_, bf16[1,32,384,128]{3,2,1,0:T(8,128)(2,1)} %get-tuple-element.260.refs_1_.refs_9_, ...), custom_call_target="tpu_custom_call" | custom-call | flops 120795952 | bytes 314572 | tf_op jit(solution)/shard_map/pallas_call | solution.py:723
  375.1 6.6 %shard_map.352 = bf16[8,768,128]{2,1,0:T(8,128)(2,1)} custom-call(s32[1]{0:T(128)S(6)} %select_n.101.start_ref, bf16[768,1536]{1,0:T(8,128)(2,1)} %get-tuple-element.211.w_ref, bf16[1,32,384,128]{3,2,1,0:T(8,128)(2,1)} %get-tuple-element.259.refs_0_.refs_8_, bf16[1,32,384,128]{3,2,1,0:T(8,128)(2,1)} %get-tuple-element.260.refs_1_.refs_9_, ...), custom_call_target="tpu_custom_call" | custom-call | flops 120795952 | bytes 314572 | tf_op jit(solution)/shard_map/pallas_call | solution.py:723
  381.8 7.1 %shard_map.353 = bf16[8,768,128]{2,1,0:T(8,128)(2,1)} custom-call(s32[1]{0:T(128)S(6)} %select_n.94.start_ref, bf16[768,1536]{1,0:T(8,128)(2,1)} %get-tuple-element.211.w_ref, bf16[1,32,384,128]{3,2,1,0:T(8,128)(2,1)} %get-tuple-element.259.refs_0_.refs_8_, bf16[1,32,384,128]{3,2,1,0:T(8,128)(2,1)} %get-tuple-element.260.refs_1_.refs_9_, ...), custom_call_target="tpu_custom_call" | custom-call | flops 120795952 | bytes 314572 | tf_op jit(solution)/shard_map/pallas_call | solution.py:723
  390.2 7.0 %all-to-all-start.1 = ((bf16[8,128,768]{2,1,0:T(8,128)(2,1)}), bf16[8,128,768]{2,1,0:T(8,128)(2,1)S(1)}, u32[]{:S(2)}, u32[]{:S(2)}) async-start(bf16[8,128,768]{2,1,0:T(8,128)(2,1)} %bitcast.123), calls=%async_computation.1 | async-start | bytes 3145728 | tf_op jit(solution)/shard_map/all_to_all | solution.py:1177
  397.9 6.9 %shard_map.354.refs_0_ = f32[8,768,128]{2,1,0:T(8,128)} custom-call(s32[1]{0:T(128)S(6)} %select_n.93.start_ref, bf16[768,1536]{1,0:T(8,128)(2,1)} %get-tuple-element.211.w_ref, bf16[1,32,384,128]{3,2,1,0:T(8,128)(2,1)} %get-tuple-element.259.refs_0_.refs_8_, bf16[1,32,384,128]{3,2,1,0:T(8,128)(2,1)} %get-tuple-element.260.refs_1_.refs_9_, ...), custom_call_target="tpu_custom_call" | custom-call | flops 120795952 | bytes 314572 | tf_op jit(solution)/shard_map/pallas_call | solution.py:723
  404.8 28.7 %shard_map.355 = (bf16[192,2304]{1,0:T(8,128)(2,1)}, bf16[192,2304]{1,0:T(8,128)(2,1)}, bf16[192,2304]{1,0:T(8,128)(2,1)}, bf16[192,2304]{1,0:T(8,128)(2,1)}) custom-call(s32[8]{0:T(128)} %concatenate.49.at_ref, bf16[8,768,128]{2,1,0:T(8,128)(2,1)} %get-tuple-element.177.x_ref.refs_0_, bf16[8,768,128]{2,1,0:T(8,128)(2,1)} %copy-done, ...), custom_call_target="tpu_custom_call" | custom-call | flops 724775744 | bytes 1572864 | tf_op jit(solution)/shard_map/pallas_call | solution.py:792
  433.5 10.7 %shard_map.356 = (bf16[1024,768]{1,0:T(8,128)(2,1)}, f32[2,768,128]{2,1,0:T(8,128)}) custom-call(s32[1,1024]{1,0:T(1,128)} %bitcast.146, bf16[8,768,128]{2,1,0:T(8,128)(2,1)} %get-tuple-element.172.xd_ref, bf16[8,768,128]{2,1,0:T(8,128)(2,1)} %get-tuple-element.210.gd_ref, f32[768,128]{1,0:T(8,128)} %broadcast_in_dim.97.gain_ref, ...), custom_call_target="tpu_custom_call" | custom-call | flops 80530640 | bytes 314572 | tf_op jit(solution)/shard_map/pallas_call | solution.py:225
  445.5 1.7 collective-permute-start.16
  451.0 6.7 %all-to-all-start.2 = ((f32[32,8,128]{2,1,0:T(8,128)}), f32[32,8,128]{2,1,0:T(8,128)S(1)}, u32[]{:S(2)}, u32[]{:S(2)}) async-start(f32[32,8,128]{2,1,0:T(8,128)} %pad.18.clone), calls=%async_computation.2 | async-start | bytes 262144 | tf_op jit(solution)/shard_map/all_to_all | solution.py:1272
  457.6 9.7 %shard_map.357 = (f32[1,192,128]{2,1,0:T(8,128)}, f32[1,192,128]{2,1,0:T(8,128)}, f32[1,384,128]{2,1,0:T(8,128)}) custom-call(f32[2,192,128]{2,1,0:T(8,128)} %bitcast.121, f32[1,8,384,512]{3,2,1,0:T(8,128)} %get-tuple-element.292.gh_ref, bf16[512,256]{1,0:T(8,128)(2,1)} %constant.220.back_ref), custom_call_target="tpu_custom_call" | custom-call | flops 768000000 | bytes 314572 | tf_op jit(solution)/shard_map/pallas_call | solution.py:450
  467.4 9.8 %shard_map.358 = (f32[1,192,128]{2,1,0:T(8,128)}, f32[1,192,128]{2,1,0:T(8,128)}, f32[1,384,128]{2,1,0:T(8,128)}) custom-call(f32[2,192,128]{2,1,0:T(8,128)} %bitcast.122, f32[1,8,384,512]{3,2,1,0:T(8,128)} %get-tuple-element.294.gh_ref, bf16[512,256]{1,0:T(8,128)(2,1)} %constant.220.back_ref), custom_call_target="tpu_custom_call" | custom-call | flops 768000000 | bytes 314572 | tf_op jit(solution)/shard_map/pallas_call | solution.py:450
  479.5 4.6 shard_map.359
  484.1 5.3 all-to-all-done.2
  490.4 3.9 all-to-all-start.3
  495.6 4.6 collective-permute-start.28
  502.3 6.9 %collective-permute-start.24 = (f32[99,128]{1,0:T(8,128)S(1)}, f32[99,128]{1,0:T(8,128)S(1)}, u32[]{:S(2)}, u32[]{:S(2)}) collective-permute-start(f32[99,128]{1,0:T(8,128)S(1)} %get-tuple-element.425), channel_id=1, source_target_pairs={{0,19},{1,27},{2,18},{3,26},{4,3},{5,11},{6,2},{7,10},{8,17},{9,25... | collective-permute-start | bytes 152072 | tf_op jit(solution)/shard_map/ppermute | solution.py:1260
  509.2 2.4 add_convert_fusion
  512.5 2.0 collective-permute-start.23
  514.5 2.5 collective-permute-done.27
  522.1 2.9 collective-permute-start.19
  528.7 15.8 %collective-permute-done.19 = bf16[96,2304]{1,0:T(8,128)(2,1)S(1)} collective-permute-done((bf16[96,2304]{1,0:T(8,128)(2,1)S(1)}, bf16[96,2304]{1,0:T(8,128)(2,1)S(1)}, u32[]{:S(2)}, u32[]{:S(2)}) %collective-permute-start.19) | collective-permute-done | bytes 442400 | tf_op jit(solution)/shard_map/ppermute | solution.py:1174
  548.2 4.6 shard_map.360
  (197 shorter events, 59.8 us)
Async XLA Ops:
  2.6 87.2 %collective-permute-start = (s32[1027]{0:T(1024)S(1)}, s32[1027]{0:T(1024)S(1)}, u32[]{:S(2)}, u32[]{:S(2)}) collective-permute-start(s32[1027]{0:T(1024)S(1)} %pad_add_fusion), channel_id=1, source_target_pairs={{0,4},{2,0},{4,6},{6,2},{1,5},{3,1},{5,7},{7,3},{8,12},{10,8},{12,... | collective-permute-start | bytes 12332 | tf_op jit(solution)/shard_map/ppermute | solution.py:1171
  91.7 13.3 %copy-start.25 = (s32[1024]{0:T(1024)}, s32[1024]{0:T(1024)S(1)}, u32[]{:S(2)}) copy-start(s32[1024]{0:T(1024)S(1)} %slice.142) | copy-start | bytes 12292
  105.9 40.8 %collective-permute-start.1 = (bf16[8,768,128]{2,1,0:T(8,128)(2,1)}, bf16[8,768,128]{2,1,0:T(8,128)(2,1)S(1)}, u32[]{:S(2)}, u32[]{:S(2)}) collective-permute-start(bf16[8,768,128]{2,1,0:T(8,128)(2,1)} %get-tuple-element.177.x_ref.refs_0_), channel_id=1, source_target_pairs={{0,4},{4,0},{1,5},{5,1},{2,6},{6,2},{3,7},{7,3},{8,12},{12,8},{9,1... | collective-permute-start | bytes 4718600 | tf_op jit(solution)/shard_map/ppermute | solution.py:1165
  110.5 54.4 %collective-permute-start.2 = (bf16[8,768,128]{2,1,0:T(8,128)(2,1)}, bf16[8,768,128]{2,1,0:T(8,128)(2,1)S(1)}, u32[]{:S(2)}, u32[]{:S(2)}) collective-permute-start(bf16[8,768,128]{2,1,0:T(8,128)(2,1)} %get-tuple-element.177.x_ref.refs_0_), channel_id=1, source_target_pairs={{0,1},{1,0},{2,3},{3,2},{4,5},{5,4},{6,7},{7,6},{8,9},{9,8},{10,11... | collective-permute-start | bytes 4718600 | tf_op jit(solution)/shard_map/ppermute | solution.py:1165
  114.9 31.8 %all-to-all-start = ((bf16[8,128,768]{2,1,0:T(8,128)(2,1)}), bf16[8,128,768]{2,1,0:T(8,128)(2,1)}, u32[]{:S(2)}, u32[]{:S(2)}) async-start(bf16[8,128,768]{2,1,0:T(8,128)(2,1)} %bitcast.119), calls=%async_computation | async-start | bytes 3145728 | tf_op jit(solution)/shard_map/all_to_all | solution.py:1177
  146.7 9.8 %copy-start = (bf16[8,768,128]{2,1,0:T(8,128)(2,1)}, bf16[8,768,128]{2,1,0:T(8,128)(2,1)S(1)}, u32[]{:S(2)}) copy-start(bf16[8,768,128]{2,1,0:T(8,128)(2,1)S(1)} %collective-permute-done.1.x_ref.refs_1_) | copy-start | bytes 4718596
  165.0 10.7 %collective-permute-start.3 = (bf16[8,768,128]{2,1,0:T(8,128)(2,1)S(1)}, bf16[8,768,128]{2,1,0:T(8,128)(2,1)S(1)}, u32[]{:S(2)}, u32[]{:S(2)}) collective-permute-start(bf16[8,768,128]{2,1,0:T(8,128)(2,1)S(1)} %collective-permute-done.2.x_ref.refs_2_), channel_id=1, source_target_pairs={{0,4},{4,0},{1,5},{5,1},{2,6},{6,2},{3,7},{7,3},{8,12},{12,8},{9,1... | collective-permute-start | bytes 4718600 | tf_op jit(solution)/shard_map/ppermute | solution.py:1165
  165.0 20.2 %collective-permute-start.4 = (bf16[1024,768]{1,0:T(8,128)(2,1)}, bf16[1024,768]{1,0:T(8,128)(2,1)}, u32[]{:S(2)}, u32[]{:S(2)}) collective-permute-start(bf16[1024,768]{1,0:T(8,128)(2,1)} %bitcast.22), channel_id=1, source_target_pairs={{0,4},{2,0},{4,6},{6,2},{1,5},{3,1},{5,7},{7,3},{8,12},{10,8},{12,... | collective-permute-start | bytes 4718600 | tf_op jit(solution)/shard_map/ppermute | solution.py:1171
  193.4 58.6 %collective-permute-start.5 = (bf16[8,768,128]{2,1,0:T(8,128)(2,1)}, bf16[8,768,128]{2,1,0:T(8,128)(2,1)S(1)}, u32[]{:S(2)}, u32[]{:S(2)}) collective-permute-start(bf16[8,768,128]{2,1,0:T(8,128)(2,1)} %get-tuple-element.215.refs_0_.refs_4_), channel_id=1, source_target_pairs={{0,4},{4,0},{1,5},{5,1},{2,6},{6,2},{3,7},{7,3},{8,12},{12,8},{9,1... | collective-permute-start | bytes 4718600 | tf_op jit(solution)/shard_map/ppermute | solution.py:1165
  212.7 39.2 %collective-permute-start.6 = (bf16[8,768,128]{2,1,0:T(8,128)(2,1)}, bf16[8,768,128]{2,1,0:T(8,128)(2,1)S(1)}, u32[]{:S(2)}, u32[]{:S(2)}) collective-permute-start(bf16[8,768,128]{2,1,0:T(8,128)(2,1)} %get-tuple-element.215.refs_0_.refs_4_), channel_id=1, source_target_pairs={{0,1},{1,0},{2,3},{3,2},{4,5},{5,4},{6,7},{7,6},{8,9},{9,8},{10,11... | collective-permute-start | bytes 4718600 | tf_op jit(solution)/shard_map/ppermute | solution.py:1165
  252.0 6.1 %copy-start.4 = (bf16[8,768,128]{2,1,0:T(8,128)(2,1)}, bf16[8,768,128]{2,1,0:T(8,128)(2,1)S(1)}, u32[]{:S(2)}) copy-start(bf16[8,768,128]{2,1,0:T(8,128)(2,1)S(1)} %collective-permute-done.6.refs_2_.refs_6_) | copy-start | bytes 4718596
  258.0 6.0 %collective-permute-start.7 = (bf16[8,768,128]{2,1,0:T(8,128)(2,1)}, bf16[8,768,128]{2,1,0:T(8,128)(2,1)}, u32[]{:S(2)}, u32[]{:S(2)}) collective-permute-start(bf16[8,768,128]{2,1,0:T(8,128)(2,1)} %shard_map.344), channel_id=1, source_target_pairs={{0,4},{4,0},{1,5},{5,1},{2,6},{6,2},{3,7},{7,3},{8,12},{12,8},{9,1... | collective-permute-start | bytes 4718600 | tf_op jit(solution)/shard_map/ppermute | solution.py:1165
  258.1 11.1 %collective-permute-start.8 = (bf16[8,768,128]{2,1,0:T(8,128)(2,1)S(1)}, bf16[8,768,128]{2,1,0:T(8,128)(2,1)S(1)}, u32[]{:S(2)}, u32[]{:S(2)}) collective-permute-start(bf16[8,768,128]{2,1,0:T(8,128)(2,1)S(1)} %collective-permute-done.6.refs_2_.refs_6_), channel_id=1, source_target_pairs={{0,4},{4,0},{1,5},{5,1},{2,6},{6,2},{3,7},{7,3},{8,12},{12,8},{9,1... | collective-permute-start | bytes 4718600 | tf_op jit(solution)/shard_map/ppermute | solution.py:1165
  270.4 16.0 %copy-start.9 = (bf16[8,768,128]{2,1,0:T(8,128)(2,1)S(1)}, bf16[8,768,128]{2,1,0:T(8,128)(2,1)}, u32[]{:S(2)}) copy-start(bf16[8,768,128]{2,1,0:T(8,128)(2,1)} %shard_map.345) | copy-start | bytes 4718596
  286.5 35.8 %collective-permute-start.9 = (bf16[8,768,128]{2,1,0:T(8,128)(2,1)S(1)}, bf16[8,768,128]{2,1,0:T(8,128)(2,1)S(1)}, u32[]{:S(2)}, u32[]{:S(2)}) collective-permute-start(bf16[8,768,128]{2,1,0:T(8,128)(2,1)S(1)} %copy-done.9), channel_id=1, source_target_pairs={{0,4},{4,0},{1,5},{5,1},{2,6},{6,2},{3,7},{7,3},{8,12},{12,8},{9,1... | collective-permute-start | bytes 4718600 | tf_op jit(solution)/shard_map/ppermute | solution.py:1165
  286.6 36.4 %collective-permute-start.10 = (bf16[8,768,128]{2,1,0:T(8,128)(2,1)}, bf16[8,768,128]{2,1,0:T(8,128)(2,1)}, u32[]{:S(2)}, u32[]{:S(2)}) collective-permute-start(bf16[8,768,128]{2,1,0:T(8,128)(2,1)} %shard_map.346), channel_id=1, source_target_pairs={{0,1},{1,0},{2,3},{3,2},{4,5},{5,4},{6,7},{7,6},{8,9},{9,8},{10,11... | collective-permute-start | bytes 4718600 | tf_op jit(solution)/shard_map/ppermute | solution.py:1165
  330.8 37.2 %collective-permute-start.11 = (bf16[1024,768]{1,0:T(8,128)(2,1)}, bf16[1024,768]{1,0:T(8,128)(2,1)S(1)}, u32[]{:S(2)}, u32[]{:S(2)}) collective-permute-start(bf16[1024,768]{1,0:T(8,128)(2,1)} %shard_map.349), channel_id=1, source_target_pairs={{4,0},{0,2},{6,4},{2,6},{5,1},{1,3},{7,5},{3,7},{12,8},{8,10},{14,... | collective-permute-start | bytes 4718600 | tf_op jit(solution)/shard_map/ppermute | solution.py:1174
  368.0 7.1 %copy-start.10 = (bf16[1024,768]{1,0:T(8,128)(2,1)}, bf16[1024,768]{1,0:T(8,128)(2,1)S(1)}, u32[]{:S(2)}) copy-start(bf16[1024,768]{1,0:T(8,128)(2,1)S(1)} %collective-permute-done.11) | copy-start | bytes 4718596
  375.1 6.7 %collective-permute-start.12 = (bf16[8,768,128]{2,1,0:T(8,128)(2,1)}, bf16[8,768,128]{2,1,0:T(8,128)(2,1)}, u32[]{:S(2)}, u32[]{:S(2)}) collective-permute-start(bf16[8,768,128]{2,1,0:T(8,128)(2,1)} %shard_map.351), channel_id=1, source_target_pairs={{0,4},{4,0},{1,5},{5,1},{2,6},{6,2},{3,7},{7,3},{8,12},{12,8},{9,1... | collective-permute-start | bytes 4718600 | tf_op jit(solution)/shard_map/ppermute | solution.py:1165
  381.8 7.1 %copy-start.8 = (bf16[8,768,128]{2,1,0:T(8,128)(2,1)S(1)}, bf16[8,768,128]{2,1,0:T(8,128)(2,1)}, u32[]{:S(2)}) copy-start(bf16[8,768,128]{2,1,0:T(8,128)(2,1)} %shard_map.352) | copy-start | bytes 4718596
  388.9 44.7 %collective-permute-start.13 = (bf16[8,768,128]{2,1,0:T(8,128)(2,1)S(1)}, bf16[8,768,128]{2,1,0:T(8,128)(2,1)}, u32[]{:S(2)}, u32[]{:S(2)}) collective-permute-start(bf16[8,768,128]{2,1,0:T(8,128)(2,1)S(1)} %copy-done.8), channel_id=1, source_target_pairs={{0,4},{4,0},{1,5},{5,1},{2,6},{6,2},{3,7},{7,3},{8,12},{12,8},{9,1... | collective-permute-start | bytes 4718600 | tf_op jit(solution)/shard_map/ppermute | solution.py:1165
  389.3 44.2 %collective-permute-start.14 = (bf16[8,768,128]{2,1,0:T(8,128)(2,1)}, bf16[8,768,128]{2,1,0:T(8,128)(2,1)}, u32[]{:S(2)}, u32[]{:S(2)}) collective-permute-start(bf16[8,768,128]{2,1,0:T(8,128)(2,1)} %shard_map.353), channel_id=1, source_target_pairs={{0,1},{1,0},{2,3},{3,2},{4,5},{5,4},{6,7},{7,6},{8,9},{9,8},{10,11... | collective-permute-start | bytes 4718600 | tf_op jit(solution)/shard_map/ppermute | solution.py:1165
  390.2 43.3 %all-to-all-start.1 = ((bf16[8,128,768]{2,1,0:T(8,128)(2,1)}), bf16[8,128,768]{2,1,0:T(8,128)(2,1)S(1)}, u32[]{:S(2)}, u32[]{:S(2)}) async-start(bf16[8,128,768]{2,1,0:T(8,128)(2,1)} %bitcast.123), calls=%async_computation.1 | async-start | bytes 3145728 | tf_op jit(solution)/shard_map/all_to_all | solution.py:1177
  433.5 10.7 %copy-start.7 = (bf16[8,128,768]{2,1,0:T(8,128)(2,1)}, bf16[8,128,768]{2,1,0:T(8,128)(2,1)S(1)}, u32[]{:S(2)}) copy-start(bf16[8,128,768]{2,1,0:T(8,128)(2,1)S(1)} %all-to-all-done.1) | copy-start | bytes 4718596
  433.5 10.9 %copy-start.24 = (s32[1024]{0:T(1024)S(1)}, s32[1024]{0:T(1024)}, u32[]{:S(2)}) copy-start(s32[1024]{0:T(1024)} %convert_reduce_fusion.1) | copy-start | bytes 12292
  433.5 15.1 %copy-start.15 = (f32[768,128]{1,0:T(8,128)S(1)}, f32[768,128]{1,0:T(8,128)}, u32[]{:S(2)}) copy-start(f32[768,128]{1,0:T(8,128)} %get-tuple-element.303) | copy-start | bytes 1179652
  444.2 45.3 %collective-permute-start.15 = (bf16[1024,768]{1,0:T(8,128)(2,1)}, bf16[1024,768]{1,0:T(8,128)(2,1)}, u32[]{:S(2)}, u32[]{:S(2)}) collective-permute-start(bf16[1024,768]{1,0:T(8,128)(2,1)} %get-tuple-element.287), channel_id=1, source_target_pairs={{4,0},{0,2},{6,4},{2,6},{5,1},{1,3},{7,5},{3,7},{12,8},{8,10},{14,... | collective-permute-start | bytes 4718600 | tf_op jit(solution)/shard_map/ppermute | solution.py:1174
  445.5 44.0 %collective-permute-start.16 = (bf16[192,2304]{1,0:T(8,128)(2,1)}, bf16[192,2304]{1,0:T(8,128)(2,1)S(1)}, u32[]{:S(2)}, u32[]{:S(2)}) collective-permute-start(bf16[192,2304]{1,0:T(8,128)(2,1)} %get-tuple-element.289), channel_id=1, source_target_pairs={{0,8},{8,0},{16,24},{24,16},{1,9},{9,1},{17,25},{25,17},{2,10},{10... | collective-permute-start | bytes 2654216 | tf_op jit(solution)/shard_map/ppermute | solution.py:1165
  447.2 42.3 %collective-permute-start.17 = (bf16[192,2304]{1,0:T(8,128)(2,1)}, bf16[192,2304]{1,0:T(8,128)(2,1)}, u32[]{:S(2)}, u32[]{:S(2)}) collective-permute-start(bf16[192,2304]{1,0:T(8,128)(2,1)} %get-tuple-element.290), channel_id=1, source_target_pairs={{0,16},{8,24},{16,0},{24,8},{1,17},{9,25},{17,1},{25,9},{2,18},{10... | collective-permute-start | bytes 2654216 | tf_op jit(solution)/shard_map/ppermute | solution.py:1165
  448.4 41.1 %collective-permute-start.18 = (bf16[192,2304]{1,0:T(8,128)(2,1)}, bf16[192,2304]{1,0:T(8,128)(2,1)}, u32[]{:S(2)}, u32[]{:S(2)}) collective-permute-start(bf16[192,2304]{1,0:T(8,128)(2,1)} %get-tuple-element.291), channel_id=1, source_target_pairs={{0,24},{8,16},{16,8},{24,0},{1,25},{9,17},{17,9},{25,1},{2,26},{10... | collective-permute-start | bytes 2654216 | tf_op jit(solution)/shard_map/ppermute | solution.py:1165
  451.0 38.5 %all-to-all-start.2 = ((f32[32,8,128]{2,1,0:T(8,128)}), f32[32,8,128]{2,1,0:T(8,128)S(1)}, u32[]{:S(2)}, u32[]{:S(2)}) async-start(f32[32,8,128]{2,1,0:T(8,128)} %pad.18.clone), calls=%async_computation.2 | async-start | bytes 262144 | tf_op jit(solution)/shard_map/all_to_all | solution.py:1272
  467.4 9.8 %copy-start.13 = (f32[1,384,256]{2,1,0:T(8,128)S(1)}, f32[1,384,256]{2,1,0:T(8,128)}, u32[]{:S(2)}) copy-start(f32[1,384,256]{2,1,0:T(8,128)} %get-tuple-element.300) | copy-start | bytes 1179652
  467.4 9.9 %copy-start.14 = (f32[1,384,256]{2,1,0:T(8,128)S(1)}, f32[1,384,256]{2,1,0:T(8,128)}, u32[]{:S(2)}) copy-start(f32[1,384,256]{2,1,0:T(8,128)} %get-tuple-element.301) | copy-start | bytes 1179652
  467.4 9.9 %copy-start.16 = (f32[1,384,128]{2,1,0:T(8,128)S(1)}, f32[1,384,128]{2,1,0:T(8,128)}, u32[]{:S(2)}) copy-start(f32[1,384,128]{2,1,0:T(8,128)} %get-tuple-element.298) | copy-start | bytes 589828
  490.4 56.6 %all-to-all-start.3 = ((bf16[8,128,768]{2,1,0:T(8,128)(2,1)}), bf16[8,128,768]{2,1,0:T(8,128)(2,1)S(1)}, u32[]{:S(2)}, u32[]{:S(2)}) async-start(bf16[8,128,768]{2,1,0:T(8,128)(2,1)} %bitcast.50), calls=%async_computation.3 | async-start | bytes 3145728 | tf_op jit(solution)/shard_map/all_to_all | solution.py:1177
  495.6 16.9 %collective-permute-start.28 = (f32[99,128]{1,0:T(8,128)S(1)}, f32[99,128]{1,0:T(8,128)S(1)}, u32[]{:S(2)}, u32[]{:S(2)}) collective-permute-start(f32[99,128]{1,0:T(8,128)S(1)} %get-tuple-element.421), channel_id=1, source_target_pairs={{0,23},{1,31},{2,22},{3,30},{4,7},{5,15},{6,6},{7,14},{8,21},{9,29... | collective-permute-start | bytes 152072 | tf_op jit(solution)/shard_map/ppermute | solution.py:1260
  500.2 16.8 %collective-permute-start.27 = (f32[99,128]{1,0:T(8,128)S(1)}, f32[99,128]{1,0:T(8,128)S(1)}, u32[]{:S(2)}, u32[]{:S(2)}) collective-permute-start(f32[99,128]{1,0:T(8,128)S(1)} %get-tuple-element.422), channel_id=1, source_target_pairs={{0,22},{1,30},{2,23},{3,31},{4,6},{5,14},{6,7},{7,15},{8,20},{9,28... | collective-permute-start | bytes 152072 | tf_op jit(solution)/shard_map/ppermute | solution.py:1260
  500.2 18.1 %collective-permute-start.26 = (f32[99,128]{1,0:T(8,128)S(1)}, f32[99,128]{1,0:T(8,128)S(1)}, u32[]{:S(2)}, u32[]{:S(2)}) collective-permute-start(f32[99,128]{1,0:T(8,128)S(1)} %get-tuple-element.423), channel_id=1, source_target_pairs={{0,21},{1,29},{2,20},{3,28},{4,5},{5,13},{6,4},{7,12},{8,23},{9,31... | collective-permute-start | bytes 152072 | tf_op jit(solution)/shard_map/ppermute | solution.py:1260
  501.7 18.7 %collective-permute-start.25 = (f32[99,128]{1,0:T(8,128)S(1)}, f32[99,128]{1,0:T(8,128)S(1)}, u32[]{:S(2)}, u32[]{:S(2)}) collective-permute-start(f32[99,128]{1,0:T(8,128)S(1)} %get-tuple-element.424), channel_id=1, source_target_pairs={{0,20},{1,28},{2,21},{3,29},{4,4},{5,12},{6,5},{7,13},{8,22},{9,30... | collective-permute-start | bytes 152072 | tf_op jit(solution)/shard_map/ppermute | solution.py:1260
  502.3 19.7 %collective-permute-start.24 = (f32[99,128]{1,0:T(8,128)S(1)}, f32[99,128]{1,0:T(8,128)S(1)}, u32[]{:S(2)}, u32[]{:S(2)}) collective-permute-start(f32[99,128]{1,0:T(8,128)S(1)} %get-tuple-element.425), channel_id=1, source_target_pairs={{0,19},{1,27},{2,18},{3,26},{4,3},{5,11},{6,2},{7,10},{8,17},{9,25... | collective-permute-start | bytes 152072 | tf_op jit(solution)/shard_map/ppermute | solution.py:1260
  511.6 13.6 %copy-start.17 = (f32[2,48,64]{2,1,0:T(8,128)S(1)}, f32[2,48,64]{2,1,0:T(8,128)}, u32[]{:S(2)}) copy-start(f32[2,48,64]{2,1,0:T(8,128)} %param.37) | copy-start | bytes 73732
  511.6 13.6 %copy-start.18 = (f32[2,48,64]{2,1,0:T(8,128)S(1)}, f32[2,48,64]{2,1,0:T(8,128)}, u32[]{:S(2)}) copy-start(f32[2,48,64]{2,1,0:T(8,128)} %param.39) | copy-start | bytes 73732
  511.7 13.6 %copy-start.19 = (f32[2,48,64]{2,1,0:T(8,128)S(1)}, f32[2,48,64]{2,1,0:T(8,128)}, u32[]{:S(2)}) copy-start(f32[2,48,64]{2,1,0:T(8,128)} %param.38) | copy-start | bytes 73732
  512.5 12.5 %collective-permute-start.23 = (f32[99,128]{1,0:T(8,128)S(1)}, f32[99,128]{1,0:T(8,128)S(1)}, u32[]{:S(2)}, u32[]{:S(2)}) collective-permute-start(f32[99,128]{1,0:T(8,128)S(1)} %get-tuple-element.426), channel_id=1, source_target_pairs={{0,18},{1,26},{2,19},{3,27},{4,2},{5,10},{6,3},{7,11},{8,16},{9,24... | collective-permute-start | bytes 152072 | tf_op jit(solution)/shard_map/ppermute | solution.py:1260
  517.0 8.0 %collective-permute-start.21 = (f32[99,128]{1,0:T(8,128)S(1)}, f32[99,128]{1,0:T(8,128)S(1)}, u32[]{:S(2)}, u32[]{:S(2)}) collective-permute-start(f32[99,128]{1,0:T(8,128)S(1)} %get-tuple-element.427), channel_id=1, source_target_pairs={{0,16},{1,24},{2,17},{3,25},{4,0},{5,8},{6,1},{7,9},{8,18},{9,26},... | collective-permute-start | bytes 152072 | tf_op jit(solution)/shard_map/ppermute | solution.py:1260
  518.3 6.7 %collective-permute-start.22 = (f32[99,128]{1,0:T(8,128)S(1)}, f32[99,128]{1,0:T(8,128)S(1)}, u32[]{:S(2)}, u32[]{:S(2)}) collective-permute-start(f32[99,128]{1,0:T(8,128)S(1)} %get-tuple-element.420), channel_id=1, source_target_pairs={{0,17},{1,25},{2,16},{3,24},{4,1},{5,9},{6,0},{7,8},{8,19},{9,27},... | collective-permute-start | bytes 152072 | tf_op jit(solution)/shard_map/ppermute | solution.py:1260
  520.4 8.3 %collective-permute-start.20 = (bf16[96,2304]{1,0:T(8,128)(2,1)}, bf16[96,2304]{1,0:T(8,128)(2,1)S(1)}, u32[]{:S(2)}, u32[]{:S(2)}) collective-permute-start(bf16[96,2304]{1,0:T(8,128)(2,1)} %get-tuple-element.419), channel_id=1, source_target_pairs={{0,6},{2,2},{4,4},{6,0},{1,7},{3,3},{5,5},{7,1},{8,14},{10,10},{12... | collective-permute-start | bytes 1327112 | tf_op jit(solution)/shard_map/ppermute | solution.py:1244
  522.1 22.4 %collective-permute-start.19 = (bf16[96,2304]{1,0:T(8,128)(2,1)S(1)}, bf16[96,2304]{1,0:T(8,128)(2,1)S(1)}, u32[]{:S(2)}, u32[]{:S(2)}) collective-permute-start(bf16[96,2304]{1,0:T(8,128)(2,1)S(1)} %get-tuple-element.418), channel_id=1, source_target_pairs={{4,0},{0,2},{6,4},{2,6},{5,1},{1,3},{7,5},{3,7},{12,8},{8,10},{14,... | collective-permute-start | bytes 1327112 | tf_op jit(solution)/shard_map/ppermute | solution.py:1174
  (11 other events, 20.2 us)
where the time goes:
time: 563 us; the launch traced here: 553 us
  Pallas kernels  386 us (69%)
  starting transfers between devices  81.6 us (14%)
  waiting for transfers between devices  32.1 us (6%)
  local copies, waits for them, and re-layouts  27.8 us (5%)
  other arithmetic  23.5 us (4%)
    pallas_call x1, Pallas kernels, meet(): pl.pallas_call(partial(meet_body, axes), in_specs=[vmem] * 5, out_specs=[...  73.1 us
    pallas_call x2, Pallas kernels, ssm_back(): pl.pallas_call(partial(back_body, nb, nseq, cc, 64, k == 1), grid=(ch //...  57.4 us
    pallas_call x8, Pallas kernels, mul_rows(): pl.pallas_call(partial(mul_body, count, extra is not None), grid_spec=plt...  49.1 us
    pallas_call x1, Pallas kernels, ssm_scan(): pl.pallas_call(partial(scan_body, nb, nseq, cc, 32), grid=(2, ch // cc),...  36.5 us
    pallas_call x4, Pallas kernels, chained(): pl.pallas_call(body, grid_spec=pltpu.PrefetchScalarGridSpec(num_scalar_pr...  33.7 us
    ppermute x15, starting transfers between devices, flip(): return lax.ppermute(x, axis, [(i, i ^ bit) for i in range(self.axes[axis])])  30.9 us
    pallas_call x1, Pallas kernels, outer_sums(): pl.pallas_call(partial(outer_body, ch, many, cuts, parts), grid_spec=pltp...  28.7 us
    ppermute x3, waiting for transfers between devices, ungroup(): return lax.ppermute(x, ('c', 'h'), self.back)  23.4 us
  transfers between devices with their start and end apart: 33, of which 5 were waited for; matrix products, arithmetic and copies ran while one was open for 7% of the time, Pallas kernels for 56%

commit v1 on v0

--- a/solution.py
+++ b/solution.py
@@ -832,9 +832,10 @@
 
 
 def meet_body(
-    axes, rank_ref, x_ref, chan_ref, norm_ref, pack_ref, got_ref, call_ref, nall_ref, wall_ref, send_s, *sems
+    axes, rank_ref, x_ref, g_ref, chan_ref, norm_ref, pack_ref, got_ref, gotg_ref, call_ref, nall_ref, wall_ref,
+    send_s, sendg_s, *sems
 ):
-    xs_sem, xr_sem, cs_sem, cr_sem, ns_sem, nr_sem, ws_sem, wr_sem, own_sem = sems
+    xs_sem, xr_sem, gs_sem, gr_sem, cs_sem, cr_sem, ns_sem, nr_sem, ws_sem, wr_sem, own_sem = sems
     q, c, h, w = (lax.axis_index(name) for name in axes)
     rows = x_ref.shape[0]
     piece = rows // 8
@@ -895,19 +896,37 @@
     pieces = [(kq, kh) for kh in (0, 1) for kq in (1, 2, 3, 0)]
     spot = lax.broadcasted_iota(jnp.int32, (piece, rows), 0)
 
-    def row_copy(kq, kh):
+    x_side = (send_s, got_ref, xs_sem, xr_sem, 0)
+    g_side = (sendg_s, gotg_ref, gs_sem, gr_sem, 3)
+
+    def row_copy(side, kq, kh):
+        held, got, send, recv, _ = side
         at = 2 * kq + kh
-        return remote(
-            send_s.at[at], got_ref.at[2 * q + c], xs_sem.at[at], xr_sem.at[2 * kq + c], (q ^ kq, 1 - h, h ^ kh, w)
-        )
-
-    def own_copy():
-        return pltpu.make_async_copy(send_s.at[0], got_ref.at[2 * q + c], own_sem.at[0])
+        return remote(held.at[at], got.at[2 * q + c], send.at[at], recv.at[2 * kq + c], (q ^ kq, 1 - h, h ^ kh, w))
+
+    def own_copy(side):
+        held, got, _, _, at = side
+        return pltpu.make_async_copy(held.at[0], got.at[2 * q + c], own_sem.at[at])
+
+    def send_rows(side, kq, kh):
+        if (kq, kh) == (0, 0):
+
+            @pl.when(c != h)
+            def _():
+                own_copy(side).start()
+
+            @pl.when(c == h)
+            def _():
+                row_copy(side, 0, 0).start()
+
+        else:
+            row_copy(side, kq, kh).start()
 
     for kq, kh in pieces:
         chunk = 2 * (q ^ kq) + (h ^ kh)
         pick = jnp.where(spot + chunk * piece == rank_ref[...], 1.0, 0.0).astype(bf16)
         send_s[2 * kq + kh] = nn(pick, x_ref[...]).astype(bf16)
+        sendg_s[2 * kq + kh] = nn(pick, g_ref[...]).astype(bf16)
         if (kq, kh) == (1, 1):
             for at in range(2):
 
@@ -921,18 +940,7 @@
 
                 for bits in range(1, 4):
                     pass_on(at, bits).start()
-        if (kq, kh) == (0, 0):
-
-            @pl.when(c != h)
-            def _():
-                own_copy().start()
-
-            @pl.when(c == h)
-            def _():
-                row_copy(0, 0).start()
-
-        else:
-            row_copy(kq, kh).start()
+        send_rows(x_side, kq, kh)
 
     place = 2 * (1 - c) + w
     spot_c = 4 * c + 2 * h + w
@@ -967,18 +975,11 @@
             def _():
                 chan_copy(0).start()
 
+    for kq, kh in pieces[4:] + pieces[:4]:
+        send_rows(g_side, kq, kh)
+
     for bits in range(1, 32):
         norm_copy(bits).wait()
-    for at in range(8):
-
-        @pl.when((c != h) & (at == c))
-        def _():
-            own_copy().wait()
-
-        @pl.when(jnp.logical_not((c != h) & (at == c)))
-        def _(at=at):
-            remote(send_s.at[at], got_ref.at[at], xs_sem.at[at], xr_sem.at[at], peer(1)).wait_recv()
-
     chan_came(far_spot).wait_recv()
     for bits in range(1, 4):
         chan_pass(bits).start()
@@ -1003,15 +1004,27 @@
     def _():
         second_copy().wait_send()
 
-    for kq, kh in pieces:
-        if (kq, kh) == (0, 0):
-
-            @pl.when(c == h)
-            def _():
-                row_copy(0, 0).wait_send()
-
-        else:
-            row_copy(kq, kh).wait_send()
+    for side in (x_side, g_side):
+        held, got, send, recv, _ = side
+        for at in range(8):
+
+            @pl.when((c != h) & (at == c))
+            def _(side=side):
+                own_copy(side).wait()
+
+            @pl.when(jnp.logical_not((c != h) & (at == c)))
+            def _(at=at, held=held, got=got, send=send, recv=recv):
+                remote(held.at[at], got.at[at], send.at[at], recv.at[at], peer(1)).wait_recv()
+
+        for kq, kh in pieces:
+            if (kq, kh) == (0, 0):
+
+                @pl.when(c == h)
+                def _(side=side):
+                    row_copy(side, 0, 0).wait_send()
+
+            else:
+                row_copy(side, kq, kh).wait_send()
     for at in range(1, 5):
         chan_copy(at).wait_send()
 
@@ -1020,25 +1033,26 @@
         chan_copy(0).wait_send()
 
 
-def meet(axes, rank, x, chan, norm, pack):
+def meet(axes, rank, x, g, chan, norm, pack):
     rows, width = x.shape
     vmem = pl.BlockSpec(memory_space=pltpu.VMEM)
     sem = pltpu.SemaphoreType.DMA
     return pl.pallas_call(
         partial(meet_body, axes),
-        in_specs=[vmem] * 5,
-        out_specs=[vmem] * 4,
+        in_specs=[vmem] * 6,
+        out_specs=[vmem] * 5,
         out_shape=[
+            jax.ShapeDtypeStruct((8, rows // 8, width), bf16),
             jax.ShapeDtypeStruct((8, rows // 8, width), bf16),
             jax.ShapeDtypeStruct((8,) + chan.shape, f32),
             jax.ShapeDtypeStruct((32,) + norm.shape, f32),
             jax.ShapeDtypeStruct((8 * pack.shape[0], pack.shape[1]), bf16),
         ],
-        scratch_shapes=[pltpu.VMEM((8, rows // 8, width), bf16)]
-        + [sem((8,)), sem((8,)), sem((8,)), sem((8,)), sem((32,)), sem((32,)), sem((8,)), sem((8,)), sem((3,))],
+        scratch_shapes=[pltpu.VMEM((8, rows // 8, width), bf16)] * 2
+        + [sem((8,)), sem((8,)), sem((8,)), sem((8,)), sem((8,)), sem((8,)), sem((32,)), sem((32,)), sem((8,)), sem((8,)), sem((4,))],
         compiler_params=pltpu.CompilerParams(collective_id=1, has_side_effects=True, vmem_limit_bytes=60 * MIB),
         cost_estimate=cost(2 * rows * rows * width, 100 * rows * width),
-    )(rank.reshape(1, rows), x, chan, norm, pack)
+    )(rank.reshape(1, rows), x, g, chan, norm, pack)
 
 
 def sequence_tables(lens, nb):
@@ -1120,9 +1134,9 @@
     def order(self, pieces):
         return jnp.append(jnp.arange(pieces * self.n_t, dtype=jnp.int32), 0)
 
-    def enter(self, rank, x, chan, norm, pack):
-        (sent,) = permute_to(rank, [x])
-        return (self.spread(sent),) + self.gather_channels(chan, norm) + (lax.all_gather(pack, "dp", axis=0, tiled=True),)
+    def enter(self, rank, x, g, chan, norm, pack):
+        sent_x, sent_g = permute_to(rank, [x, g])
+        return (self.spread(sent_x), self.spread(sent_g)) + self.gather_channels(chan, norm) + (lax.all_gather(pack, "dp", axis=0, tiled=True),)
 
     def gather_channels(self, chan, norm):
         perm = [(f, (f % self.n_dp) * self.n_t + f // self.n_dp) for f in range(self.n_dp * self.n_t)]
@@ -1137,17 +1151,13 @@
         return [lax.psum_scatter(gw[0], "dp", scatter_dimension=0, tiled=True)]
 
     def grads_last(self, parts):
-        return parts[0].astype(f32)
-
-    def scatter_channels(self, sums):
-        return lax.psum_scatter(sums, "dp", scatter_dimension=0, tiled=True)
-
-    def owner_channels(self, sums):
+        return parts[0], lambda part: part.astype(f32)
+
+    def scatter_small(self, sums, norm):
+        sums = lax.psum_scatter(sums, "dp", scatter_dimension=0, tiled=True)
+        norm = lax.psum_scatter(norm, self.both, scatter_dimension=1, tiled=True)
         perm = [((f % self.n_dp) * self.n_t + f // self.n_dp, f) for f in range(self.n_dp * self.n_t)]
-        return lax.ppermute(sums, self.both, perm)
-
-    def scatter_norm(self, sums):
-        return lax.psum_scatter(sums, self.both, scatter_dimension=1, tiled=True)
+        return (sums, norm), lambda part: (lax.ppermute(part[0], self.both, perm), part[1])
 
 
 class Pairs:
@@ -1222,12 +1232,12 @@
     def spot(self):
         return 2 * lax.axis_index("q") + lax.axis_index("h")
 
-    def enter(self, rank, x, chan, norm, pack):
+    def enter(self, rank, x, g, chan, norm, pack):
         small = norm.shape[1]
         norm = jnp.pad(norm, ((0, 5), (0, BLK - small)))
-        got, chan, norm, weights = meet(self.both, rank, x, chan, norm, pack)
+        got, got_g, chan, norm, weights = meet(self.both, rank, x, g, chan, norm, pack)
         norm = norm[:, :3, :small].transpose(1, 0, 2).reshape(3, -1)
-        return got.reshape(x.shape), chan, norm, weights
+        return got.reshape(x.shape), got_g.reshape(x.shape), chan, norm, weights
 
     def grads_send(self, gw):
         return [gw[0]] + [self.flip(gw[bit], "q", bit) for bit in range(1, self.quads)]
@@ -1241,36 +1251,41 @@
         h = lax.axis_index("h")
         first = jnp.where(h == 0, total[:half], total[half:])
         second = jnp.where(h == 0, total[half:], total[:half])
-        return self.ungroup(first).astype(f32) + lax.ppermute(second, ("c", "h"), self.turned).astype(f32)
+
+        def finish(parts):
+            return self.ungroup(parts[0]).astype(f32) + lax.ppermute(parts[1], ("c", "h"), self.turned).astype(f32)
+
+        return (first, second), finish
 
     def cut_order(self):
         return (lax.axis_index("q") ^ jnp.arange(self.quads)).astype(jnp.int32)
 
-    def scatter_channels(self, sums):
+    def scatter_small(self, sums, norm):
         count = 2 * self.quads
         rows, wide = sums.shape[0] // count, sums.shape[1]
-        sums = jnp.pad(sums, ((0, 0), (0, -wide % 8))).reshape(count, -1, BLK)
-        sums = jnp.take(sums, jnp.arange(count) ^ self.spot(), axis=0)
-        total = None
-        for apart in range(count):
-            perm = []
-            for source in range(4 * count):
-                q, c, h, w = source // 8, source // 4 % 2, source // 2 % 2, source % 2
-                perm.append((source, count * (2 * (1 - c) + w) + ((2 * q + h) ^ apart)))
-            part = lax.ppermute(sums[apart], self.both, perm)
-            total = part if total is None else total + part
-        return total.reshape(rows, -1)[:, :wide]
-
-    def owner_channels(self, sums):
-        return sums
-
-    def scatter_norm(self, sums):
-        count = 8 * self.quads
-        part = sums.reshape(3, count, -1).transpose(1, 0, 2)
-        wide = part.shape[2]
-        part = jnp.pad(part, ((0, 0), (0, 5), (0, BLK - wide)))
-        part = lax.all_to_all(part, self.both, split_axis=0, concat_axis=0, tiled=True)
-        return jnp.sum(part, axis=0)[:3, :wide]
+        norm = norm.reshape(3, 4 * count, -1).transpose(1, 0, 2)
+        small = norm.shape[2]
+        norm = jnp.pad(norm, ((0, 0), (0, 5), (0, BLK - small)))
+        norm = lax.all_to_all(norm, self.both, split_axis=0, concat_axis=0, tiled=True)
+        flat = jnp.pad(sums, ((0, 0), (0, -wide % 8))).reshape(count, -1, BLK)
+        near = jnp.arange(self.quads) ^ lax.axis_index("q")
+        h = lax.axis_index("h")
+        keep, give = jnp.take(flat, 2 * near + h, axis=0), jnp.take(flat, 2 * near + 1 - h, axis=0)
+
+        def finish(parts):
+            keep, give, norm = parts
+            part = keep + self.flip(give, "h")
+            total = None
+            for apart in range(self.quads):
+                perm = []
+                for source in range(4 * count):
+                    q, c, h, w = source // 8, source // 4 % 2, source // 2 % 2, source % 2
+                    perm.append((source, count * (2 * (1 - c) + w) + 2 * (q ^ apart) + h))
+                got = lax.ppermute(part[apart], self.both, perm)
+                total = got if total is None else total + got
+            return total.reshape(rows, -1)[:, :wide], jnp.sum(norm, axis=0)[:3, :small]
+
+        return (keep, give, norm), finish
 
 
 def local(
@@ -1312,8 +1327,8 @@
         ]
     )
     norm = jnp.stack([ln_gain, ln_bias, b_out])
-    got_x, chan_all, norm_all, w_all = net.enter(rank, tokens, chan, norm, pack)
-    got_x, chan_all, norm_all, w_all, table, cotangent = after((got_x, chan_all, norm_all, w_all, table, cotangent))
+    got_x, got_g, chan_all, norm_all, w_all = net.enter(rank, tokens, cotangent, chan, norm, pack)
+    got_x, got_g, chan_all, norm_all, w_all, table = after((got_x, got_g, chan_all, norm_all, w_all, table))
 
     place, lens = table[:rows], table[rows:]
     gain = lanes(norm_all[0])
@@ -1333,28 +1348,23 @@
     tab, seq = sequence_tables(lens, nb)
 
     xt, xd = deal_x(place, got_x, gain, shift)
-    xt, cotangent, ld_pairs, w_pairs, skip, w_all = after((xt, cotangent, ld_pairs, w_pairs, skip, w_all))
+    xt, ld_pairs, w_pairs, skip, w_all = after((xt, ld_pairs, w_pairs, skip, w_all))
     x_got = net.gather_first(xt)
-    (sent_g,) = permute_to(rank, [cotangent])
-    got_g = net.spread(sent_g)
     kh = spectra(ld_pairs, w_pairs, skip, wave)
     w_in, w_back, w_in_t, w_back_t = split_weights(w_all, 4 * ch)
     bias_in = lanes(small[2:6].reshape(-1))
     bias_out = lanes(norm_all[2])
-    early, got_g, kh, w_in_t, bias_in = after((x_got[:-1], got_g, kh, w_in_t, bias_in))
-    got_g = net.regroup(got_g)
+    gt, gd, g_bias_out = deal_g(place, got_g, live_own)
+    early, kh, w_in_t, bias_in, gt = after((x_got[:-1], kh, w_in_t, bias_in, gt))
     kept = None
     for part, start in net.gathered(xt, early):
         kept = project(part, start, nb, live, w_in_t, bias_in, kept)
-    kept, late = after((kept, x_got[-1]))
+    kept, late, gt = after((kept, x_got[-1], gt))
+    g_got = net.gather_first(gt)
     xs = net.gather_last(xt, early + [late])
     for part, start in xs[len(early) + 1 if early else 0 :]:
         kept = project(part, start, nb, live, w_in_t, bias_in, kept)
-    kept, got_g = after((kept, got_g))
     a, da, gg, dg = kept
-    gt, gd, g_bias_out = deal_g(place, got_g, live_own)
-    gt, a = after((gt, a))
-    g_got = net.gather_first(gt)
     y, mix = ssm_scan(tab, seq, a, kh, wave, back, gg)
     g_got, y, mix = after((g_got, y, mix))
     gs = net.gather_last(gt, g_got)
@@ -1396,11 +1406,13 @@
     sums = jnp.concatenate(
         [s0[0], s0[1], s1[0], s1[1], jnp.concatenate([g0[:, :, 0], gb_gate, gb_in], axis=0).T], axis=1
     )
-    norm_sums = net.scatter_norm(jnp.sum(jnp.concatenate([norm_sums, g_bias_out[None]], axis=0), axis=2))
-    sent_in, gw, sums, norm_sums, layer_out = after((sent_in, gw, sums, norm_sums, layer_out))
+    norm_sums = jnp.sum(jnp.concatenate([norm_sums, g_bias_out[None]], axis=0), axis=2)
+    part, finish = net.scatter_small(sums, norm_sums)
+    gw, gw_finish = net.grads_last(gw)
+    sent_in, gw, part, layer_out = after((sent_in, gw, part, layer_out))
     in_grad = permute_from(rank, net.spread(sent_in))
-    sums = net.owner_channels(net.scatter_channels(sums))
-    gw = net.grads_last(gw)
+    gw = gw_finish(gw)
+    sums, norm_sums = finish(part)
     s0 = jnp.stack([sums[:, :STATE], sums[:, STATE : 2 * STATE]])
     s1 = jnp.stack([sums[:, 2 * STATE : 3 * STATE], sums[:, 3 * STATE : 4 * STATE]])
     tail = sums[:, 4 * STATE :].T

time: 563 us -> 556 us (0.988)
  starting transfers between devices: 81.6 us -> 58.3 us
  Pallas kernels: 386 us -> 400 us
    pallas_call x2 -> x1, Pallas kernels: 77.5 us -> 93.7 us  [meet(): pl.pallas_call(partial(meet_body, axes), in_specs=[vmem] * 6, out_specs=[...]
    ppermute x9 -> x5, starting transfers between devices: 20.2 us -> 11 us  [the longest x4 9.35 us: finish(): got = lax.ppermute(part[apart], self.both, perm)]
    ppermute x15 -> x16, starting transfers between devices: 30.9 us -> 22.3 us  [flip(): return lax.ppermute(x, axis, [(i, i ^ bit) for i in range(self.axes[axis])])]
    ppermute x15 -> x16, waiting for transfers between devices: 0.74 us -> 7.29 us  [flip(): return lax.ppermute(x, axis, [(i, i ^ bit) for i in range(self.axes[axis])])]
    all_to_all x3 -> x2, starting transfers between devices: 16 us -> 13.5 us  [spread(): lax.all_to_all(x, ('q', 'c'), split_axis=0, concat_axis=0, tiled=True)]
  transfers between devices with their start and end apart: 33 -> 28, of which waited for: 5 -> 6; matrix products, arithmetic and copies ran while one was open for 7% -> 7% of each run, Pallas kernels for 56% -> 61%
where the time goes in v1:
time: 556 us; the launch traced here: 550 us
  Pallas kernels  400 us (72%)
  starting transfers between devices  58.3 us (10%)
  waiting for transfers between devices  36 us (6%)
  local copies, waits for them, and re-layouts  30.8 us (6%)
  other arithmetic  23.5 us (4%)
    pallas_call x1, Pallas kernels, meet(): pl.pallas_call(partial(meet_body, axes), in_specs=[vmem] * 6, out_specs=[...  93.7 us
    pallas_call x2, Pallas kernels, ssm_back(): pl.pallas_call(partial(back_body, nb, nseq, cc, 64, k == 1), grid=(ch //...  56 us
    pallas_call x8, Pallas kernels, mul_rows(): pl.pallas_call(partial(mul_body, count, extra is not None), grid_spec=plt...  48.5 us
    pallas_call x1, Pallas kernels, ssm_scan(): pl.pallas_call(partial(scan_body, nb, nseq, cc, 32), grid=(2, ch // cc),...  35.4 us
    pallas_call x4, Pallas kernels, chained(): pl.pallas_call(body, grid_spec=pltpu.PrefetchScalarGridSpec(num_scalar_pr...  33.8 us
    pallas_call x1, Pallas kernels, outer_sums(): pl.pallas_call(partial(outer_body, ch, many, cuts, parts), grid_spec=pltp...  28.7 us
    ppermute x3, waiting for transfers between devices, ungroup(): return lax.ppermute(x, ('c', 'h'), self.back)  23.3 us
    ppermute x16, starting transfers between devices, flip(): return lax.ppermute(x, axis, [(i, i ^ bit) for i in range(self.axes[axis])])  22.3 us
  transfers between devices with their start and end apart: 28, of which 6 were waited for; matrix products, arithmetic and copies ran while one was open for 7% of the time, Pallas kernels for 61%

profile of v1, /device:TPU:1, one launch (start us, length us, event | category | flops | bytes accessed | tf_op | source)
XLA Modules:
  0.0 550.1 jit_solution(7606058909015318834)
XLA Ops:
  2.6 3.1 collective-permute-start
  5.7 1.9 convert_reduce_fusion.1
  14.5 1.7 pad_maximum_fusion.pack_ref
  16.2 93.7 %shard_map.332 = (bf16[8,128,768]{2,1,0:T(8,128)(2,1)}, bf16[8,128,768]{2,1,0:T(8,128)(2,1)}, f32[8,104,128]{2,1,0:T(8,128)}, f32[32,8,128]{2,1,0:T(8,128)}, bf16[768,2304]{1,0:T(8,128)(2,1)}) custom-call(s32[1,1024]{1,0:T(1,128)} %bitcast.135, bf16[1024,768]{1,0:T(8,128)(2,1)} %x_ref.1, bf16[1024,768]{1,0:T(8,128)(2,1)} %g_ref.1, ...), custom_call_target="tpu_custom_call" | custom-call | flops 80530640 | bytes 3932160 | tf_op jit(solution)/shard_map/pallas_call | solution.py:1040
  117.2 9.1 %shard_map.333 = (bf16[8,768,128]{2,1,0:T(8,128)(2,1)}, bf16[8,768,128]{2,1,0:T(8,128)(2,1)}) custom-call(s32[1024,1]{1,0:T(8,128)} %copy.111.place_ref, bf16[1024,768]{1,0:T(8,128)(2,1)} %bitcast.113, f32[768,128]{1,0:T(8,128)} %broadcast_in_dim.96.gain_ref, f32[768,128]{1,0:T(8,128)} %broadcast_in_dim.98.shift_ref), custom_call_target="tpu_custom_call" | custom-call | flops 80530640 | bytes 235929 | tf_op jit(solution)/shard_map/pallas_call | solution.py:137
  127.2 12.0 %collective-permute-start.1 = (bf16[8,768,128]{2,1,0:T(8,128)(2,1)}, bf16[8,768,128]{2,1,0:T(8,128)(2,1)S(1)}, u32[]{:S(2)}, u32[]{:S(2)}) collective-permute-start(bf16[8,768,128]{2,1,0:T(8,128)(2,1)} %get-tuple-element.176.x_ref.refs_0_), channel_id=1, source_target_pairs={{0,4},{4,0},{1,5},{5,1},{2,6},{6,2},{3,7},{7,3},{8,12},{12,8},{9,1... | collective-permute-start | bytes 4718600 | tf_op jit(solution)/shard_map/ppermute | solution.py:1175
  140.3 5.9 %shard_map.335 = (bf16[768,1536]{1,0:T(8,128)(2,1)}, bf16[768,768]{1,0:T(8,128)(2,1)}, bf16[1536,768]{1,0:T(8,128)(2,1)}, bf16[768,768]{1,0:T(8,128)(2,1)}) custom-call(bf16[768,2304]{1,0:T(8,128)(2,1)} %get-tuple-element.173.w_ref), custom_call_target="tpu_custom_call" | custom-call | bytes 530841 | tf_op jit(solution)/shard_map/pallas_call | solution.py:821
  147.6 8.1 %shard_map.334 = (bf16[8,768,128]{2,1,0:T(8,128)(2,1)}, bf16[8,768,128]{2,1,0:T(8,128)(2,1)}, f32[768,128]{1,0:T(8,128)}) custom-call(s32[1024,1]{1,0:T(8,128)} %copy.111.place_ref, bf16[1024,768]{1,0:T(8,128)(2,1)} %bitcast.112, f32[8,1,128]{2,1,0:T(1,128)} %bitcast.133), custom_call_target="tpu_custom_call" | custom-call | flops 80530640 | bytes 235929 | tf_op jit(solution)/shard_map/pallas_call | solution.py:152
  155.7 18.4 %shard_map.336.kh_ref = f32[2,8,384,512]{3,2,1,0:T(8,128)} custom-call(f32[2,192,128]{2,1,0:T(8,128)} %bitcast.108, f32[2,192,128]{2,1,0:T(8,128)} %bitcast.118, f32[2,384,128]{2,1,0:T(8,128)} %broadcast_in_dim.100.d_ref, bf16[256,512]{1,0:T(8,128)(2,1)} %constant.216.wave_ref), custom_call_target="tpu_custom_call" | custom-call | flops 1536000000 | bytes 629145 | tf_op jit(solution)/shard_map/pallas_call | solution.py:392
  175.6 8.5 %shard_map.337 = (bf16[2,32,384,128]{3,2,1,0:T(8,128)(2,1)}, bf16[2,32,384,128]{3,2,1,0:T(8,128)(2,1)}, bf16[2,32,384,128]{3,2,1,0:T(8,128)(2,1)}, bf16[2,32,384,128]{3,2,1,0:T(8,128)(2,1)}) custom-call(s32[1]{0:T(128)S(6)} %select_n.79.start_ref, bf16[8,768,128]{2,1,0:T(8,128)(2,1)} %get-tuple-element.176.x_ref.refs_0_, f32[16,1,256]{2,1,0:T(1,128)} %bitcast.121, ...), custom_call_target="tpu_custom_call" | custom-call | flops 120795952 | bytes 393216 | tf_op jit(solution)/shard_map/pallas_call | solution.py:273
  184.0 8.5 %shard_map.338 = (bf16[2,32,384,128]{3,2,1,0:T(8,128)(2,1)}, bf16[2,32,384,128]{3,2,1,0:T(8,128)(2,1)}, bf16[2,32,384,128]{3,2,1,0:T(8,128)(2,1)}, bf16[2,32,384,128]{3,2,1,0:T(8,128)(2,1)}) custom-call(s32[1]{0:T(128)S(6)} %select_n.81.start_ref, ...), custom_call_target="tpu_custom_call", output_to_operand_aliasing={{0}: (5, {}), {1}: (6, {}), {2}: (7, {}), {3}: (8, {})} | custom-call | flops 120795952 | bytes 393216 | tf_op jit(solution)/shard_map/pallas_call | solution.py:273
  197.4 8.4 %shard_map.339 = (bf16[2,32,384,128]{3,2,1,0:T(8,128)(2,1)}, bf16[2,32,384,128]{3,2,1,0:T(8,128)(2,1)}, bf16[2,32,384,128]{3,2,1,0:T(8,128)(2,1)}, bf16[2,32,384,128]{3,2,1,0:T(8,128)(2,1)}) custom-call(s32[1]{0:T(128)S(6)} %select_n.86.start_ref, ...), custom_call_target="tpu_custom_call", output_to_operand_aliasing={{0}: (5, {}), {1}: (6, {}), {2}: (7, {}), {3}: (8, {})} | custom-call | flops 120795952 | bytes 393216 | tf_op jit(solution)/shard_map/pallas_call | solution.py:273
  207.0 8.4 %shard_map.340 = (bf16[2,32,384,128]{3,2,1,0:T(8,128)(2,1)}, bf16[2,32,384,128]{3,2,1,0:T(8,128)(2,1)}, bf16[2,32,384,128]{3,2,1,0:T(8,128)(2,1)}, bf16[2,32,384,128]{3,2,1,0:T(8,128)(2,1)}) custom-call(s32[1]{0:T(128)S(6)} %select_n.80.start_ref, ...), custom_call_target="tpu_custom_call", output_to_operand_aliasing={{0}: (5, {}), {1}: (6, {}), {2}: (7, {}), {3}: (8, {})} | custom-call | flops 120795952 | bytes 393216 | tf_op jit(solution)/shard_map/pallas_call | solution.py:273
  215.4 35.4 %shard_map.341 = (bf16[2,32,384,128]{3,2,1,0:T(8,128)(2,1)}, bf16[2,32,384,128]{3,2,1,0:T(8,128)(2,1)}) custom-call(s32[2,17]{1,0:T(2,128)} %pad_add_fusion.1.tab_ref, s32[2,4]{1,0:T(2,128)} %pad_add_fusion.2.seq_ref, bf16[2,32,384,128]{3,2,1,0:T(8,128)(2,1)} %get-tuple-element.235.a_ref, f32[2,8,384,512]{3,2,1,0:T(8,128)} %shard_map.336.kh_ref, ...), custom_call_target="tpu_custom_call" | custom-call | flops 1920000000 | bytes 1258291 | tf_op jit(solution)/shard_map/pallas_call | solution.py:653
  250.9 4.9 shard_map.343
  257.1 5.3 shard_map.344
  263.6 5.2 shard_map.345
  270.0 16.0 %shard_map.346.gm_ref = bf16[2,32,384,128]{3,2,1,0:T(8,128)(2,1)} custom-call(s32[4]{0:T(128)} %pad_add_fusion.3.at_ref, bf16[8,768,128]{2,1,0:T(8,128)(2,1)} %get-tuple-element.194.refs_0_.refs_4_, bf16[8,768,128]{2,1,0:T(8,128)(2,1)} %collective-permute-done.3.refs_1_.refs_5_, bf16[8,768,128]{2,1,0:T(8,128)(2,1)} %collective-permute-done.4.refs_2_.refs_6_, ...), custom_call_target="tpu_custom_call" | custom-call | flops 241591904 | bytes 629145 | tf_op jit(solution)/shard_map/pallas_call | solution.py:338
  286.6 5.2 shard_map.342.refs_0_
  291.8 27.9 %shard_map.347 = (bf16[1,32,384,128]{3,2,1,0:T(8,128)(2,1)}, bf16[1,32,384,128]{3,2,1,0:T(8,128)(2,1)}, f32[1,8,384,512]{3,2,1,0:T(8,128)}, f32[1,384,256]{2,1,0:T(8,128)}) custom-call(s32[2,17]{1,0:T(2,128)} %pad_add_fusion.1.tab_ref, s32[2,4]{1,0:T(2,128)} %pad_add_fusion.2.seq_ref, bf16[2,32,384,128]{3,2,1,0:T(8,128)(2,1)} %get-tuple-element.235.a_ref, ...), custom_call_target="tpu_custom_call" | custom-call | flops 1536000000 | bytes 1258291 | tf_op jit(solution)/shard_map/pallas_call | solution.py:680
  319.7 3.1 collective-permute-done.9.refs_2_
  323.7 6.8 %shard_map.348 = bf16[1024,768]{1,0:T(8,128)(2,1)} custom-call(s32[1,1024]{1,0:T(1,128)} %bitcast.131, bf16[8,768,128]{2,1,0:T(8,128)(2,1)} %get-tuple-element.167.xd_ref, f32[8,1,128]{2,1,0:T(1,128)} %bitcast.134, f32[768,128]{1,0:T(8,128)} %broadcast_in_dim.102.bias_ref, f32[8,768,128]{2,1,0:T(8,128)} %shard_map.342.refs_0_, ...), custom_call_target="tpu_custom_call" | custom-call | flops 80530640 | bytes 235929 | tf_op jit(solution)/shard_map/pallas_call | solution.py:189
  331.4 28.0 %shard_map.349 = (bf16[1,32,384,128]{3,2,1,0:T(8,128)(2,1)}, bf16[1,32,384,128]{3,2,1,0:T(8,128)(2,1)}, f32[1,8,384,512]{3,2,1,0:T(8,128)}, f32[1,384,256]{2,1,0:T(8,128)}) custom-call(s32[2,17]{1,0:T(2,128)} %pad_add_fusion.1.tab_ref, s32[2,4]{1,0:T(2,128)} %pad_add_fusion.2.seq_ref, bf16[2,32,384,128]{3,2,1,0:T(8,128)(2,1)} %get-tuple-element.235.a_ref, ...), custom_call_target="tpu_custom_call" | custom-call | flops 1536000000 | bytes 1258291 | tf_op jit(solution)/shard_map/pallas_call | solution.py:680
  359.5 12.1 %collective-permute-done.10 = bf16[1024,768]{1,0:T(8,128)(2,1)S(1)} collective-permute-done((bf16[1024,768]{1,0:T(8,128)(2,1)}, bf16[1024,768]{1,0:T(8,128)(2,1)S(1)}, u32[]{:S(2)}, u32[]{:S(2)}) %collective-permute-start.10) | collective-permute-done | bytes 1572896 | tf_op jit(solution)/shard_map/ppermute | solution.py:1184
  371.5 7.2 %shard_map.350 = bf16[8,768,128]{2,1,0:T(8,128)(2,1)} custom-call(s32[1]{0:T(128)S(6)} %select_n.80.start_ref, bf16[768,1536]{1,0:T(8,128)(2,1)} %get-tuple-element.174.w_ref, bf16[1,32,384,128]{3,2,1,0:T(8,128)(2,1)} %get-tuple-element.247.refs_0_.refs_8_, bf16[1,32,384,128]{3,2,1,0:T(8,128)(2,1)} %get-tuple-element.248.refs_1_.refs_9_, ...), custom_call_target="tpu_custom_call" | custom-call | flops 120795952 | bytes 314572 | tf_op jit(solution)/shard_map/pallas_call | solution.py:723
  378.7 6.6 %shard_map.351 = bf16[8,768,128]{2,1,0:T(8,128)(2,1)} custom-call(s32[1]{0:T(128)S(6)} %select_n.88.start_ref, bf16[768,1536]{1,0:T(8,128)(2,1)} %get-tuple-element.174.w_ref, bf16[1,32,384,128]{3,2,1,0:T(8,128)(2,1)} %get-tuple-element.247.refs_0_.refs_8_, bf16[1,32,384,128]{3,2,1,0:T(8,128)(2,1)} %get-tuple-element.248.refs_1_.refs_9_, ...), custom_call_target="tpu_custom_call" | custom-call | flops 120795952 | bytes 314572 | tf_op jit(solution)/shard_map/pallas_call | solution.py:723
  385.4 7.1 %shard_map.352 = bf16[8,768,128]{2,1,0:T(8,128)(2,1)} custom-call(s32[1]{0:T(128)S(6)} %select_n.86.start_ref, bf16[768,1536]{1,0:T(8,128)(2,1)} %get-tuple-element.174.w_ref, bf16[1,32,384,128]{3,2,1,0:T(8,128)(2,1)} %get-tuple-element.247.refs_0_.refs_8_, bf16[1,32,384,128]{3,2,1,0:T(8,128)(2,1)} %get-tuple-element.248.refs_1_.refs_9_, ...), custom_call_target="tpu_custom_call" | custom-call | flops 120795952 | bytes 314572 | tf_op jit(solution)/shard_map/pallas_call | solution.py:723
  394.2 8.6 %all-to-all-start = ((bf16[8,128,768]{2,1,0:T(8,128)(2,1)}), bf16[8,128,768]{2,1,0:T(8,128)(2,1)S(1)}, u32[]{:S(2)}, u32[]{:S(2)}) async-start(bf16[8,128,768]{2,1,0:T(8,128)(2,1)} %bitcast.111), calls=%async_computation | async-start | bytes 3145728 | tf_op jit(solution)/shard_map/all_to_all | solution.py:1187
  404.5 6.9 %shard_map.353.refs_0_ = f32[8,768,128]{2,1,0:T(8,128)} custom-call(s32[1]{0:T(128)S(6)} %select_n.79.start_ref, bf16[768,1536]{1,0:T(8,128)(2,1)} %get-tuple-element.174.w_ref, bf16[1,32,384,128]{3,2,1,0:T(8,128)(2,1)} %get-tuple-element.247.refs_0_.refs_8_, bf16[1,32,384,128]{3,2,1,0:T(8,128)(2,1)} %get-tuple-element.248.refs_1_.refs_9_, ...), custom_call_target="tpu_custom_call" | custom-call | flops 120795952 | bytes 314572 | tf_op jit(solution)/shard_map/pallas_call | solution.py:723
  411.5 28.7 %shard_map.354 = (bf16[192,2304]{1,0:T(8,128)(2,1)}, bf16[192,2304]{1,0:T(8,128)(2,1)}, bf16[192,2304]{1,0:T(8,128)(2,1)}, bf16[192,2304]{1,0:T(8,128)(2,1)}) custom-call(s32[8]{0:T(128)} %concatenate.49.at_ref, bf16[8,768,128]{2,1,0:T(8,128)(2,1)} %get-tuple-element.176.x_ref.refs_0_, bf16[8,768,128]{2,1,0:T(8,128)(2,1)} %copy-done, ...), custom_call_target="tpu_custom_call" | custom-call | flops 724775744 | bytes 1572864 | tf_op jit(solution)/shard_map/pallas_call | solution.py:792
  440.2 10.6 %shard_map.355 = (bf16[1024,768]{1,0:T(8,128)(2,1)}, f32[2,768,128]{2,1,0:T(8,128)}) custom-call(s32[1,1024]{1,0:T(1,128)} %bitcast.132, bf16[8,768,128]{2,1,0:T(8,128)(2,1)} %get-tuple-element.167.xd_ref, bf16[8,768,128]{2,1,0:T(8,128)(2,1)} %get-tuple-element.169.gd_ref, f32[768,128]{1,0:T(8,128)} %broadcast_in_dim.96.gain_ref, ...), custom_call_target="tpu_custom_call" | custom-call | flops 80530640 | bytes 314572 | tf_op jit(solution)/shard_map/pallas_call | solution.py:225
  450.9 2.6 collective-permute-start.17
  454.0 9.9 %shard_map.356 = (f32[1,192,128]{2,1,0:T(8,128)}, f32[1,192,128]{2,1,0:T(8,128)}, f32[1,384,128]{2,1,0:T(8,128)}) custom-call(f32[2,192,128]{2,1,0:T(8,128)} %bitcast.109, f32[1,8,384,512]{3,2,1,0:T(8,128)} %get-tuple-element.280.gh_ref, bf16[512,256]{1,0:T(8,128)(2,1)} %constant.219.back_ref), custom_call_target="tpu_custom_call" | custom-call | flops 768000000 | bytes 314572 | tf_op jit(solution)/shard_map/pallas_call | solution.py:450
  464.0 9.8 %shard_map.357 = (f32[1,192,128]{2,1,0:T(8,128)}, f32[1,192,128]{2,1,0:T(8,128)}, f32[1,384,128]{2,1,0:T(8,128)}) custom-call(f32[2,192,128]{2,1,0:T(8,128)} %bitcast.110, f32[1,8,384,512]{3,2,1,0:T(8,128)} %get-tuple-element.282.gh_ref, bf16[512,256]{1,0:T(8,128)(2,1)} %constant.219.back_ref), custom_call_target="tpu_custom_call" | custom-call | flops 768000000 | bytes 314572 | tf_op jit(solution)/shard_map/pallas_call | solution.py:450
  480.5 1.5 maximum_reduce_fusion
  482.9 6.0 %all-to-all-start.1 = ((f32[32,8,128]{2,1,0:T(8,128)}), f32[32,8,128]{2,1,0:T(8,128)S(1)}, u32[]{:S(2)}, u32[]{:S(2)}) async-start(f32[32,8,128]{2,1,0:T(8,128)} %pad.19.clone), calls=%async_computation.1 | async-start | bytes 262144 | tf_op jit(solution)/shard_map/all_to_all | solution.py:1269
  489.1 4.6 shard_map.358
  493.7 1.6 add_convert_fusion
  496.2 2.2 collective-permute-start.20
  498.5 4.9 all-to-all-start.2
  503.4 4.2 collective-permute-done.20
  508.4 3.7 collective-permute-start.21
  512.1 4.9 collective-permute-start.22
  517.5 1.7 collective-permute-start.19
  519.2 4.6 collective-permute-done.24
  526.1 2.2 subtract_multiply_fusion
  530.4 11.2 %collective-permute-done.18 = bf16[96,2304]{1,0:T(8,128)(2,1)S(1)} collective-permute-done((bf16[96,2304]{1,0:T(8,128)(2,1)S(1)}, bf16[96,2304]{1,0:T(8,128)(2,1)S(1)}, u32[]{:S(2)}, u32[]{:S(2)}) %collective-permute-start.18) | collective-permute-done | bytes 442400 | tf_op jit(solution)/shard_map/ppermute | solution.py:1184
  545.3 4.6 shard_map.359
  (184 shorter events, 54.7 us)
Async XLA Ops:
  2.6 108.4 %collective-permute-start = (s32[1027]{0:T(1024)S(1)}, s32[1027]{0:T(1024)S(1)}, u32[]{:S(2)}, u32[]{:S(2)}) collective-permute-start(s32[1027]{0:T(1024)S(1)} %pad_add_fusion), channel_id=1, source_target_pairs={{0,4},{2,0},{4,6},{6,2},{1,5},{3,1},{5,7},{7,3},{8,12},{10,8},{12,... | collective-permute-start | bytes 12332 | tf_op jit(solution)/shard_map/ppermute | solution.py:1181
  112.8 13.5 %copy-start.19 = (s32[1024]{0:T(1024)}, s32[1024]{0:T(1024)S(1)}, u32[]{:S(2)}) copy-start(s32[1024]{0:T(1024)S(1)} %slice.131) | copy-start | bytes 12292
  127.2 46.9 %collective-permute-start.1 = (bf16[8,768,128]{2,1,0:T(8,128)(2,1)}, bf16[8,768,128]{2,1,0:T(8,128)(2,1)S(1)}, u32[]{:S(2)}, u32[]{:S(2)}) collective-permute-start(bf16[8,768,128]{2,1,0:T(8,128)(2,1)} %get-tuple-element.176.x_ref.refs_0_), channel_id=1, source_target_pairs={{0,4},{4,0},{1,5},{5,1},{2,6},{6,2},{3,7},{7,3},{8,12},{12,8},{9,1... | collective-permute-start | bytes 4718600 | tf_op jit(solution)/shard_map/ppermute | solution.py:1175
  139.2 53.3 %collective-permute-start.2 = (bf16[8,768,128]{2,1,0:T(8,128)(2,1)}, bf16[8,768,128]{2,1,0:T(8,128)(2,1)S(1)}, u32[]{:S(2)}, u32[]{:S(2)}) collective-permute-start(bf16[8,768,128]{2,1,0:T(8,128)(2,1)} %get-tuple-element.176.x_ref.refs_0_), channel_id=1, source_target_pairs={{0,1},{1,0},{2,3},{3,2},{4,5},{5,4},{6,7},{7,6},{8,9},{9,8},{10,11... | collective-permute-start | bytes 4718600 | tf_op jit(solution)/shard_map/ppermute | solution.py:1175
  147.0 27.1 %copy-start.12 = (f32[4096]{0:T(1024)}, f32[4096]{0:T(1024)S(1)}, u32[]{:S(2)}) copy-start(f32[4096]{0:T(1024)S(1)} %convert_reduce_fusion.2) | copy-start | bytes 49156
  174.1 9.9 %copy-start = (bf16[8,768,128]{2,1,0:T(8,128)(2,1)}, bf16[8,768,128]{2,1,0:T(8,128)(2,1)S(1)}, u32[]{:S(2)}) copy-start(bf16[8,768,128]{2,1,0:T(8,128)(2,1)S(1)} %collective-permute-done.1.x_ref.refs_1_) | copy-start | bytes 4718596
  192.5 4.9 copy-start.1
  192.5 13.3 %collective-permute-start.5 = (bf16[8,768,128]{2,1,0:T(8,128)(2,1)S(1)}, bf16[8,768,128]{2,1,0:T(8,128)(2,1)S(1)}, u32[]{:S(2)}, u32[]{:S(2)}) collective-permute-start(bf16[8,768,128]{2,1,0:T(8,128)(2,1)S(1)} %collective-permute-done.2.x_ref.refs_2_), channel_id=1, source_target_pairs={{0,4},{4,0},{1,5},{5,1},{2,6},{6,2},{3,7},{7,3},{8,12},{12,8},{9,1... | collective-permute-start | bytes 4718600 | tf_op jit(solution)/shard_map/ppermute | solution.py:1175
  193.0 57.8 %collective-permute-start.3 = (bf16[8,768,128]{2,1,0:T(8,128)(2,1)}, bf16[8,768,128]{2,1,0:T(8,128)(2,1)}, u32[]{:S(2)}, u32[]{:S(2)}) collective-permute-start(bf16[8,768,128]{2,1,0:T(8,128)(2,1)} %get-tuple-element.194.refs_0_.refs_4_), channel_id=1, source_target_pairs={{0,4},{4,0},{1,5},{5,1},{2,6},{6,2},{3,7},{7,3},{8,12},{12,8},{9,1... | collective-permute-start | bytes 4718600 | tf_op jit(solution)/shard_map/ppermute | solution.py:1175
  193.3 57.6 %collective-permute-start.4 = (bf16[8,768,128]{2,1,0:T(8,128)(2,1)}, bf16[8,768,128]{2,1,0:T(8,128)(2,1)}, u32[]{:S(2)}, u32[]{:S(2)}) collective-permute-start(bf16[8,768,128]{2,1,0:T(8,128)(2,1)} %get-tuple-element.194.refs_0_.refs_4_), channel_id=1, source_target_pairs={{0,1},{1,0},{2,3},{3,2},{4,5},{5,4},{6,7},{7,6},{8,9},{9,8},{10,11... | collective-permute-start | bytes 4718600 | tf_op jit(solution)/shard_map/ppermute | solution.py:1175
  255.8 6.6 %collective-permute-start.6 = (bf16[8,768,128]{2,1,0:T(8,128)(2,1)}, bf16[8,768,128]{2,1,0:T(8,128)(2,1)S(1)}, u32[]{:S(2)}, u32[]{:S(2)}) collective-permute-start(bf16[8,768,128]{2,1,0:T(8,128)(2,1)} %shard_map.343), channel_id=1, source_target_pairs={{0,4},{4,0},{1,5},{5,1},{2,6},{6,2},{3,7},{7,3},{8,12},{12,8},{9,1... | collective-permute-start | bytes 4718600 | tf_op jit(solution)/shard_map/ppermute | solution.py:1175
  256.5 12.3 %collective-permute-start.7 = (bf16[8,768,128]{2,1,0:T(8,128)(2,1)}, bf16[8,768,128]{2,1,0:T(8,128)(2,1)S(1)}, u32[]{:S(2)}, u32[]{:S(2)}) collective-permute-start(bf16[8,768,128]{2,1,0:T(8,128)(2,1)} %collective-permute-done.4.refs_2_.refs_6_), channel_id=1, source_target_pairs={{0,4},{4,0},{1,5},{5,1},{2,6},{6,2},{3,7},{7,3},{8,12},{12,8},{9,1... | collective-permute-start | bytes 4718600 | tf_op jit(solution)/shard_map/ppermute | solution.py:1175
  268.8 1.2 copy-start.3
  270.0 16.0 %copy-start.7 = (bf16[8,768,128]{2,1,0:T(8,128)(2,1)S(1)}, bf16[8,768,128]{2,1,0:T(8,128)(2,1)}, u32[]{:S(2)}) copy-start(bf16[8,768,128]{2,1,0:T(8,128)(2,1)} %shard_map.344) | copy-start | bytes 4718596
  286.0 33.7 %collective-permute-start.8 = (bf16[8,768,128]{2,1,0:T(8,128)(2,1)S(1)}, bf16[8,768,128]{2,1,0:T(8,128)(2,1)S(1)}, u32[]{:S(2)}, u32[]{:S(2)}) collective-permute-start(bf16[8,768,128]{2,1,0:T(8,128)(2,1)S(1)} %copy-done.7), channel_id=1, source_target_pairs={{0,4},{4,0},{1,5},{5,1},{2,6},{6,2},{3,7},{7,3},{8,12},{12,8},{9,1... | collective-permute-start | bytes 4718600 | tf_op jit(solution)/shard_map/ppermute | solution.py:1175
  286.6 36.3 %collective-permute-start.9 = (bf16[8,768,128]{2,1,0:T(8,128)(2,1)}, bf16[8,768,128]{2,1,0:T(8,128)(2,1)}, u32[]{:S(2)}, u32[]{:S(2)}) collective-permute-start(bf16[8,768,128]{2,1,0:T(8,128)(2,1)} %shard_map.345), channel_id=1, source_target_pairs={{0,1},{1,0},{2,3},{3,2},{4,5},{5,4},{6,7},{7,6},{8,9},{9,8},{10,11... | collective-permute-start | bytes 4718600 | tf_op jit(solution)/shard_map/ppermute | solution.py:1175
  319.7 4.0 copy-start.10
  330.6 41.0 %collective-permute-start.10 = (bf16[1024,768]{1,0:T(8,128)(2,1)}, bf16[1024,768]{1,0:T(8,128)(2,1)S(1)}, u32[]{:S(2)}, u32[]{:S(2)}) collective-permute-start(bf16[1024,768]{1,0:T(8,128)(2,1)} %shard_map.348), channel_id=1, source_target_pairs={{4,0},{0,2},{6,4},{2,6},{5,1},{1,3},{7,5},{3,7},{12,8},{8,10},{14,... | collective-permute-start | bytes 4718600 | tf_op jit(solution)/shard_map/ppermute | solution.py:1184
  371.5 7.2 %copy-start.8 = (bf16[1024,768]{1,0:T(8,128)(2,1)}, bf16[1024,768]{1,0:T(8,128)(2,1)S(1)}, u32[]{:S(2)}) copy-start(bf16[1024,768]{1,0:T(8,128)(2,1)S(1)} %collective-permute-done.10) | copy-start | bytes 4718596
  378.7 6.7 %collective-permute-start.11 = (bf16[8,768,128]{2,1,0:T(8,128)(2,1)}, bf16[8,768,128]{2,1,0:T(8,128)(2,1)}, u32[]{:S(2)}, u32[]{:S(2)}) collective-permute-start(bf16[8,768,128]{2,1,0:T(8,128)(2,1)} %shard_map.350), channel_id=1, source_target_pairs={{0,4},{4,0},{1,5},{5,1},{2,6},{6,2},{3,7},{7,3},{8,12},{12,8},{9,1... | collective-permute-start | bytes 4718600 | tf_op jit(solution)/shard_map/ppermute | solution.py:1175
  385.4 7.1 %copy-start.6 = (bf16[8,768,128]{2,1,0:T(8,128)(2,1)S(1)}, bf16[8,768,128]{2,1,0:T(8,128)(2,1)}, u32[]{:S(2)}) copy-start(bf16[8,768,128]{2,1,0:T(8,128)(2,1)} %shard_map.351) | copy-start | bytes 4718596
  392.4 10.4 %copy-start.20 = (s32[1024]{0:T(1024)S(1)}, s32[1024]{0:T(1024)}, u32[]{:S(2)}) copy-start(s32[1024]{0:T(1024)} %convert_reduce_fusion.1) | copy-start | bytes 12292
  392.4 47.7 %collective-permute-start.12 = (bf16[8,768,128]{2,1,0:T(8,128)(2,1)S(1)}, bf16[8,768,128]{2,1,0:T(8,128)(2,1)}, u32[]{:S(2)}, u32[]{:S(2)}) collective-permute-start(bf16[8,768,128]{2,1,0:T(8,128)(2,1)S(1)} %copy-done.6), channel_id=1, source_target_pairs={{0,4},{4,0},{1,5},{5,1},{2,6},{6,2},{3,7},{7,3},{8,12},{12,8},{9,1... | collective-permute-start | bytes 4718600 | tf_op jit(solution)/shard_map/ppermute | solution.py:1175
  393.0 47.2 %collective-permute-start.13 = (bf16[8,768,128]{2,1,0:T(8,128)(2,1)}, bf16[8,768,128]{2,1,0:T(8,128)(2,1)}, u32[]{:S(2)}, u32[]{:S(2)}) collective-permute-start(bf16[8,768,128]{2,1,0:T(8,128)(2,1)} %shard_map.352), channel_id=1, source_target_pairs={{0,1},{1,0},{2,3},{3,2},{4,5},{5,4},{6,7},{7,6},{8,9},{9,8},{10,11... | collective-permute-start | bytes 4718600 | tf_op jit(solution)/shard_map/ppermute | solution.py:1175
  394.2 46.0 %all-to-all-start = ((bf16[8,128,768]{2,1,0:T(8,128)(2,1)}), bf16[8,128,768]{2,1,0:T(8,128)(2,1)S(1)}, u32[]{:S(2)}, u32[]{:S(2)}) async-start(bf16[8,128,768]{2,1,0:T(8,128)(2,1)} %bitcast.111), calls=%async_computation | async-start | bytes 3145728 | tf_op jit(solution)/shard_map/all_to_all | solution.py:1187
  440.2 10.7 %copy-start.4 = (bf16[8,128,768]{2,1,0:T(8,128)(2,1)}, bf16[8,128,768]{2,1,0:T(8,128)(2,1)S(1)}, u32[]{:S(2)}) copy-start(bf16[8,128,768]{2,1,0:T(8,128)(2,1)S(1)} %all-to-all-done) | copy-start | bytes 4718596
  450.8 13.1 %copy-start.13 = (f32[1,384,256]{2,1,0:T(8,128)S(1)}, f32[1,384,256]{2,1,0:T(8,128)}, u32[]{:S(2)}) copy-start(f32[1,384,256]{2,1,0:T(8,128)} %get-tuple-element.288) | copy-start | bytes 1179652
  450.8 45.4 %collective-permute-start.14 = (bf16[1024,768]{1,0:T(8,128)(2,1)}, bf16[1024,768]{1,0:T(8,128)(2,1)}, u32[]{:S(2)}, u32[]{:S(2)}) collective-permute-start(bf16[1024,768]{1,0:T(8,128)(2,1)} %get-tuple-element.275), channel_id=1, source_target_pairs={{4,0},{0,2},{6,4},{2,6},{5,1},{1,3},{7,5},{3,7},{12,8},{8,10},{14,... | collective-permute-start | bytes 4718600 | tf_op jit(solution)/shard_map/ppermute | solution.py:1184
  450.9 42.8 %collective-permute-start.17 = (bf16[192,2304]{1,0:T(8,128)(2,1)}, bf16[192,2304]{1,0:T(8,128)(2,1)S(1)}, u32[]{:S(2)}, u32[]{:S(2)}) collective-permute-start(bf16[192,2304]{1,0:T(8,128)(2,1)} %get-tuple-element.279), channel_id=1, source_target_pairs={{0,24},{8,16},{16,8},{24,0},{1,25},{9,17},{17,9},{25,1},{2,26},{10... | collective-permute-start | bytes 2654216 | tf_op jit(solution)/shard_map/ppermute | solution.py:1175
  453.5 40.2 %collective-permute-start.16 = (bf16[192,2304]{1,0:T(8,128)(2,1)}, bf16[192,2304]{1,0:T(8,128)(2,1)S(1)}, u32[]{:S(2)}, u32[]{:S(2)}) collective-permute-start(bf16[192,2304]{1,0:T(8,128)(2,1)} %get-tuple-element.278), channel_id=1, source_target_pairs={{0,16},{8,24},{16,0},{24,8},{1,17},{9,25},{17,1},{25,9},{2,18},{10... | collective-permute-start | bytes 2654216 | tf_op jit(solution)/shard_map/ppermute | solution.py:1175
  454.0 39.7 %collective-permute-start.15 = (bf16[192,2304]{1,0:T(8,128)(2,1)}, bf16[192,2304]{1,0:T(8,128)(2,1)}, u32[]{:S(2)}, u32[]{:S(2)}) collective-permute-start(bf16[192,2304]{1,0:T(8,128)(2,1)} %get-tuple-element.277), channel_id=1, source_target_pairs={{0,8},{8,0},{16,24},{24,16},{1,9},{9,1},{17,25},{25,17},{2,10},{10... | collective-permute-start | bytes 2654216 | tf_op jit(solution)/shard_map/ppermute | solution.py:1175
  463.9 9.9 %copy-start.18 = (f32[1,192,128]{2,1,0:T(8,128)S(1)}, f32[1,192,128]{2,1,0:T(8,128)}, u32[]{:S(2)}) copy-start(f32[1,192,128]{2,1,0:T(8,128)} %get-tuple-element.281) | copy-start | bytes 294916
  463.9 10.9 %copy-start.17 = (f32[1,192,128]{2,1,0:T(8,128)S(1)}, f32[1,192,128]{2,1,0:T(8,128)}, u32[]{:S(2)}) copy-start(f32[1,192,128]{2,1,0:T(8,128)} %get-tuple-element.284) | copy-start | bytes 294916
  464.0 12.0 %copy-start.15 = (f32[1,384,128]{2,1,0:T(8,128)S(1)}, f32[1,384,128]{2,1,0:T(8,128)}, u32[]{:S(2)}) copy-start(f32[1,384,128]{2,1,0:T(8,128)} %get-tuple-element.286) | copy-start | bytes 589828
  478.8 1.7 copy-start.14
  482.9 13.3 %all-to-all-start.1 = ((f32[32,8,128]{2,1,0:T(8,128)}), f32[32,8,128]{2,1,0:T(8,128)S(1)}, u32[]{:S(2)}, u32[]{:S(2)}) async-start(f32[32,8,128]{2,1,0:T(8,128)} %pad.19.clone), calls=%async_computation.1 | async-start | bytes 262144 | tf_op jit(solution)/shard_map/all_to_all | solution.py:1269
  489.1 4.7 copy-start.11
  496.2 11.4 %collective-permute-start.20 = (f32[4,99,128]{2,1,0:T(8,128)S(1)}, f32[4,99,128]{2,1,0:T(8,128)S(1)}, u32[]{:S(2)}, u32[]{:S(2)}) collective-permute-start(f32[4,99,128]{2,1,0:T(8,128)S(1)} %broadcast_select_fusion.2), channel_id=1, source_target_pairs={{0,2},{2,0},{1,3},{3,1},{4,6},{6,4},{5,7},{7,5},{8,10},{10,8},{9,1... | collective-permute-start | bytes 608264 | tf_op jit(solution)/shard_map/ppermute | solution.py:1175
  498.5 27.7 %copy-start.16 = (f32[2,48,64]{2,1,0:T(8,128)S(1)}, f32[2,48,64]{2,1,0:T(8,128)}, u32[]{:S(2)}) copy-start(f32[2,48,64]{2,1,0:T(8,128)} %param.39) | copy-start | bytes 73732
  498.5 27.7 %copy-start.22 = (f32[2,48]{1,0:T(2,128)S(1)}, f32[2,48]{1,0:T(2,128)}, u32[]{:S(2)}) copy-start(f32[2,48]{1,0:T(2,128)} %copy-done.21) | copy-start | bytes 1156
  498.5 27.7 %copy-start.23 = (f32[2,48]{1,0:T(2,128)S(1)}, f32[2,48]{1,0:T(2,128)}, u32[]{:S(2)}) copy-start(f32[2,48]{1,0:T(2,128)} %get-tuple-element.432) | copy-start | bytes 1156
  498.5 45.6 %all-to-all-start.2 = ((bf16[8,128,768]{2,1,0:T(8,128)(2,1)}), bf16[8,128,768]{2,1,0:T(8,128)(2,1)S(1)}, u32[]{:S(2)}, u32[]{:S(2)}) async-start(bf16[8,128,768]{2,1,0:T(8,128)(2,1)} %bitcast.49), calls=%async_computation.2 | async-start | bytes 3145728 | tf_op jit(solution)/shard_map/all_to_all | solution.py:1187
  507.7 16.1 %collective-permute-start.24 = (f32[99,128]{1,0:T(8,128)S(1)}, f32[99,128]{1,0:T(8,128)S(1)}, u32[]{:S(2)}, u32[]{:S(2)}) collective-permute-start(f32[99,128]{1,0:T(8,128)S(1)} %get-tuple-element.416), channel_id=1, source_target_pairs={{0,22},{1,30},{2,23},{3,31},{4,6},{5,14},{6,7},{7,15},{8,20},{9,28... | collective-permute-start | bytes 152072 | tf_op jit(solution)/shard_map/ppermute | solution.py:1284
  507.7 17.4 %collective-permute-start.23 = (f32[99,128]{1,0:T(8,128)S(1)}, f32[99,128]{1,0:T(8,128)S(1)}, u32[]{:S(2)}, u32[]{:S(2)}) collective-permute-start(f32[99,128]{1,0:T(8,128)S(1)} %get-tuple-element.417), channel_id=1, source_target_pairs={{0,20},{1,28},{2,21},{3,29},{4,4},{5,12},{6,5},{7,13},{8,22},{9,30... | collective-permute-start | bytes 152072 | tf_op jit(solution)/shard_map/ppermute | solution.py:1284
  508.4 16.8 %collective-permute-start.21 = (f32[99,128]{1,0:T(8,128)S(1)}, f32[99,128]{1,0:T(8,128)S(1)}, u32[]{:S(2)}, u32[]{:S(2)}) collective-permute-start(f32[99,128]{1,0:T(8,128)S(1)} %get-tuple-element.418), channel_id=1, source_target_pairs={{0,16},{1,24},{2,17},{3,25},{4,0},{5,8},{6,1},{7,9},{8,18},{9,26},... | collective-permute-start | bytes 152072 | tf_op jit(solution)/shard_map/ppermute | solution.py:1284
  512.1 13.8 %collective-permute-start.22 = (f32[99,128]{1,0:T(8,128)S(1)}, f32[99,128]{1,0:T(8,128)S(1)}, u32[]{:S(2)}, u32[]{:S(2)}) collective-permute-start(f32[99,128]{1,0:T(8,128)S(1)} %get-tuple-element.415), channel_id=1, source_target_pairs={{0,18},{1,26},{2,19},{3,27},{4,2},{5,10},{6,3},{7,11},{8,16},{9,24... | collective-permute-start | bytes 152072 | tf_op jit(solution)/shard_map/ppermute | solution.py:1284
  517.5 12.8 %collective-permute-start.19 = (bf16[96,2304]{1,0:T(8,128)(2,1)}, bf16[96,2304]{1,0:T(8,128)(2,1)S(1)}, u32[]{:S(2)}, u32[]{:S(2)}) collective-permute-start(bf16[96,2304]{1,0:T(8,128)(2,1)} %get-tuple-element.297), channel_id=1, source_target_pairs={{0,6},{2,2},{4,4},{6,0},{1,7},{3,3},{5,5},{7,1},{8,14},{10,10},{12... | collective-permute-start | bytes 1327112 | tf_op jit(solution)/shard_map/ppermute | solution.py:1256
  523.8 17.8 %collective-permute-start.18 = (bf16[96,2304]{1,0:T(8,128)(2,1)S(1)}, bf16[96,2304]{1,0:T(8,128)(2,1)S(1)}, u32[]{:S(2)}, u32[]{:S(2)}) collective-permute-start(bf16[96,2304]{1,0:T(8,128)(2,1)S(1)} %get-tuple-element.296), channel_id=1, source_target_pairs={{4,0},{0,2},{6,4},{2,6},{5,1},{1,3},{7,5},{3,7},{12,8},{8,10},{14,... | collective-permute-start | bytes 1327112 | tf_op jit(solution)/shard_map/ppermute | solution.py:1184
  (4 other events, 4.5 us)

commit v2 on v1

--- a/solution.py
+++ b/solution.py
@@ -808,19 +808,25 @@
     )(order, *xs, *gs, *gp, *gpg, mix)
 
 
-def join_body(split, w_ref, head_ref, tail_ref, head_t_ref, tail_t_ref):
-    head_ref[...] = w_ref[:, :split]
-    tail_ref[...] = w_ref[:, split:]
-    head_t_ref[...] = w_ref[:, :split].T
-    tail_t_ref[...] = w_ref[:, split:].T
-
-
-def split_weights(w, split):
-    rows, wide = w.shape
+def join_body(parts, split, at_ref, *refs):
+    head_ref, tail_ref, head_t_ref, tail_t_ref = refs[parts:]
+    deep = refs[0].shape[0]
+    for at in range(parts):
+        rows = pl.ds(pl.multiple_of(at_ref[at] * deep, 16), deep)
+        head_ref[rows, :] = refs[at][:, :split]
+        tail_ref[rows, :] = refs[at][:, split:]
+    head_t_ref[...] = head_ref[...].T
+    tail_t_ref[...] = tail_ref[...].T
+
+
+def join_weights(order, parts, split):
+    count = len(parts)
+    deep, wide = parts[0].shape
+    rows = deep * count
     vmem = pl.BlockSpec(memory_space=pltpu.VMEM)
     return pl.pallas_call(
-        partial(join_body, split),
-        in_specs=[vmem],
+        partial(join_body, count, split),
+        in_specs=[pl.BlockSpec(memory_space=pltpu.SMEM)] + [vmem] * count,
         out_specs=[vmem] * 4,
         out_shape=[
             jax.ShapeDtypeStruct(shape, bf16)
@@ -828,14 +834,11 @@
         ],
         compiler_params=params(48),
         cost_estimate=cost(0, 6 * rows * wide),
-    )(w)
-
-
-def meet_body(
-    axes, rank_ref, x_ref, g_ref, chan_ref, norm_ref, pack_ref, got_ref, gotg_ref, call_ref, nall_ref, wall_ref,
-    send_s, sendg_s, *sems
-):
-    xs_sem, xr_sem, gs_sem, gr_sem, cs_sem, cr_sem, ns_sem, nr_sem, ws_sem, wr_sem, own_sem = sems
+    )(order, *parts)
+
+
+def meet_body(axes, rank_ref, x_ref, chan_ref, norm_ref, got_ref, call_ref, nall_ref, send_s, *sems):
+    xs_sem, xr_sem, cs_sem, cr_sem, ns_sem, nr_sem, own_sem = sems
     q, c, h, w = (lax.axis_index(name) for name in axes)
     rows = x_ref.shape[0]
     piece = rows // 8
@@ -854,37 +857,6 @@
             src_ref=src, dst_ref=dst, send_sem=send, recv_sem=recv, device_id=to, device_id_type=pl.DeviceIdType.MESH
         )
 
-    deep = pack_ref.shape[0]
-
-    def shard(at):
-        return wall_ref.at[pl.ds(pl.multiple_of(at * deep, 16), deep)]
-
-    def first_copy():
-        return remote(pack_ref, shard(2 * q + c), ws_sem.at[0], wr_sem.at[c], (q, 1 - h, c, w))
-
-    def second_copy():
-        return remote(pack_ref, shard(2 * q + c), ws_sem.at[1], wr_sem.at[c], (q, 1 - h, 1 - c, w))
-
-    def own_shard():
-        return pltpu.make_async_copy(pack_ref, shard(2 * q + c), own_sem.at[2])
-
-    def shard_came(at):
-        return remote(pack_ref, shard(2 * q + at), ws_sem.at[0], wr_sem.at[at], peer(1))
-
-    def pass_on(at, bits):
-        spot_w = 3 * at + bits + 1
-        return remote(shard(2 * q + at), shard(2 * q + at), ws_sem.at[spot_w], wr_sem.at[spot_w], (q ^ bits, c, h, w))
-
-    first_copy().start()
-
-    @pl.when(c != h)
-    def _():
-        own_shard().start()
-
-    @pl.when(c == h)
-    def _():
-        second_copy().start()
-
     nall_ref[flat] = norm_ref[...]
 
     def norm_copy(bits):
@@ -893,93 +865,80 @@
     for bits in range(1, 32):
         norm_copy(bits).start()
 
-    pieces = [(kq, kh) for kh in (0, 1) for kq in (1, 2, 3, 0)]
+    place = 2 * (1 - c) + w
+    spot_c = 4 * c + 2 * h + w
+
+    def chan_copy(at):
+        to = (q ^ at, 1 - q // 2, h, q % 2) if at < 4 else (2 * c + w, 1 - q // 2, 1 - h, q % 2)
+        return remote(chan_ref, call_ref.at[spot_c], cs_sem.at[at], cr_sem.at[spot_c], to)
+
+    def own_chan():
+        return pltpu.make_async_copy(chan_ref, call_ref.at[spot_c], own_sem.at[1])
+
+    def chan_came(at):
+        return remote(chan_ref, call_ref.at[at], cs_sem.at[0], cr_sem.at[at], peer(1))
+
+    far_spot = 4 * (q // 2) + 2 * (1 - h) + q % 2
+
+    def chan_pass(bits):
+        return remote(
+            call_ref.at[far_spot], call_ref.at[far_spot], cs_sem.at[4 + bits], cr_sem.at[far_spot], (q ^ bits, c, h, w)
+        )
+
+    for at in (4, 1, 2, 3, 0):
+        if at:
+            chan_copy(at).start()
+        else:
+
+            @pl.when(place == q)
+            def _():
+                own_chan().start()
+
+            @pl.when(place != q)
+            def _():
+                chan_copy(0).start()
+
+    pieces = [(kq, kh) for kh in (1, 0) for kq in (1, 2, 3, 0)]
     spot = lax.broadcasted_iota(jnp.int32, (piece, rows), 0)
 
-    x_side = (send_s, got_ref, xs_sem, xr_sem, 0)
-    g_side = (sendg_s, gotg_ref, gs_sem, gr_sem, 3)
-
-    def row_copy(side, kq, kh):
-        held, got, send, recv, _ = side
+    def row_copy(kq, kh):
         at = 2 * kq + kh
-        return remote(held.at[at], got.at[2 * q + c], send.at[at], recv.at[2 * kq + c], (q ^ kq, 1 - h, h ^ kh, w))
-
-    def own_copy(side):
-        held, got, _, _, at = side
-        return pltpu.make_async_copy(held.at[0], got.at[2 * q + c], own_sem.at[at])
-
-    def send_rows(side, kq, kh):
-        if (kq, kh) == (0, 0):
-
-            @pl.when(c != h)
-            def _():
-                own_copy(side).start()
-
-            @pl.when(c == h)
-            def _():
-                row_copy(side, 0, 0).start()
-
-        else:
-            row_copy(side, kq, kh).start()
+        return remote(
+            send_s.at[at], got_ref.at[2 * q + c], xs_sem.at[at], xr_sem.at[2 * kq + c], (q ^ kq, 1 - h, h ^ kh, w)
+        )
+
+    def own_copy():
+        return pltpu.make_async_copy(send_s.at[0], got_ref.at[2 * q + c], own_sem.at[0])
 
     for kq, kh in pieces:
         chunk = 2 * (q ^ kq) + (h ^ kh)
         pick = jnp.where(spot + chunk * piece == rank_ref[...], 1.0, 0.0).astype(bf16)
         send_s[2 * kq + kh] = nn(pick, x_ref[...]).astype(bf16)
-        sendg_s[2 * kq + kh] = nn(pick, g_ref[...]).astype(bf16)
-        if (kq, kh) == (1, 1):
-            for at in range(2):
-
-                @pl.when((c != h) & (at == c))
-                def _():
-                    own_shard().wait()
-
-                @pl.when(jnp.logical_not((c != h) & (at == c)))
-                def _(at=at):
-                    shard_came(at).wait_recv()
-
-                for bits in range(1, 4):
-                    pass_on(at, bits).start()
-        send_rows(x_side, kq, kh)
-
-    place = 2 * (1 - c) + w
-    spot_c = 4 * c + 2 * h + w
-
-    def chan_copy(at):
-        to = (q ^ at, 1 - q // 2, h, q % 2) if at < 4 else (2 * c + w, 1 - q // 2, 1 - h, q % 2)
-        return remote(chan_ref, call_ref.at[spot_c], cs_sem.at[at], cr_sem.at[spot_c], to)
-
-    def own_chan():
-        return pltpu.make_async_copy(chan_ref, call_ref.at[spot_c], own_sem.at[1])
-
-    def chan_came(at):
-        return remote(chan_ref, call_ref.at[at], cs_sem.at[0], cr_sem.at[at], peer(1))
-
-    far_spot = 4 * (q // 2) + 2 * (1 - h) + q % 2
-
-    def chan_pass(bits):
-        return remote(
-            call_ref.at[far_spot], call_ref.at[far_spot], cs_sem.at[4 + bits], cr_sem.at[far_spot], (q ^ bits, c, h, w)
-        )
-
-    for at in (4, 1, 2, 3, 0):
-        if at:
-            chan_copy(at).start()
+        if (kq, kh) == (0, 0):
+
+            @pl.when(c != h)
+            def _():
+                own_copy().start()
+
+            @pl.when(c == h)
+            def _():
+                row_copy(0, 0).start()
+
         else:
-
-            @pl.when(place == q)
-            def _():
-                own_chan().start()
-
-            @pl.when(place != q)
-            def _():
-                chan_copy(0).start()
-
-    for kq, kh in pieces[4:] + pieces[:4]:
-        send_rows(g_side, kq, kh)
+            row_copy(kq, kh).start()
 
     for bits in range(1, 32):
         norm_copy(bits).wait()
+    for at in range(8):
+
+        @pl.when((c != h) & (at == c))
+        def _():
+            own_copy().wait()
+
+        @pl.when(jnp.logical_not((c != h) & (at == c)))
+        def _(at=at):
+            remote(send_s.at[at], got_ref.at[at], xs_sem.at[at], xr_sem.at[at], peer(1)).wait_recv()
+
     chan_came(far_spot).wait_recv()
     for bits in range(1, 4):
         chan_pass(bits).start()
@@ -995,36 +954,15 @@
 
     for bits in range(1, 4):
         chan_pass(bits).wait_send()
-    for at in range(2):
-        for bits in range(1, 4):
-            pass_on(at, bits).wait()
-    first_copy().wait_send()
-
-    @pl.when(c == h)
-    def _():
-        second_copy().wait_send()
-
-    for side in (x_side, g_side):
-        held, got, send, recv, _ = side
-        for at in range(8):
-
-            @pl.when((c != h) & (at == c))
-            def _(side=side):
-                own_copy(side).wait()
-
-            @pl.when(jnp.logical_not((c != h) & (at == c)))
-            def _(at=at, held=held, got=got, send=send, recv=recv):
-                remote(held.at[at], got.at[at], send.at[at], recv.at[at], peer(1)).wait_recv()
-
-        for kq, kh in pieces:
-            if (kq, kh) == (0, 0):
-
-                @pl.when(c == h)
-                def _(side=side):
-                    row_copy(side, 0, 0).wait_send()
-
-            else:
-                row_copy(side, kq, kh).wait_send()
+    for kq, kh in pieces:
+        if (kq, kh) == (0, 0):
+
+            @pl.when(c == h)
+            def _():
+                row_copy(0, 0).wait_send()
+
+        else:
+            row_copy(kq, kh).wait_send()
     for at in range(1, 5):
         chan_copy(at).wait_send()
 
@@ -1033,26 +971,24 @@
         chan_copy(0).wait_send()
 
 
-def meet(axes, rank, x, g, chan, norm, pack):
+def meet(axes, rank, x, chan, norm):
     rows, width = x.shape
     vmem = pl.BlockSpec(memory_space=pltpu.VMEM)
     sem = pltpu.SemaphoreType.DMA
     return pl.pallas_call(
         partial(meet_body, axes),
-        in_specs=[vmem] * 6,
-        out_specs=[vmem] * 5,
+        in_specs=[vmem] * 4,
+        out_specs=[vmem] * 3,
         out_shape=[
-            jax.ShapeDtypeStruct((8, rows // 8, width), bf16),
             jax.ShapeDtypeStruct((8, rows // 8, width), bf16),
             jax.ShapeDtypeStruct((8,) + chan.shape, f32),
             jax.ShapeDtypeStruct((32,) + norm.shape, f32),
-            jax.ShapeDtypeStruct((8 * pack.shape[0], pack.shape[1]), bf16),
         ],
-        scratch_shapes=[pltpu.VMEM((8, rows // 8, width), bf16)] * 2
-        + [sem((8,)), sem((8,)), sem((8,)), sem((8,)), sem((8,)), sem((8,)), sem((32,)), sem((32,)), sem((8,)), sem((8,)), sem((4,))],
+        scratch_shapes=[pltpu.VMEM((8, rows // 8, width), bf16)]
+        + [sem((8,)), sem((8,)), sem((8,)), sem((8,)), sem((32,)), sem((32,)), sem((2,))],
         compiler_params=pltpu.CompilerParams(collective_id=1, has_side_effects=True, vmem_limit_bytes=60 * MIB),
         cost_estimate=cost(2 * rows * rows * width, 100 * rows * width),
-    )(rank.reshape(1, rows), x, g, chan, norm, pack)
+    )(rank.reshape(1, rows), x, chan, norm)
 
 
 def sequence_tables(lens, nb):
@@ -1104,27 +1040,27 @@
     def place_of_group(self):
         return lax.axis_index("tensor")
 
+    def gather_first(self, x):
+        return [lax.all_gather(x, "tensor", axis=0, tiled=True)]
+
+    def gathered(self, x, early):
+        return []
+
+    def gather_last(self, x, got):
+        return [(got[0], jnp.zeros((1,), jnp.int32))]
+
+    def scatter_first(self, w, arrays, many):
+        return [mul_rows(w, arrays, jnp.zeros((1,), jnp.int32), many * self.n_t)]
+
+    def scatter_send(self, parts):
+        return [lax.psum_scatter(parts[0], "tensor", scatter_dimension=0, tiled=True)]
+
+    def scatter_own(self, w, arrays, many):
+        return []
+
     def regroup(self, x):
         return x
 
-    def gather_first(self, x):
-        return [lax.all_gather(x, "tensor", axis=0, tiled=True)]
-
-    def gathered(self, x, early):
-        return []
-
-    def gather_last(self, x, got):
-        return [(got[0], jnp.zeros((1,), jnp.int32))]
-
-    def scatter_first(self, w, arrays, many):
-        return [mul_rows(w, arrays, jnp.zeros((1,), jnp.int32), many * self.n_t)]
-
-    def scatter_send(self, parts):
-        return [lax.psum_scatter(parts[0], "tensor", scatter_dimension=0, tiled=True)]
-
-    def scatter_own(self, w, arrays, many):
-        return []
-
     def ungroup(self, x):
         return x
 
@@ -1134,9 +1070,15 @@
     def order(self, pieces):
         return jnp.append(jnp.arange(pieces * self.n_t, dtype=jnp.int32), 0)
 
-    def enter(self, rank, x, g, chan, norm, pack):
-        sent_x, sent_g = permute_to(rank, [x, g])
-        return (self.spread(sent_x), self.spread(sent_g)) + self.gather_channels(chan, norm) + (lax.all_gather(pack, "dp", axis=0, tiled=True),)
+    def enter(self, rank, x, chan, norm):
+        (sent,) = permute_to(rank, [x])
+        return (self.spread(sent),) + self.gather_channels(chan, norm)
+
+    def weights_first(self, pack):
+        return [pack]
+
+    def weights_send(self, packs):
+        return [lax.all_gather(packs[0], "dp", axis=0, tiled=True)]
 
     def gather_channels(self, chan, norm):
         perm = [(f, (f % self.n_dp) * self.n_t + f // self.n_dp) for f in range(self.n_dp * self.n_t)]
@@ -1232,12 +1174,21 @@
     def spot(self):
         return 2 * lax.axis_index("q") + lax.axis_index("h")
 
-    def enter(self, rank, x, g, chan, norm, pack):
+    def enter(self, rank, x, chan, norm):
         small = norm.shape[1]
         norm = jnp.pad(norm, ((0, 5), (0, BLK - small)))
-        got, got_g, chan, norm, weights = meet(self.both, rank, x, g, chan, norm, pack)
+        got, chan, norm = meet(self.both, rank, x, chan, norm)
         norm = norm[:, :3, :small].transpose(1, 0, 2).reshape(3, -1)
-        return got.reshape(x.shape), got_g.reshape(x.shape), chan, norm, weights
+        return got.reshape(x.shape), chan, norm
+
+    def weights_first(self, pack):
+        return [self.regroup(pack), lax.ppermute(pack, ("c", "h"), self.turned)]
+
+    def weights_send(self, packs):
+        h = lax.axis_index("h")
+        first, second = packs
+        pair = jnp.concatenate([jnp.where(h == 0, first, second), jnp.where(h == 0, second, first)], axis=0)
+        return [pair] + [self.flip(pair, "q", bit) for bit in range(1, self.quads)]
 
     def grads_send(self, gw):
         return [gw[0]] + [self.flip(gw[bit], "q", bit) for bit in range(1, self.quads)]
@@ -1327,8 +1278,12 @@
         ]
     )
     norm = jnp.stack([ln_gain, ln_bias, b_out])
-    got_x, got_g, chan_all, norm_all, w_all = net.enter(rank, tokens, cotangent, chan, norm, pack)
-    got_x, got_g, chan_all, norm_all, w_all, table = after((got_x, got_g, chan_all, norm_all, w_all, table))
+    (sent_g,) = permute_to(rank, [cotangent])
+    sent_g, tokens = after((sent_g, tokens))
+    got_g = net.spread(sent_g)
+    got_x, chan_all, norm_all = net.enter(rank, tokens, chan, norm)
+    got_x, got_g, chan_all, norm_all, pack, table = after((got_x, got_g, chan_all, norm_all, pack, table))
+    packs = net.weights_first(pack)
 
     place, lens = table[:rows], table[rows:]
     gain = lanes(norm_all[0])
@@ -1348,23 +1303,24 @@
     tab, seq = sequence_tables(lens, nb)
 
     xt, xd = deal_x(place, got_x, gain, shift)
-    xt, ld_pairs, w_pairs, skip, w_all = after((xt, ld_pairs, w_pairs, skip, w_all))
     x_got = net.gather_first(xt)
+    _, ld_pairs, w_pairs, skip, packs = after((xt, ld_pairs, w_pairs, skip, packs))
+    w_parts = net.weights_send(packs)
     kh = spectra(ld_pairs, w_pairs, skip, wave)
-    w_in, w_back, w_in_t, w_back_t = split_weights(w_all, 4 * ch)
+    w_parts, x_got, kh, norm_all, small, got_g = after((w_parts, x_got, kh, norm_all, small, got_g))
     bias_in = lanes(small[2:6].reshape(-1))
     bias_out = lanes(norm_all[2])
+    got_g = net.regroup(got_g)
+    w_in, w_back, w_in_t, w_back_t = join_weights(net.cut_order(), w_parts, 4 * ch)
+    xs = net.gather_last(xt, x_got)
+    kept = None
+    for part, start in xs:
+        kept = project(part, start, nb, live, w_in_t, bias_in, kept)
+    kept, got_g = after((kept, got_g))
+    a, da, gg, dg = kept
     gt, gd, g_bias_out = deal_g(place, got_g, live_own)
-    early, kh, w_in_t, bias_in, gt = after((x_got[:-1], kh, w_in_t, bias_in, gt))
-    kept = None
-    for part, start in net.gathered(xt, early):
-        kept = project(part, start, nb, live, w_in_t, bias_in, kept)
-    kept, late, gt = after((kept, x_got[-1], gt))
+    gt, a = after((gt, a))
     g_got = net.gather_first(gt)
-    xs = net.gather_last(xt, early + [late])
-    for part, start in xs[len(early) + 1 if early else 0 :]:
-        kept = project(part, start, nb, live, w_in_t, bias_in, kept)
-    a, da, gg, dg = kept
     y, mix = ssm_scan(tab, seq, a, kh, wave, back, gg)
     g_got, y, mix = after((g_got, y, mix))
     gs = net.gather_last(gt, g_got)

time: 556 us -> 544 us (0.978)
  Pallas kernels: 400 us -> 350 us
  starting transfers between devices: 58.3 us -> 83.5 us
  waiting for transfers between devices: 36 us -> 52.1 us
    pallas_call x2 -> x3, Pallas kernels: 99.6 us -> 49.5 us  [the longest x1 40.1 us: meet(): pl.pallas_call(partial(meet_body, axes), in_specs=[vmem] * 4, out_specs=[...]
    ppermute x16 -> x19, waiting for transfers between devices: 7.29 us -> 27 us  [flip(): return lax.ppermute(x, axis, [(i, i ^ bit) for i in range(self.axes[axis])])]
    all_to_all x2 -> x3, starting transfers between devices: 13.5 us -> 23.1 us  [spread(): lax.all_to_all(x, ('q', 'c'), split_axis=0, concat_axis=0, tiled=True)]
    ppermute x1 -> x3, starting transfers between devices: 3.14 us -> 11.6 us  [regroup(): return lax.ppermute(x, ('c', 'h'), self.there)]
    ppermute x16 -> x19, starting transfers between devices: 22.3 us -> 24.2 us  [flip(): return lax.ppermute(x, axis, [(i, i ^ bit) for i in range(self.axes[axis])])]
  transfers between devices with their start and end apart: 28 -> 35, of which waited for: 6 -> 8; matrix products, arithmetic and copies ran while one was open for 7% -> 8% of each run, Pallas kernels for 61% -> 52%
where the time goes in v2:
time: 544 us; the launch traced here: 534 us
  Pallas kernels  350 us (64%)
  starting transfers between devices  83.5 us (15%)
  waiting for transfers between devices  52.1 us (10%)
  local copies, waits for them, and re-layouts  25.3 us (5%)
  other arithmetic  21.1 us (4%)
    pallas_call x2, Pallas kernels, ssm_back(): pl.pallas_call(partial(back_body, nb, nseq, cc, 64, k == 1), grid=(ch //...  55.7 us
    pallas_call x8, Pallas kernels, mul_rows(): pl.pallas_call(partial(mul_body, count, extra is not None), grid_spec=plt...  49 us
    pallas_call x1, Pallas kernels, meet(): pl.pallas_call(partial(meet_body, axes), in_specs=[vmem] * 4, out_specs=[...  40.1 us
    pallas_call x1, Pallas kernels, ssm_scan(): pl.pallas_call(partial(scan_body, nb, nseq, cc, 32), grid=(2, ch // cc),...  35.4 us
    pallas_call x4, Pallas kernels, chained(): pl.pallas_call(body, grid_spec=pltpu.PrefetchScalarGridSpec(num_scalar_pr...  34.3 us
    pallas_call x1, Pallas kernels, outer_sums(): pl.pallas_call(partial(outer_body, ch, many, cuts, parts), grid_spec=pltp...  28.7 us
    ppermute x19, waiting for transfers between devices, flip(): return lax.ppermute(x, axis, [(i, i ^ bit) for i in range(self.axes[axis])])  27 us
    ppermute x19, starting transfers between devices, flip(): return lax.ppermute(x, axis, [(i, i ^ bit) for i in range(self.axes[axis])])  24.2 us
  transfers between devices with their start and end apart: 35, of which 8 were waited for; matrix products, arithmetic and copies ran while one was open for 8% of the time, Pallas kernels for 52%

profile of v2, /device:TPU:1, one launch (start us, length us, event | category | flops | bytes accessed | tf_op | source)
XLA Modules:
  0.0 534.3 jit_solution(17552022946698598751)
XLA Ops:
  2.6 4.4 shard_map.332
  7.1 5.4 %all-to-all-start = ((bf16[8,128,768]{2,1,0:T(8,128)(2,1)}), bf16[8,128,768]{2,1,0:T(8,128)(2,1)S(1)}, u32[]{:S(2)}, u32[]{:S(2)}) async-start(bf16[8,128,768]{2,1,0:T(8,128)(2,1)} %bitcast.109), calls=%async_computation | async-start | bytes 3145728 | tf_op jit(solution)/shard_map/all_to_all | solution.py:1129
  13.1 2.4 collective-permute-start
  18.1 40.1 %shard_map.333 = (bf16[8,128,768]{2,1,0:T(8,128)(2,1)}, f32[8,104,128]{2,1,0:T(8,128)}, f32[32,8,128]{2,1,0:T(8,128)}) custom-call(s32[1,1024]{1,0:T(1,128)} %bitcast.133, bf16[1024,768]{1,0:T(8,128)(2,1)} %x_ref, f32[104,128]{1,0:T(8,128)} %pad_maximum_fusion.3.chan_ref, f32[8,128]{1,0:T(8,128)} %select_maximum_fusion.norm_ref), custom_call_target="tpu_custom_call" | custom-call | flops 80530640 | bytes 3932160 | tf_op jit(solution)/shard_map/pallas_call | solution.py:978
  60.1 8.5 %collective-permute-start.1 = (bf16[96,2304]{1,0:T(8,128)(2,1)}, bf16[96,2304]{1,0:T(8,128)(2,1)}, u32[]{:S(2)}, u32[]{:S(2)}) collective-permute-start(bf16[96,2304]{1,0:T(8,128)(2,1)} %pad_maximum_fusion.1), channel_id=1, source_target_pairs={{0,4},{2,0},{4,6},{6,2},{1,5},{3,1},{5,7},{7,3},{8,12},{10,8},{12,... | collective-permute-start | bytes 1327112 | tf_op jit(solution)/shard_map/ppermute | solution.py:1123
  68.5 5.0 collective-permute-start.2
  76.5 8.9 %shard_map.334 = (bf16[8,768,128]{2,1,0:T(8,128)(2,1)}, bf16[8,768,128]{2,1,0:T(8,128)(2,1)}) custom-call(s32[1024,1]{1,0:T(8,128)} %copy.111.place_ref, bf16[1024,768]{1,0:T(8,128)(2,1)} %bitcast.115, f32[768,128]{1,0:T(8,128)} %broadcast_in_dim.96.gain_ref, f32[768,128]{1,0:T(8,128)} %broadcast_in_dim.98.shift_ref), custom_call_target="tpu_custom_call" | custom-call | flops 80530640 | bytes 235929 | tf_op jit(solution)/shard_map/pallas_call | solution.py:137
  85.4 4.8 collective-permute-start.6
  90.2 4.1 collective-permute-start.7
  102.0 18.4 %shard_map.335.kh_ref = f32[2,8,384,512]{3,2,1,0:T(8,128)} custom-call(f32[2,192,128]{2,1,0:T(8,128)} %bitcast.110, f32[2,192,128]{2,1,0:T(8,128)} %bitcast.120, f32[2,384,128]{2,1,0:T(8,128)} %broadcast_in_dim.100.d_ref, bf16[256,512]{1,0:T(8,128)(2,1)} %constant.216.wave_ref), custom_call_target="tpu_custom_call" | custom-call | flops 1536000000 | bytes 629145 | tf_op jit(solution)/shard_map/pallas_call | solution.py:392
  121.5 18.3 %collective-permute-done.5.refs_3_ = bf16[192,2304]{1,0:T(8,128)(2,1)} collective-permute-done((bf16[192,2304]{1,0:T(8,128)(2,1)}, bf16[192,2304]{1,0:T(8,128)(2,1)}, u32[]{:S(2)}, u32[]{:S(2)}) %collective-permute-start.5) | collective-permute-done | bytes 884768 | tf_op jit(solution)/shard_map/ppermute | solution.py:1117
  139.9 2.3 collective-permute-start.8
  146.0 5.0 shard_map.336
  152.3 8.8 %shard_map.337 = (bf16[2,32,384,128]{3,2,1,0:T(8,128)(2,1)}, bf16[2,32,384,128]{3,2,1,0:T(8,128)(2,1)}, bf16[2,32,384,128]{3,2,1,0:T(8,128)(2,1)}, bf16[2,32,384,128]{3,2,1,0:T(8,128)(2,1)}) custom-call(s32[1]{0:T(128)S(6)} %select_n.92.start_ref, bf16[8,768,128]{2,1,0:T(8,128)(2,1)} %get-tuple-element.174.x_ref.refs_0_, f32[16,1,256]{2,1,0:T(1,128)} %bitcast.123, ...), custom_call_target="tpu_custom_call" | custom-call | flops 120795952 | bytes 393216 | tf_op jit(solution)/shard_map/pallas_call | solution.py:273
  161.1 8.5 %shard_map.338 = (bf16[2,32,384,128]{3,2,1,0:T(8,128)(2,1)}, bf16[2,32,384,128]{3,2,1,0:T(8,128)(2,1)}, bf16[2,32,384,128]{3,2,1,0:T(8,128)(2,1)}, bf16[2,32,384,128]{3,2,1,0:T(8,128)(2,1)}) custom-call(s32[1]{0:T(128)S(6)} %select_n.91.start_ref, ...), custom_call_target="tpu_custom_call", output_to_operand_aliasing={{0}: (5, {}), {1}: (6, {}), {2}: (7, {}), {3}: (8, {})} | custom-call | flops 120795952 | bytes 393216 | tf_op jit(solution)/shard_map/pallas_call | solution.py:273
  169.6 8.4 %shard_map.339 = (bf16[2,32,384,128]{3,2,1,0:T(8,128)(2,1)}, bf16[2,32,384,128]{3,2,1,0:T(8,128)(2,1)}, bf16[2,32,384,128]{3,2,1,0:T(8,128)(2,1)}, bf16[2,32,384,128]{3,2,1,0:T(8,128)(2,1)}) custom-call(s32[1]{0:T(128)S(6)} %select_n.90.start_ref, ...), custom_call_target="tpu_custom_call", output_to_operand_aliasing={{0}: (5, {}), {1}: (6, {}), {2}: (7, {}), {3}: (8, {})} | custom-call | flops 120795952 | bytes 393216 | tf_op jit(solution)/shard_map/pallas_call | solution.py:273
  178.0 8.5 %shard_map.340 = (bf16[2,32,384,128]{3,2,1,0:T(8,128)(2,1)}, bf16[2,32,384,128]{3,2,1,0:T(8,128)(2,1)}, bf16[2,32,384,128]{3,2,1,0:T(8,128)(2,1)}, bf16[2,32,384,128]{3,2,1,0:T(8,128)(2,1)}) custom-call(s32[1]{0:T(128)S(6)} %select_n.85.start_ref, ...), custom_call_target="tpu_custom_call", output_to_operand_aliasing={{0}: (5, {}), {1}: (6, {}), {2}: (7, {}), {3}: (8, {})} | custom-call | flops 120795952 | bytes 393216 | tf_op jit(solution)/shard_map/pallas_call | solution.py:273
  186.5 8.1 %shard_map.341 = (bf16[8,768,128]{2,1,0:T(8,128)(2,1)}, bf16[8,768,128]{2,1,0:T(8,128)(2,1)}, f32[768,128]{1,0:T(8,128)}) custom-call(s32[1024,1]{1,0:T(8,128)} %copy.111.place_ref, bf16[1024,768]{1,0:T(8,128)(2,1)} %collective-permute-done.9.g_ref, f32[8,1,128]{2,1,0:T(1,128)} %bitcast.138), custom_call_target="tpu_custom_call" | custom-call | flops 80530640 | bytes 235929 | tf_op jit(solution)/shard_map/pallas_call | solution.py:152
  199.0 35.4 %shard_map.342 = (bf16[2,32,384,128]{3,2,1,0:T(8,128)(2,1)}, bf16[2,32,384,128]{3,2,1,0:T(8,128)(2,1)}) custom-call(s32[2,17]{1,0:T(2,128)} %pad_add_fusion.1.tab_ref, s32[2,4]{1,0:T(2,128)} %pad_add_fusion.2.seq_ref, bf16[2,32,384,128]{3,2,1,0:T(8,128)(2,1)} %get-tuple-element.247.a_ref, f32[2,8,384,512]{3,2,1,0:T(8,128)} %shard_map.335.kh_ref, ...), custom_call_target="tpu_custom_call" | custom-call | flops 1920000000 | bytes 1258291 | tf_op jit(solution)/shard_map/pallas_call | solution.py:653
  234.4 6.0 %shard_map.344 = bf16[8,768,128]{2,1,0:T(8,128)(2,1)} custom-call(s32[1]{0:T(128)S(6)} %select_n.85.start_ref, bf16[768,768]{1,0:T(8,128)(2,1)} %get-tuple-element.212.w_ref, bf16[2,32,384,128]{3,2,1,0:T(8,128)(2,1)} %get-tuple-element.265.refs_0_.refs_12_), custom_call_target="tpu_custom_call" | custom-call | flops 60397976 | bytes 235929 | tf_op jit(solution)/shard_map/pallas_call | solution.py:723
  241.8 4.9 shard_map.345
  246.7 5.2 shard_map.346
  253.2 16.0 %shard_map.347.gm_ref = bf16[2,32,384,128]{3,2,1,0:T(8,128)(2,1)} custom-call(s32[4]{0:T(128)} %pad_add_fusion.3.at_ref, bf16[8,768,128]{2,1,0:T(8,128)(2,1)} %get-tuple-element.215.refs_0_.refs_4_, bf16[8,768,128]{2,1,0:T(8,128)(2,1)} %copy-done.2, bf16[8,768,128]{2,1,0:T(8,128)(2,1)} %copy-done.3, bf16[8,768,128]{2,1,0:T(8,128)(2,1)} %copy-done.4, ...), custom_call_target="tpu_custom_call" | custom-call | flops 241591904 | bytes 629145 | tf_op jit(solution)/shard_map/pallas_call | solution.py:338
  269.7 5.2 shard_map.343.refs_0_
  274.8 27.9 %shard_map.348 = (bf16[1,32,384,128]{3,2,1,0:T(8,128)(2,1)}, bf16[1,32,384,128]{3,2,1,0:T(8,128)(2,1)}, f32[1,8,384,512]{3,2,1,0:T(8,128)}, f32[1,384,256]{2,1,0:T(8,128)}) custom-call(s32[2,17]{1,0:T(2,128)} %pad_add_fusion.1.tab_ref, s32[2,4]{1,0:T(2,128)} %pad_add_fusion.2.seq_ref, bf16[2,32,384,128]{3,2,1,0:T(8,128)(2,1)} %get-tuple-element.247.a_ref, ...), custom_call_target="tpu_custom_call" | custom-call | flops 1536000000 | bytes 1258291 | tf_op jit(solution)/shard_map/pallas_call | solution.py:680
  302.8 3.1 collective-permute-done.15.refs_2_
  306.8 6.9 %shard_map.349 = bf16[1024,768]{1,0:T(8,128)(2,1)} custom-call(s32[1,1024]{1,0:T(1,128)} %bitcast.136, bf16[8,768,128]{2,1,0:T(8,128)(2,1)} %get-tuple-element.173.xd_ref, f32[8,1,128]{2,1,0:T(1,128)} %bitcast.139, f32[768,128]{1,0:T(8,128)} %broadcast_in_dim.104.bias_ref, f32[8,768,128]{2,1,0:T(8,128)} %shard_map.343.refs_0_, ...), custom_call_target="tpu_custom_call" | custom-call | flops 80530640 | bytes 235929 | tf_op jit(solution)/shard_map/pallas_call | solution.py:189
  314.6 27.8 %shard_map.350 = (bf16[1,32,384,128]{3,2,1,0:T(8,128)(2,1)}, bf16[1,32,384,128]{3,2,1,0:T(8,128)(2,1)}, f32[1,8,384,512]{3,2,1,0:T(8,128)}, f32[1,384,256]{2,1,0:T(8,128)}) custom-call(s32[2,17]{1,0:T(2,128)} %pad_add_fusion.1.tab_ref, s32[2,4]{1,0:T(2,128)} %pad_add_fusion.2.seq_ref, bf16[2,32,384,128]{3,2,1,0:T(8,128)(2,1)} %get-tuple-element.247.a_ref, ...), custom_call_target="tpu_custom_call" | custom-call | flops 1536000000 | bytes 1258291 | tf_op jit(solution)/shard_map/pallas_call | solution.py:680
  342.4 8.5 %collective-permute-done.16 = bf16[1024,768]{1,0:T(8,128)(2,1)S(1)} collective-permute-done((bf16[1024,768]{1,0:T(8,128)(2,1)}, bf16[1024,768]{1,0:T(8,128)(2,1)S(1)}, u32[]{:S(2)}, u32[]{:S(2)}) %collective-permute-start.16) | collective-permute-done | bytes 1572896 | tf_op jit(solution)/shard_map/ppermute | solution.py:1126
  350.9 7.2 %shard_map.351 = bf16[8,768,128]{2,1,0:T(8,128)(2,1)} custom-call(s32[1]{0:T(128)S(6)} %select_n.85.start_ref, bf16[768,1536]{1,0:T(8,128)(2,1)} %get-tuple-element.210.w_ref, bf16[1,32,384,128]{3,2,1,0:T(8,128)(2,1)} %get-tuple-element.259.refs_0_.refs_8_, bf16[1,32,384,128]{3,2,1,0:T(8,128)(2,1)} %get-tuple-element.260.refs_1_.refs_9_, ...), custom_call_target="tpu_custom_call" | custom-call | flops 120795952 | bytes 314572 | tf_op jit(solution)/shard_map/pallas_call | solution.py:723
  358.1 6.6 %shard_map.352 = bf16[8,768,128]{2,1,0:T(8,128)(2,1)} custom-call(s32[1]{0:T(128)S(6)} %select_n.99.start_ref, bf16[768,1536]{1,0:T(8,128)(2,1)} %get-tuple-element.210.w_ref, bf16[1,32,384,128]{3,2,1,0:T(8,128)(2,1)} %get-tuple-element.259.refs_0_.refs_8_, bf16[1,32,384,128]{3,2,1,0:T(8,128)(2,1)} %get-tuple-element.260.refs_1_.refs_9_, ...), custom_call_target="tpu_custom_call" | custom-call | flops 120795952 | bytes 314572 | tf_op jit(solution)/shard_map/pallas_call | solution.py:723
  364.8 7.1 %shard_map.353 = bf16[8,768,128]{2,1,0:T(8,128)(2,1)} custom-call(s32[1]{0:T(128)S(6)} %select_n.90.start_ref, bf16[768,1536]{1,0:T(8,128)(2,1)} %get-tuple-element.210.w_ref, bf16[1,32,384,128]{3,2,1,0:T(8,128)(2,1)} %get-tuple-element.259.refs_0_.refs_8_, bf16[1,32,384,128]{3,2,1,0:T(8,128)(2,1)} %get-tuple-element.260.refs_1_.refs_9_, ...), custom_call_target="tpu_custom_call" | custom-call | flops 120795952 | bytes 314572 | tf_op jit(solution)/shard_map/pallas_call | solution.py:723
  373.9 12.8 %all-to-all-start.1 = ((bf16[8,128,768]{2,1,0:T(8,128)(2,1)}), bf16[8,128,768]{2,1,0:T(8,128)(2,1)S(1)}, u32[]{:S(2)}, u32[]{:S(2)}) async-start(bf16[8,128,768]{2,1,0:T(8,128)(2,1)} %bitcast.114), calls=%async_computation.1 | async-start | bytes 3145728 | tf_op jit(solution)/shard_map/all_to_all | solution.py:1129
  388.5 6.9 %shard_map.354.refs_0_ = f32[8,768,128]{2,1,0:T(8,128)} custom-call(s32[1]{0:T(128)S(6)} %select_n.92.start_ref, bf16[768,1536]{1,0:T(8,128)(2,1)} %get-tuple-element.210.w_ref, bf16[1,32,384,128]{3,2,1,0:T(8,128)(2,1)} %get-tuple-element.259.refs_0_.refs_8_, bf16[1,32,384,128]{3,2,1,0:T(8,128)(2,1)} %get-tuple-element.260.refs_1_.refs_9_, ...), custom_call_target="tpu_custom_call" | custom-call | flops 120795952 | bytes 314572 | tf_op jit(solution)/shard_map/pallas_call | solution.py:723
  395.4 28.7 %shard_map.355 = (bf16[192,2304]{1,0:T(8,128)(2,1)}, bf16[192,2304]{1,0:T(8,128)(2,1)}, bf16[192,2304]{1,0:T(8,128)(2,1)}, bf16[192,2304]{1,0:T(8,128)(2,1)}) custom-call(s32[8]{0:T(128)} %concatenate.53.at_ref, bf16[8,768,128]{2,1,0:T(8,128)(2,1)} %get-tuple-element.174.x_ref.refs_0_, bf16[8,768,128]{2,1,0:T(8,128)(2,1)} %copy-done, ...), custom_call_target="tpu_custom_call" | custom-call | flops 724775744 | bytes 1572864 | tf_op jit(solution)/shard_map/pallas_call | solution.py:792
  424.1 10.6 %shard_map.356 = (bf16[1024,768]{1,0:T(8,128)(2,1)}, f32[2,768,128]{2,1,0:T(8,128)}) custom-call(s32[1,1024]{1,0:T(1,128)} %bitcast.137, bf16[8,768,128]{2,1,0:T(8,128)(2,1)} %get-tuple-element.173.xd_ref, bf16[8,768,128]{2,1,0:T(8,128)(2,1)} %get-tuple-element.209.gd_ref, f32[768,128]{1,0:T(8,128)} %broadcast_in_dim.96.gain_ref, ...), custom_call_target="tpu_custom_call" | custom-call | flops 80530640 | bytes 314572 | tf_op jit(solution)/shard_map/pallas_call | solution.py:225
  434.8 2.6 collective-permute-start.23
  437.7 9.9 %shard_map.357 = (f32[1,192,128]{2,1,0:T(8,128)}, f32[1,192,128]{2,1,0:T(8,128)}, f32[1,384,128]{2,1,0:T(8,128)}) custom-call(f32[2,192,128]{2,1,0:T(8,128)} %bitcast.111, f32[1,8,384,512]{3,2,1,0:T(8,128)} %get-tuple-element.292.gh_ref, bf16[512,256]{1,0:T(8,128)(2,1)} %constant.219.back_ref), custom_call_target="tpu_custom_call" | custom-call | flops 768000000 | bytes 314572 | tf_op jit(solution)/shard_map/pallas_call | solution.py:450
  447.7 9.8 %shard_map.358 = (f32[1,192,128]{2,1,0:T(8,128)}, f32[1,192,128]{2,1,0:T(8,128)}, f32[1,384,128]{2,1,0:T(8,128)}) custom-call(f32[2,192,128]{2,1,0:T(8,128)} %bitcast.112, f32[1,8,384,512]{3,2,1,0:T(8,128)} %get-tuple-element.294.gh_ref, bf16[512,256]{1,0:T(8,128)(2,1)} %constant.219.back_ref), custom_call_target="tpu_custom_call" | custom-call | flops 768000000 | bytes 314572 | tf_op jit(solution)/shard_map/pallas_call | solution.py:450
  466.6 6.4 %all-to-all-start.2 = ((f32[32,8,128]{2,1,0:T(8,128)}), f32[32,8,128]{2,1,0:T(8,128)S(1)}, u32[]{:S(2)}, u32[]{:S(2)}) async-start(f32[32,8,128]{2,1,0:T(8,128)} %pad.19.clone), calls=%async_computation.2 | async-start | bytes 262144 | tf_op jit(solution)/shard_map/all_to_all | solution.py:1220
  473.2 4.6 shard_map.359
  482.6 4.9 all-to-all-start.3
  487.5 4.3 collective-permute-done.26
  492.6 3.6 collective-permute-start.27
  496.2 4.9 collective-permute-start.28
  503.3 4.6 collective-permute-done.30
  514.5 11.2 %collective-permute-done.24 = bf16[96,2304]{1,0:T(8,128)(2,1)S(1)} collective-permute-done((bf16[96,2304]{1,0:T(8,128)(2,1)S(1)}, bf16[96,2304]{1,0:T(8,128)(2,1)S(1)}, u32[]{:S(2)}, u32[]{:S(2)}) %collective-permute-start.24) | collective-permute-done | bytes 442400 | tf_op jit(solution)/shard_map/ppermute | solution.py:1126
  529.3 4.6 shard_map.360
  (243 shorter events, 64.3 us)
Async XLA Ops:
  7.1 53.0 %all-to-all-start = ((bf16[8,128,768]{2,1,0:T(8,128)(2,1)}), bf16[8,128,768]{2,1,0:T(8,128)(2,1)S(1)}, u32[]{:S(2)}, u32[]{:S(2)}) async-start(bf16[8,128,768]{2,1,0:T(8,128)(2,1)} %bitcast.109), calls=%async_computation | async-start | bytes 3145728 | tf_op jit(solution)/shard_map/all_to_all | solution.py:1129
  12.4 45.7 %copy-start.26 = (bf16[96,384]{1,0:T(8,128)(2,1)S(1)}, bf16[96,384]{1,0:T(8,128)(2,1)}, u32[]{:S(2)}) copy-start(bf16[96,384]{1,0:T(8,128)(2,1)} %param.32) | copy-start | bytes 221188
  12.4 45.7 %copy-start.27 = (bf16[96,384]{1,0:T(8,128)(2,1)S(1)}, bf16[96,384]{1,0:T(8,128)(2,1)}, u32[]{:S(2)}) copy-start(bf16[96,384]{1,0:T(8,128)(2,1)} %param.30) | copy-start | bytes 221188
  13.1 47.0 %collective-permute-start = (s32[1027]{0:T(1024)S(1)}, s32[1027]{0:T(1024)S(1)}, u32[]{:S(2)}, u32[]{:S(2)}) collective-permute-start(s32[1027]{0:T(1024)S(1)} %pad_add_fusion), channel_id=1, source_target_pairs={{0,4},{2,0},{4,6},{6,2},{1,5},{3,1},{5,7},{7,3},{8,12},{10,8},{12,... | collective-permute-start | bytes 12332 | tf_op jit(solution)/shard_map/ppermute | solution.py:1123
  60.1 25.3 %copy-start.9 = (bf16[8,128,768]{2,1,0:T(8,128)(2,1)}, bf16[8,128,768]{2,1,0:T(8,128)(2,1)S(1)}, u32[]{:S(2)}) copy-start(bf16[8,128,768]{2,1,0:T(8,128)(2,1)S(1)} %all-to-all-done) | copy-start | bytes 4718596
  60.1 35.7 %collective-permute-start.1 = (bf16[96,2304]{1,0:T(8,128)(2,1)}, bf16[96,2304]{1,0:T(8,128)(2,1)}, u32[]{:S(2)}, u32[]{:S(2)}) collective-permute-start(bf16[96,2304]{1,0:T(8,128)(2,1)} %pad_maximum_fusion.1), channel_id=1, source_target_pairs={{0,4},{2,0},{4,6},{6,2},{1,5},{3,1},{5,7},{7,3},{8,12},{10,8},{12,... | collective-permute-start | bytes 1327112 | tf_op jit(solution)/shard_map/ppermute | solution.py:1123
  68.5 27.3 %collective-permute-start.2 = (bf16[96,2304]{1,0:T(8,128)(2,1)}, bf16[96,2304]{1,0:T(8,128)(2,1)}, u32[]{:S(2)}, u32[]{:S(2)}) collective-permute-start(bf16[96,2304]{1,0:T(8,128)(2,1)} %pad_maximum_fusion.1), channel_id=1, source_target_pairs={{0,6},{2,2},{4,4},{6,0},{1,7},{3,3},{5,5},{7,1},{8,14},{10,10},{12... | collective-permute-start | bytes 1327112 | tf_op jit(solution)/shard_map/ppermute | solution.py:1185
  73.5 11.9 %copy-start.29 = (s32[1024]{0:T(1024)}, s32[1024]{0:T(1024)S(1)}, u32[]{:S(2)}) copy-start(s32[1024]{0:T(1024)S(1)} %slice.130) | copy-start | bytes 12292
  74.6 19.7 %copy-start.14 = (f32[8,104,128]{2,1,0:T(8,128)S(1)}, f32[8,104,128]{2,1,0:T(8,128)}, u32[]{:S(2)}) copy-start(f32[8,104,128]{2,1,0:T(8,128)} %get-tuple-element.175) | copy-start | bytes 1277956
  85.4 54.5 %collective-permute-start.6 = (bf16[8,768,128]{2,1,0:T(8,128)(2,1)}, bf16[8,768,128]{2,1,0:T(8,128)(2,1)S(1)}, u32[]{:S(2)}, u32[]{:S(2)}) collective-permute-start(bf16[8,768,128]{2,1,0:T(8,128)(2,1)} %get-tuple-element.174.x_ref.refs_0_), channel_id=1, source_target_pairs={{0,4},{4,0},{1,5},{5,1},{2,6},{6,2},{3,7},{7,3},{8,12},{12,8},{9,1... | collective-permute-start | bytes 4718600 | tf_op jit(solution)/shard_map/ppermute | solution.py:1117
  90.2 49.7 %collective-permute-start.7 = (bf16[8,768,128]{2,1,0:T(8,128)(2,1)}, bf16[8,768,128]{2,1,0:T(8,128)(2,1)S(1)}, u32[]{:S(2)}, u32[]{:S(2)}) collective-permute-start(bf16[8,768,128]{2,1,0:T(8,128)(2,1)} %get-tuple-element.174.x_ref.refs_0_), channel_id=1, source_target_pairs={{0,1},{1,0},{2,3},{3,2},{4,5},{5,4},{6,7},{7,6},{8,9},{9,8},{10,11... | collective-permute-start | bytes 4718600 | tf_op jit(solution)/shard_map/ppermute | solution.py:1117
  99.0 21.4 %collective-permute-start.3 = (bf16[192,2304]{1,0:T(8,128)(2,1)}, bf16[192,2304]{1,0:T(8,128)(2,1)}, u32[]{:S(2)}, u32[]{:S(2)}) collective-permute-start(bf16[192,2304]{1,0:T(8,128)(2,1)} %pad_maximum_fusion.refs_0_), channel_id=1, source_target_pairs={{0,8},{8,0},{16,24},{24,16},{1,9},{9,1},{17,25},{25,17},{2,10},{10... | collective-permute-start | bytes 2654216 | tf_op jit(solution)/shard_map/ppermute | solution.py:1117
  100.7 20.8 %collective-permute-start.4 = (bf16[192,2304]{1,0:T(8,128)(2,1)}, bf16[192,2304]{1,0:T(8,128)(2,1)}, u32[]{:S(2)}, u32[]{:S(2)}) collective-permute-start(bf16[192,2304]{1,0:T(8,128)(2,1)} %pad_maximum_fusion.refs_0_), channel_id=1, source_target_pairs={{0,16},{8,24},{16,0},{24,8},{1,17},{9,25},{17,1},{25,9},{2,18},{10... | collective-permute-start | bytes 2654216 | tf_op jit(solution)/shard_map/ppermute | solution.py:1117
  101.5 38.4 %collective-permute-start.5 = (bf16[192,2304]{1,0:T(8,128)(2,1)}, bf16[192,2304]{1,0:T(8,128)(2,1)}, u32[]{:S(2)}, u32[]{:S(2)}) collective-permute-start(bf16[192,2304]{1,0:T(8,128)(2,1)} %pad_maximum_fusion.refs_0_), channel_id=1, source_target_pairs={{0,24},{8,16},{16,8},{24,0},{1,25},{9,17},{17,9},{25,1},{2,26},{10... | collective-permute-start | bytes 2654216 | tf_op jit(solution)/shard_map/ppermute | solution.py:1117
  139.9 38.2 %collective-permute-start.8 = (bf16[8,768,128]{2,1,0:T(8,128)(2,1)S(1)}, bf16[8,768,128]{2,1,0:T(8,128)(2,1)}, u32[]{:S(2)}, u32[]{:S(2)}) collective-permute-start(bf16[8,768,128]{2,1,0:T(8,128)(2,1)S(1)} %collective-permute-done.7.x_ref.refs_2_), channel_id=1, source_target_pairs={{0,4},{4,0},{1,5},{5,1},{2,6},{6,2},{3,7},{7,3},{8,12},{12,8},{9,1... | collective-permute-start | bytes 4718600 | tf_op jit(solution)/shard_map/ppermute | solution.py:1117
  142.2 44.4 %collective-permute-start.9 = (bf16[1024,768]{1,0:T(8,128)(2,1)}, bf16[1024,768]{1,0:T(8,128)(2,1)}, u32[]{:S(2)}, u32[]{:S(2)}) collective-permute-start(bf16[1024,768]{1,0:T(8,128)(2,1)} %bitcast.113), channel_id=1, source_target_pairs={{0,4},{2,0},{4,6},{6,2},{1,5},{3,1},{5,7},{7,3},{8,12},{10,8},{12,... | collective-permute-start | bytes 4718600 | tf_op jit(solution)/shard_map/ppermute | solution.py:1123
  194.7 39.7 %collective-permute-start.10 = (bf16[8,768,128]{2,1,0:T(8,128)(2,1)}, bf16[8,768,128]{2,1,0:T(8,128)(2,1)S(1)}, u32[]{:S(2)}, u32[]{:S(2)}) collective-permute-start(bf16[8,768,128]{2,1,0:T(8,128)(2,1)} %get-tuple-element.215.refs_0_.refs_4_), channel_id=1, source_target_pairs={{0,4},{4,0},{1,5},{5,1},{2,6},{6,2},{3,7},{7,3},{8,12},{12,8},{9,1... | collective-permute-start | bytes 4718600 | tf_op jit(solution)/shard_map/ppermute | solution.py:1117
  194.9 39.5 %collective-permute-start.11 = (bf16[8,768,128]{2,1,0:T(8,128)(2,1)}, bf16[8,768,128]{2,1,0:T(8,128)(2,1)S(1)}, u32[]{:S(2)}, u32[]{:S(2)}) collective-permute-start(bf16[8,768,128]{2,1,0:T(8,128)(2,1)} %get-tuple-element.215.refs_0_.refs_4_), channel_id=1, source_target_pairs={{0,1},{1,0},{2,3},{3,2},{4,5},{5,4},{6,7},{7,6},{8,9},{9,8},{10,11... | collective-permute-start | bytes 4718600 | tf_op jit(solution)/shard_map/ppermute | solution.py:1117
  240.4 6.3 %collective-permute-start.12 = (bf16[8,768,128]{2,1,0:T(8,128)(2,1)}, bf16[8,768,128]{2,1,0:T(8,128)(2,1)}, u32[]{:S(2)}, u32[]{:S(2)}) collective-permute-start(bf16[8,768,128]{2,1,0:T(8,128)(2,1)} %shard_map.344), channel_id=1, source_target_pairs={{0,4},{4,0},{1,5},{5,1},{2,6},{6,2},{3,7},{7,3},{8,12},{12,8},{9,1... | collective-permute-start | bytes 4718600 | tf_op jit(solution)/shard_map/ppermute | solution.py:1117
  241.2 10.8 %collective-permute-start.13 = (bf16[8,768,128]{2,1,0:T(8,128)(2,1)S(1)}, bf16[8,768,128]{2,1,0:T(8,128)(2,1)S(1)}, u32[]{:S(2)}, u32[]{:S(2)}) collective-permute-start(bf16[8,768,128]{2,1,0:T(8,128)(2,1)S(1)} %collective-permute-done.11.refs_2_.refs_6_), channel_id=1, source_target_pairs={{0,4},{4,0},{1,5},{5,1},{2,6},{6,2},{3,7},{7,3},{8,12},{12,8},{9,1... | collective-permute-start | bytes 4718600 | tf_op jit(solution)/shard_map/ppermute | solution.py:1117
  253.2 16.0 %copy-start.8 = (bf16[8,768,128]{2,1,0:T(8,128)(2,1)S(1)}, bf16[8,768,128]{2,1,0:T(8,128)(2,1)}, u32[]{:S(2)}) copy-start(bf16[8,768,128]{2,1,0:T(8,128)(2,1)} %shard_map.345) | copy-start | bytes 4718596
  269.2 33.5 %collective-permute-start.14 = (bf16[8,768,128]{2,1,0:T(8,128)(2,1)S(1)}, bf16[8,768,128]{2,1,0:T(8,128)(2,1)S(1)}, u32[]{:S(2)}, u32[]{:S(2)}) collective-permute-start(bf16[8,768,128]{2,1,0:T(8,128)(2,1)S(1)} %copy-done.8), channel_id=1, source_target_pairs={{0,4},{4,0},{1,5},{5,1},{2,6},{6,2},{3,7},{7,3},{8,12},{12,8},{9,1... | collective-permute-start | bytes 4718600 | tf_op jit(solution)/shard_map/ppermute | solution.py:1117
  269.6 36.3 %collective-permute-start.15 = (bf16[8,768,128]{2,1,0:T(8,128)(2,1)}, bf16[8,768,128]{2,1,0:T(8,128)(2,1)}, u32[]{:S(2)}, u32[]{:S(2)}) collective-permute-start(bf16[8,768,128]{2,1,0:T(8,128)(2,1)} %shard_map.346), channel_id=1, source_target_pairs={{0,1},{1,0},{2,3},{3,2},{4,5},{5,4},{6,7},{7,6},{8,9},{9,8},{10,11... | collective-permute-start | bytes 4718600 | tf_op jit(solution)/shard_map/ppermute | solution.py:1117
  313.7 37.2 %collective-permute-start.16 = (bf16[1024,768]{1,0:T(8,128)(2,1)}, bf16[1024,768]{1,0:T(8,128)(2,1)S(1)}, u32[]{:S(2)}, u32[]{:S(2)}) collective-permute-start(bf16[1024,768]{1,0:T(8,128)(2,1)} %shard_map.349), channel_id=1, source_target_pairs={{4,0},{0,2},{6,4},{2,6},{5,1},{1,3},{7,5},{3,7},{12,8},{8,10},{14,... | collective-permute-start | bytes 4718600 | tf_op jit(solution)/shard_map/ppermute | solution.py:1126
  358.1 6.7 %collective-permute-start.17 = (bf16[8,768,128]{2,1,0:T(8,128)(2,1)}, bf16[8,768,128]{2,1,0:T(8,128)(2,1)}, u32[]{:S(2)}, u32[]{:S(2)}) collective-permute-start(bf16[8,768,128]{2,1,0:T(8,128)(2,1)} %shard_map.351), channel_id=1, source_target_pairs={{0,4},{4,0},{1,5},{5,1},{2,6},{6,2},{3,7},{7,3},{8,12},{12,8},{9,1... | collective-permute-start | bytes 4718600 | tf_op jit(solution)/shard_map/ppermute | solution.py:1117
  371.8 14.9 %copy-start.28 = (s32[1024]{0:T(1024)S(1)}, s32[1024]{0:T(1024)}, u32[]{:S(2)}) copy-start(s32[1024]{0:T(1024)} %convert_reduce_fusion.1) | copy-start | bytes 12292
  371.8 52.2 %collective-permute-start.18 = (bf16[8,768,128]{2,1,0:T(8,128)(2,1)S(1)}, bf16[8,768,128]{2,1,0:T(8,128)(2,1)}, u32[]{:S(2)}, u32[]{:S(2)}) collective-permute-start(bf16[8,768,128]{2,1,0:T(8,128)(2,1)S(1)} %copy-done.7), channel_id=1, source_target_pairs={{0,4},{4,0},{1,5},{5,1},{2,6},{6,2},{3,7},{7,3},{8,12},{12,8},{9,1... | collective-permute-start | bytes 4718600 | tf_op jit(solution)/shard_map/ppermute | solution.py:1117
  372.4 51.7 %collective-permute-start.19 = (bf16[8,768,128]{2,1,0:T(8,128)(2,1)}, bf16[8,768,128]{2,1,0:T(8,128)(2,1)}, u32[]{:S(2)}, u32[]{:S(2)}) collective-permute-start(bf16[8,768,128]{2,1,0:T(8,128)(2,1)} %shard_map.353), channel_id=1, source_target_pairs={{0,1},{1,0},{2,3},{3,2},{4,5},{5,4},{6,7},{7,6},{8,9},{9,8},{10,11... | collective-permute-start | bytes 4718600 | tf_op jit(solution)/shard_map/ppermute | solution.py:1117
  373.9 13.9 %copy-start.34 = (s32[4]{0:T(128)S(1)}, s32[4]{0:T(128)}, u32[]{:S(2)}) copy-start(s32[4]{0:T(128)} %iota_xor_fusion.at_ref) | copy-start | bytes 52
  373.9 50.1 %all-to-all-start.1 = ((bf16[8,128,768]{2,1,0:T(8,128)(2,1)}), bf16[8,128,768]{2,1,0:T(8,128)(2,1)S(1)}, u32[]{:S(2)}, u32[]{:S(2)}) async-start(bf16[8,128,768]{2,1,0:T(8,128)(2,1)} %bitcast.114), calls=%async_computation.1 | async-start | bytes 3145728 | tf_op jit(solution)/shard_map/all_to_all | solution.py:1129
  434.7 12.9 %copy-start.15 = (f32[1,384,256]{2,1,0:T(8,128)S(1)}, f32[1,384,256]{2,1,0:T(8,128)}, u32[]{:S(2)}) copy-start(f32[1,384,256]{2,1,0:T(8,128)} %get-tuple-element.300) | copy-start | bytes 1179652
  434.7 45.6 %collective-permute-start.20 = (bf16[1024,768]{1,0:T(8,128)(2,1)}, bf16[1024,768]{1,0:T(8,128)(2,1)}, u32[]{:S(2)}, u32[]{:S(2)}) collective-permute-start(bf16[1024,768]{1,0:T(8,128)(2,1)} %get-tuple-element.287), channel_id=1, source_target_pairs={{4,0},{0,2},{6,4},{2,6},{5,1},{1,3},{7,5},{3,7},{12,8},{8,10},{14,... | collective-permute-start | bytes 4718600 | tf_op jit(solution)/shard_map/ppermute | solution.py:1126
  434.8 43.0 %collective-permute-start.23 = (bf16[192,2304]{1,0:T(8,128)(2,1)}, bf16[192,2304]{1,0:T(8,128)(2,1)S(1)}, u32[]{:S(2)}, u32[]{:S(2)}) collective-permute-start(bf16[192,2304]{1,0:T(8,128)(2,1)} %get-tuple-element.291), channel_id=1, source_target_pairs={{0,24},{8,16},{16,8},{24,0},{1,25},{9,17},{17,9},{25,1},{2,26},{10... | collective-permute-start | bytes 2654216 | tf_op jit(solution)/shard_map/ppermute | solution.py:1117
  437.4 40.4 %collective-permute-start.22 = (bf16[192,2304]{1,0:T(8,128)(2,1)}, bf16[192,2304]{1,0:T(8,128)(2,1)S(1)}, u32[]{:S(2)}, u32[]{:S(2)}) collective-permute-start(bf16[192,2304]{1,0:T(8,128)(2,1)} %get-tuple-element.290), channel_id=1, source_target_pairs={{0,16},{8,24},{16,0},{24,8},{1,17},{9,25},{17,1},{25,9},{2,18},{10... | collective-permute-start | bytes 2654216 | tf_op jit(solution)/shard_map/ppermute | solution.py:1117
  437.7 40.1 %collective-permute-start.21 = (bf16[192,2304]{1,0:T(8,128)(2,1)}, bf16[192,2304]{1,0:T(8,128)(2,1)}, u32[]{:S(2)}, u32[]{:S(2)}) collective-permute-start(bf16[192,2304]{1,0:T(8,128)(2,1)} %get-tuple-element.289), channel_id=1, source_target_pairs={{0,8},{8,0},{16,24},{24,16},{1,9},{9,1},{17,25},{25,17},{2,10},{10... | collective-permute-start | bytes 2654216 | tf_op jit(solution)/shard_map/ppermute | solution.py:1117
  447.7 12.0 %copy-start.17 = (f32[1,384,128]{2,1,0:T(8,128)S(1)}, f32[1,384,128]{2,1,0:T(8,128)}, u32[]{:S(2)}) copy-start(f32[1,384,128]{2,1,0:T(8,128)} %get-tuple-element.298) | copy-start | bytes 589828
  466.6 13.7 %all-to-all-start.2 = ((f32[32,8,128]{2,1,0:T(8,128)}), f32[32,8,128]{2,1,0:T(8,128)S(1)}, u32[]{:S(2)}, u32[]{:S(2)}) async-start(f32[32,8,128]{2,1,0:T(8,128)} %pad.19.clone), calls=%async_computation.2 | async-start | bytes 262144 | tf_op jit(solution)/shard_map/all_to_all | solution.py:1220
  480.3 11.5 %collective-permute-start.26 = (f32[4,99,128]{2,1,0:T(8,128)S(1)}, f32[4,99,128]{2,1,0:T(8,128)S(1)}, u32[]{:S(2)}, u32[]{:S(2)}) collective-permute-start(f32[4,99,128]{2,1,0:T(8,128)S(1)} %broadcast_select_fusion.4), channel_id=1, source_target_pairs={{0,2},{2,0},{1,3},{3,1},{4,6},{6,4},{5,7},{7,5},{8,10},{10,8},{9,1... | collective-permute-start | bytes 608264 | tf_op jit(solution)/shard_map/ppermute | solution.py:1117
  482.6 27.6 %copy-start.19 = (f32[2,48,64]{2,1,0:T(8,128)S(1)}, f32[2,48,64]{2,1,0:T(8,128)}, u32[]{:S(2)}) copy-start(f32[2,48,64]{2,1,0:T(8,128)} %param.39) | copy-start | bytes 73732
  482.6 27.6 %copy-start.31 = (f32[2,48]{1,0:T(2,128)S(1)}, f32[2,48]{1,0:T(2,128)}, u32[]{:S(2)}) copy-start(f32[2,48]{1,0:T(2,128)} %copy-done.30) | copy-start | bytes 1156
  482.6 27.6 %copy-start.32 = (f32[2,48]{1,0:T(2,128)S(1)}, f32[2,48]{1,0:T(2,128)}, u32[]{:S(2)}) copy-start(f32[2,48]{1,0:T(2,128)} %get-tuple-element.445) | copy-start | bytes 1156
  482.6 45.6 %all-to-all-start.3 = ((bf16[8,128,768]{2,1,0:T(8,128)(2,1)}), bf16[8,128,768]{2,1,0:T(8,128)(2,1)S(1)}, u32[]{:S(2)}, u32[]{:S(2)}) async-start(bf16[8,128,768]{2,1,0:T(8,128)(2,1)} %bitcast.50), calls=%async_computation.3 | async-start | bytes 3145728 | tf_op jit(solution)/shard_map/all_to_all | solution.py:1129
  491.9 16.0 %collective-permute-start.30 = (f32[99,128]{1,0:T(8,128)S(1)}, f32[99,128]{1,0:T(8,128)S(1)}, u32[]{:S(2)}, u32[]{:S(2)}) collective-permute-start(f32[99,128]{1,0:T(8,128)S(1)} %get-tuple-element.429), channel_id=1, source_target_pairs={{0,22},{1,30},{2,23},{3,31},{4,6},{5,14},{6,7},{7,15},{8,20},{9,28... | collective-permute-start | bytes 152072 | tf_op jit(solution)/shard_map/ppermute | solution.py:1235
  491.9 17.3 %collective-permute-start.29 = (f32[99,128]{1,0:T(8,128)S(1)}, f32[99,128]{1,0:T(8,128)S(1)}, u32[]{:S(2)}, u32[]{:S(2)}) collective-permute-start(f32[99,128]{1,0:T(8,128)S(1)} %get-tuple-element.430), channel_id=1, source_target_pairs={{0,20},{1,28},{2,21},{3,29},{4,4},{5,12},{6,5},{7,13},{8,22},{9,30... | collective-permute-start | bytes 152072 | tf_op jit(solution)/shard_map/ppermute | solution.py:1235
  492.6 16.6 %collective-permute-start.27 = (f32[99,128]{1,0:T(8,128)S(1)}, f32[99,128]{1,0:T(8,128)S(1)}, u32[]{:S(2)}, u32[]{:S(2)}) collective-permute-start(f32[99,128]{1,0:T(8,128)S(1)} %get-tuple-element.431), channel_id=1, source_target_pairs={{0,16},{1,24},{2,17},{3,25},{4,0},{5,8},{6,1},{7,9},{8,18},{9,26},... | collective-permute-start | bytes 152072 | tf_op jit(solution)/shard_map/ppermute | solution.py:1235
  496.2 13.7 %collective-permute-start.28 = (f32[99,128]{1,0:T(8,128)S(1)}, f32[99,128]{1,0:T(8,128)S(1)}, u32[]{:S(2)}, u32[]{:S(2)}) collective-permute-start(f32[99,128]{1,0:T(8,128)S(1)} %get-tuple-element.428), channel_id=1, source_target_pairs={{0,18},{1,26},{2,19},{3,27},{4,2},{5,10},{6,3},{7,11},{8,16},{9,24... | collective-permute-start | bytes 152072 | tf_op jit(solution)/shard_map/ppermute | solution.py:1235
  501.6 12.8 %collective-permute-start.25 = (bf16[96,2304]{1,0:T(8,128)(2,1)}, bf16[96,2304]{1,0:T(8,128)(2,1)S(1)}, u32[]{:S(2)}, u32[]{:S(2)}) collective-permute-start(bf16[96,2304]{1,0:T(8,128)(2,1)} %get-tuple-element.309), channel_id=1, source_target_pairs={{0,6},{2,2},{4,4},{6,0},{1,7},{3,3},{5,5},{7,1},{8,14},{10,10},{12... | collective-permute-start | bytes 1327112 | tf_op jit(solution)/shard_map/ppermute | solution.py:1207
  507.9 17.8 %collective-permute-start.24 = (bf16[96,2304]{1,0:T(8,128)(2,1)S(1)}, bf16[96,2304]{1,0:T(8,128)(2,1)S(1)}, u32[]{:S(2)}, u32[]{:S(2)}) collective-permute-start(bf16[96,2304]{1,0:T(8,128)(2,1)S(1)} %get-tuple-element.308), channel_id=1, source_target_pairs={{4,0},{0,2},{6,4},{2,6},{5,1},{1,3},{7,5},{3,7},{12,8},{8,10},{14,... | collective-permute-start | bytes 1327112 | tf_op jit(solution)/shard_map/ppermute | solution.py:1126
  (31 other events, 237.8 us)
